TPU v7x, 512 devices: a whole 4x8x8 slice. The times are simulated.
512 devices in a mesh: dp: 8 (over z), space: 64 (over y, x, core).
Axes of the slice: x: 4, y: 8, z: 8, core: 2. Of those that a mesh axis runs over, the one named last changes fastest.
Arguments:
- image: bfloat16 [8, 1024, 16, 512], P('dp', 'space'), may hold values from -6 to 6
- cotangent: bfloat16 [8, 1024, 4, 256], P('dp', 'space'), may hold values from -6 to 6
- live_count: int32 [8, 64], P('dp', 'space'), may hold values from 8 to 16, as said below
- neighbours: int32 [8, 1024, 8], P('dp', 'space'), may hold values from -1 to 1023, as said below
- weight_one: bfloat16 [3, 3, 32, 64], replicated, may hold values from -0.375 to 0.375
- weight_two: bfloat16 [3, 3, 64, 64], replicated, may hold values from -0.25 to 0.25
- gain_one: float32 [64], replicated, may hold values from 0.1 to 1.9
- gain_two: float32 [64], replicated, may hold values from 0.1 to 1.9
Outputs:
- grad_weight_one: float32 [3, 3, 32, 64], replicated
- grad_weight_two: float32 [3, 3, 64, 64], replicated
- grad_gain_one: float32 [64], replicated
- grad_gain_two: float32 [64], replicated
Inputs may be any that keep to these rules, and one draw needn't show every extreme that they name: A device's tiles fill its first live_count slots; some device of each slide holds 16 tiles. Entry j of a slot lists the global slot (device index along space times 16 plus slot) of the tile in direction j of the order NW, N, NE, W, E, SW, S, SE, or -1 for background or the window's edge; rows of dead slots are all -1. Tiles are numbered in raster order within each device's band. A tile's neighbours above and below are on its own device; those to its left lie on its own device or the one before it along space, those to its right on its own device or the one after it.
All inputs are finite; a program needn't handle non-finite values.
Results may differ from a plain program's by a relative error of at most 0.0051.
Values may be sent and summed in bfloat16 or wider, within the bound.
A program may use at most 64 MiB of HBM per device.

v0:
```python
import math

import jax
import jax.numpy as jnp
from jax import lax
from jax.sharding import Mesh
from jax.sharding import PartitionSpec as P

SPACE = ("space_0", "space_1", "space_2")


EPS = 1e-05


def from_behind(value, axis, steps):
    count = lax.axis_size(axis)
    first, last = (max(0, -steps), min(count, count - steps))
    return lax.ppermute(value, axis, [(source, source + steps) for source in range(first, last)])


def cut_along(value, dim, peers):
    before, after = (value.shape[:dim], value.shape[dim + 1 :])
    return jnp.moveaxis(value.reshape(*before, peers, -1, *after), dim, 0)


def sent_and_summed(value, axis, dim):
    peers = lax.axis_size(axis)
    pieces = lax.all_to_all(cut_along(value, dim, peers), axis, 0, 0, tiled=True)
    return jnp.sum(pieces, axis=0)


def summed_rows(value, axes, dim):
    far, near = axes
    pieces = cut_along(value, dim, lax.axis_size(far))
    nearer = sent_and_summed(pieces, near, dim + 1)
    arrived = lax.all_to_all(nearer, far, split_axis=0, concat_axis=0, tiled=True)
    return arrived.sum(axis=0)


def rows_for(lines, peers):
    spare = -lines.shape[0] % peers
    if not spare:
        return lines
    return jnp.concatenate([lines, jnp.zeros((spare, *lines.shape[1:]), lines.dtype)])


def from_everyone(value, axis):
    peers = lax.axis_size(axis)
    return lax.all_to_all(
        jnp.broadcast_to(value[None], (peers, *value.shape)), axis, 0, 0, tiled=True
    )


def in_order(pieces, dim):
    pieces = jnp.moveaxis(pieces, 0, dim)
    dims = pieces.shape
    return pieces.reshape(*dims[:dim], dims[dim] * dims[dim + 1], *dims[dim + 2 :])


def gathered_by_axis(value, axes, dim):
    far, near = axes
    first = from_everyone(value, far)
    pieces = jnp.swapaxes(from_everyone(first, near), 0, 1)
    return in_order(pieces.reshape(-1, *value.shape), dim)


def total_of(value, axes):
    lines = value.reshape(-1)
    own = summed_rows(rows_for(lines, lax.axis_size(axes[0]) * lax.axis_size(axes[1])), axes, 0)
    whole = gathered_by_axis(own, axes, 0)
    return whole[: len(lines)].reshape(value.shape)


def norm_forward(values):
    middle = jnp.mean(values, axis=-1, keepdims=True)
    centred = values - middle
    inverse = lax.rsqrt(jnp.mean(centred * centred, axis=-1, keepdims=True) + EPS)
    return (centred * inverse, inverse)


def norm_backward(grad_act, hidden, normed, inverse, gain):
    sig = jax.nn.sigmoid(hidden)
    grad_hidden = grad_act * sig * (1.0 + hidden * (1.0 - sig))
    grad_gain = jnp.sum(grad_hidden * normed, axis=(0, 1, 2))
    scaled = grad_hidden * gain
    centre = jnp.mean(scaled, axis=-1, keepdims=True)
    along = jnp.mean(scaled * normed, axis=-1, keepdims=True)
    return (inverse * (scaled - centre - normed * along), grad_gain)


def select_rows(source, idents, offset):
    positions = jnp.clip(idents - offset, 0, source.shape[0] - 1)
    picked = jnp.take(source, positions, axis=0)
    return jnp.where((idents >= 0)[:, None], picked, jnp.zeros_like(picked))


def assemble(field, south_rows, east_cols, corners):
    lower = jnp.concatenate([field, south_rows[:, None]], axis=1)
    right = jnp.concatenate([east_cols, corners[:, None]], axis=1)
    return jnp.concatenate([lower, right[:, :, None]], axis=2)


def conv_forward(padded, weight):
    return lax.conv_general_dilated(
        padded,
        weight,
        (2, 2),
        "VALID",
        dimension_numbers=("NHWC", "HWIO", "NHWC"),
        preferred_element_type=jnp.float32,
    )


def weight_grad(padded, grad_z):
    size = grad_z.shape[1]
    blocks = []
    for row_off in range(3):
        line = []
        for col_off in range(3):
            window = padded[
                :, row_off : row_off + 2 * size : 2, col_off : col_off + 2 * size : 2, :
            ]
            line.append(
                jnp.einsum("nijc,nijo->co", window, grad_z, preferred_element_type=jnp.float32)
            )
        blocks.append(jnp.stack(line))
    return jnp.stack(blocks)


def input_grad(grad_z, weight):
    size = grad_z.shape[1]
    total = jnp.zeros((grad_z.shape[0], 2 * size + 1, 2 * size + 1, weight.shape[2]), jnp.float32)
    for row_off in range(3):
        for col_off in range(3):
            term = jnp.einsum(
                "nijo,co->nijc",
                grad_z,
                weight[row_off, col_off],
                preferred_element_type=jnp.float32,
            )
            total = total.at[
                :, row_off : row_off + 2 * size : 2, col_off : col_off + 2 * size : 2, :
            ].add(term)
    return total


def on_device(image, cotangent, live_count, neighbours, weight_one, weight_two, gain_one, gain_two):
    slots = image.shape[1]
    tile = image.shape[2]
    chan_in = weight_one.shape[2]
    chan_mid = weight_one.shape[3]
    chan_out = weight_two.shape[3]
    half = tile // 2
    quarter = tile // 4
    offset = lax.axis_index(SPACE) * slots
    nearby = neighbours[0]
    live = jnp.arange(slots) < live_count[0, 0]
    field = image[0].reshape(slots, tile, tile, chan_in)
    field = jnp.where(live[:, None, None, None], field, jnp.zeros_like(field))
    south_image = select_rows(field[:, 0].reshape(slots, tile * chan_in), nearby[:, 6], offset)
    image_cols = field[:, :, 0, :].reshape(slots, tile * chan_in)
    following = from_behind(image_cols, SPACE, -1)
    source = jnp.concatenate([image_cols, following], axis=0)
    east_image = select_rows(source, nearby[:, 4], offset)
    diag_image = select_rows(source, nearby[:, 7], offset)
    padded_one = assemble(
        field,
        south_image.reshape(slots, tile, chan_in),
        east_image.reshape(slots, tile, chan_in),
        diag_image[:, :chan_in],
    )
    normed_one, inverse_one = norm_forward(conv_forward(padded_one, weight_one))
    hidden_one = normed_one * gain_one
    act_one = jax.nn.silu(hidden_one).astype(jnp.bfloat16)
    south_act = select_rows(act_one[:, 0].reshape(slots, half * chan_mid), nearby[:, 6], offset)
    act_cols = act_one[:, :, 0, :].reshape(slots, half * chan_mid)
    act_following = from_behind(act_cols, SPACE, -1)
    act_source = jnp.concatenate([act_cols, act_following], axis=0)
    east_act = select_rows(act_source, nearby[:, 4], offset)
    diag_act = select_rows(act_source, nearby[:, 7], offset)
    padded_two = assemble(
        act_one,
        south_act.reshape(slots, half, chan_mid),
        east_act.reshape(slots, half, chan_mid),
        diag_act[:, :chan_mid],
    )
    normed_two, inverse_two = norm_forward(conv_forward(padded_two, weight_two))
    hidden_two = normed_two * gain_two
    factor = 1.0 / math.sqrt(lax.axis_size("dp") * lax.axis_size(SPACE) * slots * quarter * quarter)
    grad_out = cotangent[0].reshape(slots, quarter, quarter, chan_out).astype(jnp.float32)
    grad_out = jnp.where(live[:, None, None, None], grad_out * factor, jnp.zeros_like(grad_out))
    grad_z_two, grad_gain_two = norm_backward(
        grad_out, hidden_two, normed_two, inverse_two, gain_two
    )
    grad_z_two = grad_z_two.astype(jnp.bfloat16)
    grad_weight_two = weight_grad(padded_two, grad_z_two)
    grad_padded = input_grad(grad_z_two, weight_two)
    bottom = grad_padded[:, half, :half, :].astype(jnp.bfloat16).reshape(slots, half * chan_mid)
    right = grad_padded[:, :, half, :].astype(jnp.bfloat16).reshape(slots, (half + 1) * chan_mid)
    from_north = select_rows(bottom, nearby[:, 1], offset).reshape(slots, half, chan_mid)
    previous = from_behind(right, SPACE, 1)
    rim_source = jnp.concatenate([previous, right], axis=0)
    from_west = select_rows(rim_source, nearby[:, 3], offset - slots).reshape(
        slots, half + 1, chan_mid
    )
    from_diag = select_rows(rim_source, nearby[:, 0], offset - slots).reshape(
        slots, half + 1, chan_mid
    )
    grad_act = grad_padded[:, :half, :half, :]
    grad_act = grad_act.at[:, 0].add(from_north.astype(jnp.float32))
    grad_act = grad_act.at[:, :, 0].add(from_west[:, :half].astype(jnp.float32))
    grad_act = grad_act.at[:, 0, 0].add(from_diag[:, half].astype(jnp.float32))
    grad_z_one, grad_gain_one = norm_backward(
        grad_act, hidden_one, normed_one, inverse_one, gain_one
    )
    grad_weight_one = weight_grad(padded_one, grad_z_one.astype(jnp.bfloat16))
    grad_weight_one, grad_weight_two, grad_gain_one, grad_gain_two = (
        total_of(grad_weight_one, (("dp", "space_0"), ("space_1", "space_2"))),
        total_of(grad_weight_two, (("dp", "space_0"), ("space_1", "space_2"))),
        total_of(grad_gain_one, (("dp", "space_0"), ("space_1", "space_2"))),
        total_of(grad_gain_two, (("dp", "space_0"), ("space_1", "space_2"))),
    )
    return (grad_weight_one, grad_weight_two, grad_gain_one, grad_gain_two)


def solution(mesh):
    torus = Mesh(
        mesh.devices.reshape(mesh.shape["dp"], 8, 4, 2), ("dp", "space_0", "space_1", "space_2")
    )
    return jax.shard_map(
        on_device,
        mesh=torus,
        in_specs=(
            P("dp", SPACE, None, None),
            P("dp", SPACE, None, None),
            P("dp", SPACE),
            P("dp", SPACE, None),
            P(),
            P(),
            P(),
            P(),
        ),
        out_specs=(P(), P(), P(), P()),
        check_vma=False,
    )
```

profile of v0, /device:TPU:1, one launch (start us, length us, event | category | flops | bytes accessed | tf_op | source)
XLA Modules:
  0.0 286.0 jit_solution(17392484996339360905)
XLA Ops:
  3.9 8.7 %collective-permute-start = (bf16[16,512]{1,0:T(8,128)(2,1)S(1)}, bf16[16,512]{1,0:T(8,128)(2,1)S(1)}, u32[]{:S(2)}, u32[]{:S(2)}) collective-permute-start(bf16[16,512]{1,0:T(8,128)(2,1)S(1)} %reshape_squeeze.18), channel_id=1, source_target_pairs={{1,0},{2,1},{3,2},{4,3},{5,4},{6,5},{7,6},{8,7},{9,8},{10,9},{11,1... | collective-permute-start | bytes 49160 | tf_op jit(solution)/shard_map/ppermute | solution.py:18
  58.3 3.7 %all-to-all-start.12 = ((f32[8,64,1]{1,2,0:T(1,128)}), f32[8,64,1]{1,2,0:T(1,128)S(1)}, u32[]{:S(2)}, u32[]{:S(2)}) async-start(f32[8,64,1]{1,2,0:T(1,128)} %copy.111), calls=%async_computation.12 | async-start | bytes 8192 | tf_op jit(solution)/shard_map/all_to_all | solution.py:28
  62.0 4.5 %all-to-all-done.12 = f32[8,64,1]{1,2,0:T(1,128)S(1)} async-done(((f32[8,64,1]{1,2,0:T(1,128)}), f32[8,64,1]{1,2,0:T(1,128)S(1)}, u32[]{:S(2)}, u32[]{:S(2)}) %all-to-all-start.12) | async-done | bytes 2080 | tf_op jit(solution)/shard_map/all_to_all | solution.py:28
  67.3 13.9 %all-to-all-start.13 = ((f32[64,1,1]{2,1,0:T(1,128)}), f32[64,1,1]{2,1,0:T(1,128)S(1)}, u32[]{:S(2)}, u32[]{:S(2)}) async-start(f32[64,1,1]{2,1,0:T(1,128)} %copy.112), calls=%async_computation.13 | async-start | bytes 65536 | tf_op jit(solution)/shard_map/all_to_all | solution.py:36
  81.3 10.6 %all-to-all-done.13 = f32[64,1,1]{2,1,0:T(1,128)S(1)} async-done(((f32[64,1,1]{2,1,0:T(1,128)}), f32[64,1,1]{2,1,0:T(1,128)S(1)}, u32[]{:S(2)}, u32[]{:S(2)}) %all-to-all-start.13) | async-done | bytes 288 | tf_op jit(solution)/shard_map/all_to_all | solution.py:36
  93.9 4.8 %all-to-all-start.14 = ((f32[64,1,1]{2,1,0:T(1,128)}), f32[64,1,1]{2,1,0:T(1,128)S(1)}, u32[]{:S(2)}, u32[]{:S(2)}) async-start(f32[64,1,1]{2,1,0:T(1,128)} %broadcast_in_dim.290), calls=%async_computation.14 | async-start | bytes 65536 | tf_op jit(solution)/shard_map/all_to_all | solution.py:49
  109.3 6.5 %all-to-all-start.8 = ((f32[8,64,1]{1,2,0:T(1,128)}), f32[8,64,1]{1,2,0:T(1,128)S(1)}, u32[]{:S(2)}, u32[]{:S(2)}) async-start(f32[8,64,1]{1,2,0:T(1,128)} %copy.108), calls=%async_computation.8 | async-start | bytes 8192 | tf_op jit(solution)/shard_map/all_to_all | solution.py:28
  117.0 3.3 %all-to-all-done.8 = f32[8,64,1]{1,2,0:T(1,128)S(1)} async-done(((f32[8,64,1]{1,2,0:T(1,128)}), f32[8,64,1]{1,2,0:T(1,128)S(1)}, u32[]{:S(2)}, u32[]{:S(2)}) %all-to-all-start.8) | async-done | bytes 2080 | tf_op jit(solution)/shard_map/all_to_all | solution.py:28
  120.3 4.0 %all-to-all-start = ((f32[8,1,2304]{2,1,0:T(1,128)}), f32[8,1,2304]{2,1,0:T(1,128)S(1)}, u32[]{:S(2)}, u32[]{:S(2)}) async-start(f32[8,1,2304]{2,1,0:T(1,128)} %reshape.491), calls=%async_computation | async-start | bytes 147456 | tf_op jit(solution)/shard_map/all_to_all | solution.py:28
  125.0 4.2 %all-to-all-done = f32[8,1,2304]{2,1,0:T(1,128)S(1)} async-done(((f32[8,1,2304]{2,1,0:T(1,128)}), f32[8,1,2304]{2,1,0:T(1,128)S(1)}, u32[]{:S(2)}, u32[]{:S(2)}) %all-to-all-start) | async-done | bytes 73760 | tf_op jit(solution)/shard_map/all_to_all | solution.py:28
  129.8 4.0 %all-to-all-start.15 = ((f32[8,64,1]{1,2,0:T(1,128)}), f32[8,64,1]{1,2,0:T(1,128)S(1)}, u32[]{:S(2)}, u32[]{:S(2)}) async-start(f32[8,64,1]{1,2,0:T(1,128)} %broadcast_in_dim.292), calls=%async_computation.15 | async-start | bytes 8192 | tf_op jit(solution)/shard_map/all_to_all | solution.py:49
  136.1 2.2 all-to-all-done.15
  138.3 9.0 %all-to-all-start.9 = ((f32[64,1,1]{2,1,0:T(1,128)}), f32[64,1,1]{2,1,0:T(1,128)S(1)}, u32[]{:S(2)}, u32[]{:S(2)}) async-start(f32[64,1,1]{2,1,0:T(1,128)} %copy.109), calls=%async_computation.9 | async-start | bytes 65536 | tf_op jit(solution)/shard_map/all_to_all | solution.py:36
  148.1 10.1 %all-to-all-done.9 = f32[64,1,1]{2,1,0:T(1,128)S(1)} async-done(((f32[64,1,1]{2,1,0:T(1,128)}), f32[64,1,1]{2,1,0:T(1,128)S(1)}, u32[]{:S(2)}, u32[]{:S(2)}) %all-to-all-start.9) | async-done | bytes 288 | tf_op jit(solution)/shard_map/all_to_all | solution.py:36
  158.1 4.6 %all-to-all-start.1 = ((f32[64,1,36]{2,1,0:T(1,128)}), f32[64,1,36]{2,1,0:T(1,128)S(1)}, u32[]{:S(2)}, u32[]{:S(2)}) async-start(f32[64,1,36]{2,1,0:T(1,128)} %copy.103), calls=%async_computation.1 | async-start | bytes 65536 | tf_op jit(solution)/shard_map/all_to_all | solution.py:36
  163.5 10.1 %all-to-all-done.1 = f32[64,1,36]{2,1,0:T(1,128)S(1)} async-done(((f32[64,1,36]{2,1,0:T(1,128)}), f32[64,1,36]{2,1,0:T(1,128)S(1)}, u32[]{:S(2)}, u32[]{:S(2)}) %all-to-all-start.1) | async-done | bytes 9248 | tf_op jit(solution)/shard_map/all_to_all | solution.py:36
  174.8 4.6 %all-to-all-start.10 = ((f32[64,1,1]{2,1,0:T(1,128)}), f32[64,1,1]{2,1,0:T(1,128)S(1)}, u32[]{:S(2)}, u32[]{:S(2)}) async-start(f32[64,1,1]{2,1,0:T(1,128)} %broadcast_in_dim.287), calls=%async_computation.10 | async-start | bytes 65536 | tf_op jit(solution)/shard_map/all_to_all | solution.py:49
  179.5 10.7 %all-to-all-done.10 = f32[64,1,1]{2,1,0:T(1,128)S(1)} async-done(((f32[64,1,1]{2,1,0:T(1,128)}), f32[64,1,1]{2,1,0:T(1,128)S(1)}, u32[]{:S(2)}, u32[]{:S(2)}) %all-to-all-start.10) | async-done | bytes 288 | tf_op jit(solution)/shard_map/all_to_all | solution.py:49
  190.9 4.6 %all-to-all-start.2 = ((f32[64,1,36]{2,1,0:T(1,128)}), f32[64,1,36]{2,1,0:T(1,128)S(1)}, u32[]{:S(2)}, u32[]{:S(2)}) async-start(f32[64,1,36]{2,1,0:T(1,128)} %broadcast_in_dim.281), calls=%async_computation.2 | async-start | bytes 65536 | tf_op jit(solution)/shard_map/all_to_all | solution.py:49
  196.4 9.8 %all-to-all-done.2 = f32[64,1,36]{2,1,0:T(1,128)S(1)} async-done(((f32[64,1,36]{2,1,0:T(1,128)}), f32[64,1,36]{2,1,0:T(1,128)S(1)}, u32[]{:S(2)}, u32[]{:S(2)}) %all-to-all-start.2) | async-done | bytes 9248 | tf_op jit(solution)/shard_map/all_to_all | solution.py:49
  206.2 8.9 %all-to-all-start.4 = ((f32[8,64,72]{2,1,0:T(8,128)}), f32[8,64,72]{2,1,0:T(8,128)S(1)}, u32[]{:S(2)}, u32[]{:S(2)}) async-start(f32[8,64,72]{2,1,0:T(8,128)} %bitcast.365), calls=%async_computation.4 | async-start | bytes 524288 | tf_op jit(solution)/shard_map/all_to_all | solution.py:28
  215.7 5.9 %all-to-all-done.4 = f32[8,64,72]{2,1,0:T(8,128)S(1)} async-done(((f32[8,64,72]{2,1,0:T(8,128)}), f32[8,64,72]{2,1,0:T(8,128)S(1)}, u32[]{:S(2)}, u32[]{:S(2)}) %all-to-all-start.4) | async-done | bytes 147488 | tf_op jit(solution)/shard_map/all_to_all | solution.py:28
  222.2 4.3 %all-to-all-start.11 = ((f32[8,64,1]{1,2,0:T(1,128)}), f32[8,64,1]{1,2,0:T(1,128)S(1)}, u32[]{:S(2)}, u32[]{:S(2)}) async-start(f32[8,64,1]{1,2,0:T(1,128)} %broadcast_in_dim.289), calls=%async_computation.11 | async-start | bytes 8192 | tf_op jit(solution)/shard_map/all_to_all | solution.py:49
  227.2 3.8 %all-to-all-done.11 = f32[8,64,1]{1,2,0:T(1,128)S(1)} async-done(((f32[8,64,1]{1,2,0:T(1,128)}), f32[8,64,1]{1,2,0:T(1,128)S(1)}, u32[]{:S(2)}, u32[]{:S(2)}) %all-to-all-start.11) | async-done | bytes 2080 | tf_op jit(solution)/shard_map/all_to_all | solution.py:49
  231.0 4.6 %all-to-all-start.5 = ((f32[64,1,72]{2,1,0:T(1,128)}), f32[64,1,72]{2,1,0:T(1,128)S(1)}, u32[]{:S(2)}, u32[]{:S(2)}) async-start(f32[64,1,72]{2,1,0:T(1,128)} %bitcast.130), calls=%async_computation.5 | async-start | bytes 65536 | tf_op jit(solution)/shard_map/all_to_all | solution.py:36
  236.4 10.0 %all-to-all-done.5 = f32[64,1,72]{2,1,0:T(1,128)S(1)} async-done(((f32[64,1,72]{2,1,0:T(1,128)}), f32[64,1,72]{2,1,0:T(1,128)S(1)}, u32[]{:S(2)}, u32[]{:S(2)}) %all-to-all-start.5) | async-done | bytes 18464 | tf_op jit(solution)/shard_map/all_to_all | solution.py:36
  246.4 5.1 %all-to-all-start.3 = ((f32[8,1,2304]{2,1,0:T(1,128)}), f32[8,1,2304]{2,1,0:T(1,128)S(1)}, u32[]{:S(2)}, u32[]{:S(2)}) async-start(f32[8,1,2304]{2,1,0:T(1,128)} %reshape.493), calls=%async_computation.3 | async-start | bytes 147456 | tf_op jit(solution)/shard_map/all_to_all | solution.py:49
  251.6 4.8 %all-to-all-done.3 = f32[8,1,2304]{2,1,0:T(1,128)S(1)} async-done(((f32[8,1,2304]{2,1,0:T(1,128)}), f32[8,1,2304]{2,1,0:T(1,128)S(1)}, u32[]{:S(2)}, u32[]{:S(2)}) %all-to-all-start.3) | async-done | bytes 73760 | tf_op jit(solution)/shard_map/all_to_all | solution.py:49
  257.1 4.6 %all-to-all-start.6 = ((f32[64,1,72]{2,1,0:T(1,128)}), f32[64,1,72]{2,1,0:T(1,128)S(1)}, u32[]{:S(2)}, u32[]{:S(2)}) async-start(f32[64,1,72]{2,1,0:T(1,128)} %broadcast_in_dim.284), calls=%async_computation.6 | async-start | bytes 65536 | tf_op jit(solution)/shard_map/all_to_all | solution.py:49
  264.0 8.5 %all-to-all-done.6 = f32[64,1,72]{2,1,0:T(1,128)S(1)} async-done(((f32[64,1,72]{2,1,0:T(1,128)}), f32[64,1,72]{2,1,0:T(1,128)S(1)}, u32[]{:S(2)}, u32[]{:S(2)}) %all-to-all-start.6) | async-done | bytes 18464 | tf_op jit(solution)/shard_map/all_to_all | solution.py:49
  273.2 5.3 %all-to-all-start.7 = ((f32[8,64,72]{2,1,0:T(8,128)}), f32[8,64,72]{2,1,0:T(8,128)S(1)}, u32[]{:S(2)}, u32[]{:S(2)}) async-start(f32[8,64,72]{2,1,0:T(8,128)} %broadcast_in_dim.286), calls=%async_computation.7 | async-start | bytes 524288 | tf_op jit(solution)/shard_map/all_to_all | solution.py:49
  279.5 5.4 %all-to-all-done.7 = f32[8,64,72]{2,1,0:T(8,128)S(1)} async-done(((f32[8,64,72]{2,1,0:T(8,128)}), f32[8,64,72]{2,1,0:T(8,128)S(1)}, u32[]{:S(2)}, u32[]{:S(2)}) %all-to-all-start.7) | async-done | bytes 147488 | tf_op jit(solution)/shard_map/all_to_all | solution.py:49
  (258 shorter events, 78.4 us)
Async XLA Ops:
  3.9 15.5 %collective-permute-start = (bf16[16,512]{1,0:T(8,128)(2,1)S(1)}, bf16[16,512]{1,0:T(8,128)(2,1)S(1)}, u32[]{:S(2)}, u32[]{:S(2)}) collective-permute-start(bf16[16,512]{1,0:T(8,128)(2,1)S(1)} %reshape_squeeze.18), channel_id=1, source_target_pairs={{1,0},{2,1},{3,2},{4,3},{5,4},{6,5},{7,6},{8,7},{9,8},{10,9},{11,1... | collective-permute-start | bytes 49160 | tf_op jit(solution)/shard_map/ppermute | solution.py:18
  23.1 5.1 %collective-permute-start.1 = (bf16[16,512]{1,0:T(8,128)(2,1)S(1)}, bf16[16,512]{1,0:T(8,128)(2,1)S(1)}, u32[]{:S(2)}, u32[]{:S(2)}) collective-permute-start(bf16[16,512]{1,0:T(8,128)(2,1)S(1)} %reshape_squeeze.20), channel_id=1, source_target_pairs={{1,0},{2,1},{3,2},{4,3},{5,4},{6,5},{7,6},{8,7},{9,8},{10,9},{11,1... | collective-permute-start | bytes 49160 | tf_op jit(solution)/shard_map/ppermute | solution.py:18
  54.3 45.1 %copy-start.19 = (pred[16]{0:T(512)(128)(4,1)S(1)}, pred[16]{0:T(512)(128)(4,1)}, u32[]{:S(2)}) copy-start(pred[16]{0:T(512)(128)(4,1)} %get-tuple-element.66) | copy-start | bytes 52
  54.3 45.1 %copy-start.21 = (pred[16]{0:T(512)(128)(4,1)S(1)}, pred[16]{0:T(512)(128)(4,1)}, u32[]{:S(2)}) copy-start(pred[16]{0:T(512)(128)(4,1)} %get-tuple-element.79) | copy-start | bytes 52
  54.4 46.0 %copy-start.18 = (pred[16]{0:T(512)(128)(4,1)S(1)}, pred[16]{0:T(512)(128)(4,1)}, u32[]{:S(2)}) copy-start(pred[16]{0:T(512)(128)(4,1)} %get-tuple-element.65) | copy-start | bytes 52
  54.4 46.0 %copy-start.20 = (pred[16]{0:T(512)(128)(4,1)S(1)}, pred[16]{0:T(512)(128)(4,1)}, u32[]{:S(2)}) copy-start(pred[16]{0:T(512)(128)(4,1)} %get-tuple-element.50) | copy-start | bytes 52
  54.4 46.3 %copy-start.5 = (f32[16,8,8]{0,2,1:T(8,128)S(1)}, f32[16,8,8]{0,2,1:T(8,128)}, u32[]{:S(2)}) copy-start(f32[16,8,8]{0,2,1:T(8,128)} %copy-done.4) | copy-start | bytes 12292
  54.4 46.3 %copy-start.16 = (f32[64]{0:T(128)S(1)}, f32[64]{0:T(128)}, u32[]{:S(2)}) copy-start(f32[64]{0:T(128)} %param.26) | copy-start | bytes 772
  54.6 44.1 %collective-permute-start.2 = (bf16[16,576]{1,0:T(8,128)(2,1)S(1)}, bf16[16,576]{1,0:T(8,128)(2,1)S(1)}, u32[]{:S(2)}, u32[]{:S(2)}) collective-permute-start(bf16[16,576]{1,0:T(8,128)(2,1)S(1)} %convert_element_type.52), channel_id=1, source_target_pairs={{0,1},{1,2},{2,3},{3,4},{4,5},{5,6},{6,7},{7,8},{8,9},{9,10},{10,1... | collective-permute-start | bytes 55304 | tf_op jit(solution)/shard_map/ppermute | solution.py:18
  58.3 8.2 %all-to-all-start.12 = ((f32[8,64,1]{1,2,0:T(1,128)}), f32[8,64,1]{1,2,0:T(1,128)S(1)}, u32[]{:S(2)}, u32[]{:S(2)}) async-start(f32[8,64,1]{1,2,0:T(1,128)} %copy.111), calls=%async_computation.12 | async-start | bytes 8192 | tf_op jit(solution)/shard_map/all_to_all | solution.py:28
  67.3 24.7 %all-to-all-start.13 = ((f32[64,1,1]{2,1,0:T(1,128)}), f32[64,1,1]{2,1,0:T(1,128)S(1)}, u32[]{:S(2)}, u32[]{:S(2)}) async-start(f32[64,1,1]{2,1,0:T(1,128)} %copy.112), calls=%async_computation.13 | async-start | bytes 65536 | tf_op jit(solution)/shard_map/all_to_all | solution.py:36
  93.9 15.4 %all-to-all-start.14 = ((f32[64,1,1]{2,1,0:T(1,128)}), f32[64,1,1]{2,1,0:T(1,128)S(1)}, u32[]{:S(2)}, u32[]{:S(2)}) async-start(f32[64,1,1]{2,1,0:T(1,128)} %broadcast_in_dim.290), calls=%async_computation.14 | async-start | bytes 65536 | tf_op jit(solution)/shard_map/all_to_all | solution.py:49
  106.4 27.4 %copy-start.11 = (f32[1,64,64]{2,1,0:T(8,128)S(1)}, f32[1,64,64]{2,1,0:T(8,128)}, u32[]{:S(2)}) copy-start(f32[1,64,64]{2,1,0:T(8,128)} %convolution_bitcast_fusion.6) | copy-start | bytes 49156
  106.4 27.4 %copy-start.12 = (f32[1,64,64]{2,1,0:T(8,128)S(1)}, f32[1,64,64]{2,1,0:T(8,128)}, u32[]{:S(2)}) copy-start(f32[1,64,64]{2,1,0:T(8,128)} %convolution_bitcast_fusion.7) | copy-start | bytes 49156
  106.4 27.4 %copy-start.13 = (f32[1,64,64]{2,1,0:T(8,128)S(1)}, f32[1,64,64]{2,1,0:T(8,128)}, u32[]{:S(2)}) copy-start(f32[1,64,64]{2,1,0:T(8,128)} %convolution_bitcast_fusion.8) | copy-start | bytes 49156
  109.3 11.0 %all-to-all-start.8 = ((f32[8,64,1]{1,2,0:T(1,128)}), f32[8,64,1]{1,2,0:T(1,128)S(1)}, u32[]{:S(2)}, u32[]{:S(2)}) async-start(f32[8,64,1]{1,2,0:T(1,128)} %copy.108), calls=%async_computation.8 | async-start | bytes 8192 | tf_op jit(solution)/shard_map/all_to_all | solution.py:28
  115.8 47.0 %copy-start.8 = (f32[1,64,64]{2,1,0:T(8,128)S(1)}, f32[1,64,64]{2,1,0:T(8,128)}, u32[]{:S(2)}) copy-start(f32[1,64,64]{2,1,0:T(8,128)} %convolution_bitcast_fusion.3) | copy-start | bytes 49156
  115.8 47.0 %copy-start.9 = (f32[1,64,64]{2,1,0:T(8,128)S(1)}, f32[1,64,64]{2,1,0:T(8,128)}, u32[]{:S(2)}) copy-start(f32[1,64,64]{2,1,0:T(8,128)} %convolution_bitcast_fusion.4) | copy-start | bytes 49156
  115.8 47.0 %copy-start.10 = (f32[1,64,64]{2,1,0:T(8,128)S(1)}, f32[1,64,64]{2,1,0:T(8,128)}, u32[]{:S(2)}) copy-start(f32[1,64,64]{2,1,0:T(8,128)} %convolution_bitcast_fusion.5) | copy-start | bytes 49156
  116.0 63.4 %copy-start.7 = (f32[1,64,64]{2,1,0:T(8,128)S(1)}, f32[1,64,64]{2,1,0:T(8,128)}, u32[]{:S(2)}) copy-start(f32[1,64,64]{2,1,0:T(8,128)} %convolution_bitcast_fusion.2) | copy-start | bytes 49156
  120.3 8.9 %all-to-all-start = ((f32[8,1,2304]{2,1,0:T(1,128)}), f32[8,1,2304]{2,1,0:T(1,128)S(1)}, u32[]{:S(2)}, u32[]{:S(2)}) async-start(f32[8,1,2304]{2,1,0:T(1,128)} %reshape.491), calls=%async_computation | async-start | bytes 147456 | tf_op jit(solution)/shard_map/all_to_all | solution.py:28
  129.8 8.5 %all-to-all-start.15 = ((f32[8,64,1]{1,2,0:T(1,128)}), f32[8,64,1]{1,2,0:T(1,128)S(1)}, u32[]{:S(2)}, u32[]{:S(2)}) async-start(f32[8,64,1]{1,2,0:T(1,128)} %broadcast_in_dim.292), calls=%async_computation.15 | async-start | bytes 8192 | tf_op jit(solution)/shard_map/all_to_all | solution.py:49
  138.3 19.8 %all-to-all-start.9 = ((f32[64,1,1]{2,1,0:T(1,128)}), f32[64,1,1]{2,1,0:T(1,128)S(1)}, u32[]{:S(2)}, u32[]{:S(2)}) async-start(f32[64,1,1]{2,1,0:T(1,128)} %copy.109), calls=%async_computation.9 | async-start | bytes 65536 | tf_op jit(solution)/shard_map/all_to_all | solution.py:36
  158.1 15.4 %all-to-all-start.1 = ((f32[64,1,36]{2,1,0:T(1,128)}), f32[64,1,36]{2,1,0:T(1,128)S(1)}, u32[]{:S(2)}, u32[]{:S(2)}) async-start(f32[64,1,36]{2,1,0:T(1,128)} %copy.103), calls=%async_computation.1 | async-start | bytes 65536 | tf_op jit(solution)/shard_map/all_to_all | solution.py:36
  174.8 15.4 %all-to-all-start.10 = ((f32[64,1,1]{2,1,0:T(1,128)}), f32[64,1,1]{2,1,0:T(1,128)S(1)}, u32[]{:S(2)}, u32[]{:S(2)}) async-start(f32[64,1,1]{2,1,0:T(1,128)} %broadcast_in_dim.287), calls=%async_computation.10 | async-start | bytes 65536 | tf_op jit(solution)/shard_map/all_to_all | solution.py:49
  190.9 15.4 %all-to-all-start.2 = ((f32[64,1,36]{2,1,0:T(1,128)}), f32[64,1,36]{2,1,0:T(1,128)S(1)}, u32[]{:S(2)}, u32[]{:S(2)}) async-start(f32[64,1,36]{2,1,0:T(1,128)} %broadcast_in_dim.281), calls=%async_computation.2 | async-start | bytes 65536 | tf_op jit(solution)/shard_map/all_to_all | solution.py:49
  206.2 15.4 %all-to-all-start.4 = ((f32[8,64,72]{2,1,0:T(8,128)}), f32[8,64,72]{2,1,0:T(8,128)S(1)}, u32[]{:S(2)}, u32[]{:S(2)}) async-start(f32[8,64,72]{2,1,0:T(8,128)} %bitcast.365), calls=%async_computation.4 | async-start | bytes 524288 | tf_op jit(solution)/shard_map/all_to_all | solution.py:28
  222.2 8.8 %all-to-all-start.11 = ((f32[8,64,1]{1,2,0:T(1,128)}), f32[8,64,1]{1,2,0:T(1,128)S(1)}, u32[]{:S(2)}, u32[]{:S(2)}) async-start(f32[8,64,1]{1,2,0:T(1,128)} %broadcast_in_dim.289), calls=%async_computation.11 | async-start | bytes 8192 | tf_op jit(solution)/shard_map/all_to_all | solution.py:49
  231.0 15.4 %all-to-all-start.5 = ((f32[64,1,72]{2,1,0:T(1,128)}), f32[64,1,72]{2,1,0:T(1,128)S(1)}, u32[]{:S(2)}, u32[]{:S(2)}) async-start(f32[64,1,72]{2,1,0:T(1,128)} %bitcast.130), calls=%async_computation.5 | async-start | bytes 65536 | tf_op jit(solution)/shard_map/all_to_all | solution.py:36
  246.4 10.0 %all-to-all-start.3 = ((f32[8,1,2304]{2,1,0:T(1,128)}), f32[8,1,2304]{2,1,0:T(1,128)S(1)}, u32[]{:S(2)}, u32[]{:S(2)}) async-start(f32[8,1,2304]{2,1,0:T(1,128)} %reshape.493), calls=%async_computation.3 | async-start | bytes 147456 | tf_op jit(solution)/shard_map/all_to_all | solution.py:49
  257.1 15.4 %all-to-all-start.6 = ((f32[64,1,72]{2,1,0:T(1,128)}), f32[64,1,72]{2,1,0:T(1,128)S(1)}, u32[]{:S(2)}, u32[]{:S(2)}) async-start(f32[64,1,72]{2,1,0:T(1,128)} %broadcast_in_dim.284), calls=%async_computation.6 | async-start | bytes 65536 | tf_op jit(solution)/shard_map/all_to_all | solution.py:49
  273.2 11.7 %all-to-all-start.7 = ((f32[8,64,72]{2,1,0:T(8,128)}), f32[8,64,72]{2,1,0:T(8,128)S(1)}, u32[]{:S(2)}, u32[]{:S(2)}) async-start(f32[8,64,72]{2,1,0:T(8,128)} %broadcast_in_dim.286), calls=%async_computation.7 | async-start | bytes 524288 | tf_op jit(solution)/shard_map/all_to_all | solution.py:49
  (12 other events, 75.5 us)
where the time goes:
time: 287 us; the launch traced here: 286 us
  waiting for transfers between devices  108 us (38%)
  starting transfers between devices  105 us (37%)
  local copies, waits for them, and re-layouts  27.9 us (10%)
  other arithmetic  27.7 us (10%)
  matrix products  14.5 us (5%)
    all_to_all x8, waiting for transfers between devices, from_everyone(): lax.all_to_all(jnp.broadcast_to(value[None], (peers, *value.shape)), axis...  47.3 us
    all_to_all x4, waiting for transfers between devices, summed_rows(): lax.all_to_all(nearer, far, split_axis=0, concat_axis=0, tiled=True)  40.8 us
    all_to_all x8, starting transfers between devices, from_everyone(): lax.all_to_all(jnp.broadcast_to(value[None], (peers, *value.shape)), axis...  37.2 us
    all_to_all x4, starting transfers between devices, summed_rows(): lax.all_to_all(nearer, far, split_axis=0, concat_axis=0, tiled=True)  32.1 us
    all_to_all x4, starting transfers between devices, sent_and_summed(): lax.all_to_all(cut_along(value, dim, peers), axis, 0, 0, tiled=True)  23 us
    all_to_all x4, waiting for transfers between devices, sent_and_summed(): lax.all_to_all(cut_along(value, dim, peers), axis, 0, 0, tiled=True)  18 us
    scatter-add x9, other arithmetic, input_grad(): total = total.at[:, row_off:row_off + 2 * size:2, col_off:col_off + 2 * s...  13.7 us
    ppermute x3, starting transfers between devices, from_behind(): lax.ppermute(value, axis, [(source, source + steps) for source in range(f...  12.8 us
  transfers between devices with their start and end apart: 19, of which 17 were waited for; matrix products, arithmetic and copies ran while one was open for 11% of the time, Pallas kernels for 0%

commit v1 on v0

--- a/solution.py
+++ b/solution.py
@@ -214,11 +214,14 @@
         grad_act, hidden_one, normed_one, inverse_one, gain_one
     )
     grad_weight_one = weight_grad(padded_one, grad_z_one.astype(jnp.bfloat16))
+    parts = (grad_weight_one, grad_weight_two, grad_gain_one, grad_gain_two)
+    flat = jnp.concatenate([part.reshape(-1) for part in parts])
+    flat = lax.psum(flat, ("dp", "space_0", "space_1", "space_2"))
+    sizes = [part.size for part in parts]
+    bounds = [sum(sizes[:index]) for index in range(len(sizes) + 1)]
     grad_weight_one, grad_weight_two, grad_gain_one, grad_gain_two = (
-        total_of(grad_weight_one, (("dp", "space_0"), ("space_1", "space_2"))),
-        total_of(grad_weight_two, (("dp", "space_0"), ("space_1", "space_2"))),
-        total_of(grad_gain_one, (("dp", "space_0"), ("space_1", "space_2"))),
-        total_of(grad_gain_two, (("dp", "space_0"), ("space_1", "space_2"))),
+        flat[start:end].reshape(part.shape)
+        for start, end, part in zip(bounds[:-1], bounds[1:], parts)
     )
     return (grad_weight_one, grad_weight_two, grad_gain_one, grad_gain_two)
 

time: 287 us -> 358 us (1.25)
  waiting for transfers between devices: 108 us -> 275 us
  starting transfers between devices: 105 us -> 13 us
  between operations: 2.56 us -> 15.8 us
  local copies, waits for them, and re-layouts: 27.9 us -> 19.4 us
  other arithmetic: 27.7 us -> 21 us
    psum x0 -> x1, waiting for transfers between devices: none -> 273 us  [on_device(): flat = lax.psum(flat, ('dp', 'space_0', 'space_1', 'space_2'))]
    all_to_all x16 -> x0, waiting for transfers between devices: 106 us -> none  [the longest x8 47.3 us: from_everyone(): lax.all_to_all(jnp.broadcast_to(value[None], (peers, *value.shape)), axis...]
    all_to_all x16 -> x0, starting transfers between devices: 92.3 us -> none  [the longest x8 37.2 us: from_everyone(): lax.all_to_all(jnp.broadcast_to(value[None], (peers, *value.shape)), axis...]
    broadcast_in_dim x8 -> x0, local copies, waits for them, and re-layouts: 5.81 us -> none  [from_everyone(): jnp.broadcast_to(value[None], (peers, *value.shape))]
  transfers between devices with their start and end apart: 19 -> 4, of which waited for: 17 -> 2; matrix products, arithmetic and copies ran while one was open for 11% -> 2% of each run, Pallas kernels for 0% -> 0%
where the time goes in v1:
time: 358 us
  waiting for transfers between devices  275 us (77%)
  other arithmetic  21 us (6%)
  local copies, waits for them, and re-layouts  19.4 us (5%)
  between operations  15.8 us (4%)
  matrix products  13.8 us (4%)
  starting transfers between devices  13 us (4%)
    psum x1, waiting for transfers between devices, on_device(): flat = lax.psum(flat, ('dp', 'space_0', 'space_1', 'space_2'))  273 us
    ppermute x3, starting transfers between devices, from_behind(): lax.ppermute(value, axis, [(source, source + steps) for source in range(f...  13 us
    scatter-add x9, other arithmetic, input_grad(): total = total.at[:, row_off:row_off + 2 * size:2, col_off:col_off + 2 * s...  12.1 us
    dot_general x18, matrix products, weight_grad(): jnp.einsum('nijc,nijo->co', window, grad_z, preferred_element_type=jnp.fl...  11 us
  transfers between devices with their start and end apart: 4, of which 2 were waited for; matrix products, arithmetic and copies ran while one was open for 2% of the time, Pallas kernels for 0%

profile of v1, /device:TPU:1, one launch (start us, length us, event | category | flops | bytes accessed | tf_op | source)
XLA Modules:
  0.0 357.9 jit_solution(17097383212291778513)
XLA Ops:
  7.9 1.7 reshape_squeeze.16
  10.4 8.7 %collective-permute-start = (bf16[16,512]{1,0:T(8,128)(2,1)S(1)}, bf16[16,512]{1,0:T(8,128)(2,1)S(1)}, u32[]{:S(2)}, u32[]{:S(2)}) collective-permute-start(bf16[16,512]{1,0:T(8,128)(2,1)S(1)} %reshape_squeeze.18), channel_id=1, source_target_pairs={{1,0},{2,1},{3,2},{4,3},{5,4},{6,5},{7,6},{8,7},{9,8},{10,9},{11,1... | collective-permute-start | bytes 49160 | tf_op jit(solution)/shard_map/ppermute | solution.py:18
  21.4 1.3 pad_maximum_fusion.1
  27.3 1.0 fusion.64
  29.2 2.1 collective-permute-start.1
  32.1 2.2 collective-permute-done.1
  37.6 0.8 convolution_bitcast_fusion.6
  38.4 0.8 convolution_bitcast_fusion.7
  39.2 0.8 convolution_bitcast_fusion.8
  40.8 0.8 convolution_bitcast_fusion.4
  41.6 0.8 convolution_bitcast_fusion.5
  42.4 0.8 convolution_bitcast_fusion.2
  43.2 0.8 convolution_bitcast_fusion
  44.0 0.8 convolution_bitcast_fusion.1
  46.3 1.5 scatter_fusion
  47.7 1.3 scatter_fusion.1
  49.1 1.3 scatter_fusion.2
  50.4 1.3 scatter_fusion.3
  51.7 1.3 scatter_fusion.4
  53.1 1.3 scatter_fusion.5
  54.4 1.3 scatter_fusion.6
  55.7 1.3 scatter_fusion.7
  57.1 1.3 scatter_fusion.8
  58.8 2.2 collective-permute-start.2
  67.2 1.2 convolution_bitcast_fusion.14
  68.4 1.2 convolution_bitcast_fusion.11
  70.2 3.5 concatenate.81
  73.8 272.6 %all-reduce.2.cloned.1.call-done = f32[55424]{0:T(1024)} async-done(((f32[55424]{0:T(1024)}), f32[55424]{0:T(1024)}) %all-reduce.2.cloned.1.call-update) | async-done | bytes 221712 | tf_op jit(solution)/shard_map/psum | solution.py:219
  346.3 0.9 slice.336
  347.2 0.8 reshape.268
  348.1 0.9 slice.335
  349.7 1.3 fusion.63
  (193 shorter events, 22.1 us)
Async XLA Ops:
  7.2 20.1 %copy-start = (bf16[3,3,32,64]{3,2,1,0:T(8,128)(2,1)S(1)}, bf16[3,3,32,64]{3,2,1,0:T(8,128)(2,1)}, u32[]{:S(2)}) copy-start(bf16[3,3,32,64]{3,2,1,0:T(8,128)(2,1)} %param.24) | copy-start | bytes 110596
  7.2 339.1 %all-reduce.2.cloned.1.call-start = ((), (), s32[]{:S(2)}) async-start(), calls=%async_computation | async-start | bytes 450560 | tf_op jit(solution)/shard_map/psum | solution.py:219
  9.6 9.7 %copy-start.16 = (s32[1,16,8]{1,2,0:T(8,128)S(1)}, s32[1,16,8]{1,2,0:T(8,128)}, u32[]{:S(2)}) copy-start(s32[1,16,8]{1,2,0:T(8,128)} %param.23) | copy-start | bytes 1540
  9.6 11.8 %copy-start.6 = (bf16[1,16,4,256]{3,2,1,0:T(4,128)(2,1)S(1)}, bf16[1,16,4,256]{3,2,1,0:T(4,128)(2,1)}, u32[]{:S(2)}) copy-start(bf16[1,16,4,256]{3,2,1,0:T(4,128)(2,1)} %param.21) | copy-start | bytes 98308
  10.4 15.0 %collective-permute-start = (bf16[16,512]{1,0:T(8,128)(2,1)S(1)}, bf16[16,512]{1,0:T(8,128)(2,1)S(1)}, u32[]{:S(2)}, u32[]{:S(2)}) collective-permute-start(bf16[16,512]{1,0:T(8,128)(2,1)S(1)} %reshape_squeeze.18), channel_id=1, source_target_pairs={{1,0},{2,1},{3,2},{4,3},{5,4},{6,5},{7,6},{8,7},{9,8},{10,9},{11,1... | collective-permute-start | bytes 49160 | tf_op jit(solution)/shard_map/ppermute | solution.py:18
  27.2 1.4 copy-start.1
  27.2 1.4 copy-start.17
  28.7 7.3 %copy-start.4 = (f32[16,8,8]{0,2,1:T(8,128)}, f32[16,8,8]{0,2,1:T(8,128)S(1)}, u32[]{:S(2)}) copy-start(f32[16,8,8]{0,2,1:T(8,128)S(1)} %add_rsqrt_fusion) | copy-start | bytes 12292
  28.7 7.3 %copy-start.3 = (bf16[3,3,64,64]{3,2,1,0:T(8,128)(2,1)S(1)}, bf16[3,3,64,64]{3,2,1,0:T(8,128)(2,1)}, u32[]{:S(2)}) copy-start(bf16[3,3,64,64]{3,2,1,0:T(8,128)(2,1)} %param.25) | copy-start | bytes 221188
  29.2 5.1 %collective-permute-start.1 = (bf16[16,512]{1,0:T(8,128)(2,1)S(1)}, bf16[16,512]{1,0:T(8,128)(2,1)S(1)}, u32[]{:S(2)}, u32[]{:S(2)}) collective-permute-start(bf16[16,512]{1,0:T(8,128)(2,1)S(1)} %reshape_squeeze.20), channel_id=1, source_target_pairs={{1,0},{2,1},{3,2},{4,3},{5,4},{6,5},{7,6},{8,7},{9,8},{10,9},{11,1... | collective-permute-start | bytes 49160 | tf_op jit(solution)/shard_map/ppermute | solution.py:18
  31.4 5.2 %copy-start.19 = (f32[64]{0:T(128)S(1)}, f32[64]{0:T(128)}, u32[]{:S(2)}) copy-start(f32[64]{0:T(128)} %param.27) | copy-start | bytes 772
  58.4 3.4 copy-start.25
  58.4 3.4 copy-start.26
  58.5 3.5 copy-start.7
  58.5 3.5 copy-start.8
  58.5 3.5 copy-start.9
  58.5 3.6 copy-start.11
  58.5 3.6 copy-start.12
  58.6 3.6 copy-start.13
  58.6 3.6 copy-start.10
  58.6 3.6 copy-start.14
  58.6 3.6 copy-start.15
  58.8 3.5 collective-permute-start.2
  61.1 2.0 copy-start.22
  61.1 2.0 copy-start.24
  62.0 2.0 copy-start.21
  62.1 2.0 copy-start.23
  62.2 2.1 copy-start.5
  62.2 2.1 copy-start.18
  65.0 1.3 copy-start.2
  69.6 0.7 copy-start.20
Sparse Core Ops, SparseCore 0:
  73.9 272.3 all-reduce.1

commit v2 on v1

--- a/solution.py
+++ b/solution.py
@@ -216,7 +216,7 @@
     grad_weight_one = weight_grad(padded_one, grad_z_one.astype(jnp.bfloat16))
     parts = (grad_weight_one, grad_weight_two, grad_gain_one, grad_gain_two)
     flat = jnp.concatenate([part.reshape(-1) for part in parts])
-    flat = lax.psum(flat, ("dp", "space_0", "space_1", "space_2"))
+    flat = total_of(flat, (("dp", "space_0"), ("space_1", "space_2")))
     sizes = [part.size for part in parts]
     bounds = [sum(sizes[:index]) for index in range(len(sizes) + 1)]
     grad_weight_one, grad_weight_two, grad_gain_one, grad_gain_two = (

time: 358 us -> 132 us (0.37)
  waiting for transfers between devices: 275 us -> 2.21 us
  blocking collectives: 0 us -> 63.6 us
  between operations: 15.8 us -> 2.51 us
  local copies, waits for them, and re-layouts: 19.4 us -> 15.4 us
    psum x1 -> x0, waiting for transfers between devices: 273 us -> none  [on_device(): flat = lax.psum(flat, ('dp', 'space_0', 'space_1', 'space_2'))]
    all_to_all x0 -> x4, blocking collectives: none -> 63.6 us  [the longest x2 27.2 us: from_everyone(): lax.all_to_all(jnp.broadcast_to(value[None], (peers, *value.shape)), axis...]
  transfers between devices with their start and end apart: 4 -> 3, of which waited for: 2 -> 1; matrix products, arithmetic and copies ran while one was open for 2% -> 6% of each run, Pallas kernels for 0% -> 0%
where the time goes in v2:
time: 132 us
  blocking collectives  63.6 us (48%)
  other arithmetic  21.1 us (16%)
  local copies, waits for them, and re-layouts  15.4 us (12%)
  matrix products  13.8 us (10%)
  starting transfers between devices  13 us (10%)
  between operations  2.51 us (2%)
  waiting for transfers between devices  2.21 us (2%)
    all_to_all x2, blocking collectives, from_everyone(): lax.all_to_all(jnp.broadcast_to(value[None], (peers, *value.shape)), axis...  27.2 us
    all_to_all x1, blocking collectives, summed_rows(): lax.all_to_all(nearer, far, split_axis=0, concat_axis=0, tiled=True)  26.9 us
    ppermute x3, starting transfers between devices, from_behind(): lax.ppermute(value, axis, [(source, source + steps) for source in range(f...  13 us
    scatter-add x9, other arithmetic, input_grad(): total = total.at[:, row_off:row_off + 2 * size:2, col_off:col_off + 2 * s...  12.1 us
    dot_general x18, matrix products, weight_grad(): jnp.einsum('nijc,nijo->co', window, grad_z, preferred_element_type=jnp.fl...  11 us
    all_to_all x1, blocking collectives, sent_and_summed(): lax.all_to_all(cut_along(value, dim, peers), axis, 0, 0, tiled=True)  9.49 us
    gather x9, local copies, waits for them, and re-layouts, select_rows(): picked = jnp.take(source, positions, axis=0)  5.69 us
  transfers between devices with their start and end apart: 3, of which 1 were waited for; matrix products, arithmetic and copies ran while one was open for 6% of the time, Pallas kernels for 0%

profile of v2, /device:TPU:1, one launch (start us, length us, event | category | flops | bytes accessed | tf_op | source)
XLA Modules:
  0.0 131.6 jit_solution(9712209354143488013)
XLA Ops:
  1.3 1.7 %reshape_squeeze.16 = bf16[16,16,16,32]{3,2,1,0:T(8,128)(2,1)S(1)} reshape(bf16[1,16,16,512]{3,2,1,0:T(8,128)(2,1)} %param.20) | data formatting | bytes 524288 | tf_op jit(solution)/shard_map/reshape;squeeze | solution.py:158
  3.9 8.7 %collective-permute-start = (bf16[16,512]{1,0:T(8,128)(2,1)S(1)}, bf16[16,512]{1,0:T(8,128)(2,1)S(1)}, u32[]{:S(2)}, u32[]{:S(2)}) collective-permute-start(bf16[16,512]{1,0:T(8,128)(2,1)S(1)} %reshape_squeeze.18), channel_id=1, source_target_pairs={{1,0},{2,1},{3,2},{4,3},{5,4},{6,5},{7,6},{8,7},{9,8},{10,9},{11,1... | collective-permute-start | bytes 49160 | tf_op jit(solution)/shard_map/ppermute | solution.py:18
  14.9 1.3 pad_maximum_fusion.1
  20.7 1.0 fusion.64
  22.7 2.1 %collective-permute-start.1 = (bf16[16,512]{1,0:T(8,128)(2,1)S(1)}, bf16[16,512]{1,0:T(8,128)(2,1)S(1)}, u32[]{:S(2)}, u32[]{:S(2)}) collective-permute-start(bf16[16,512]{1,0:T(8,128)(2,1)S(1)} %reshape_squeeze.20), channel_id=1, source_target_pairs={{1,0},{2,1},{3,2},{4,3},{5,4},{6,5},{7,6},{8,7},{9,8},{10,9},{11,1... | collective-permute-start | bytes 49160 | tf_op jit(solution)/shard_map/ppermute | solution.py:18
  25.5 2.2 %collective-permute-done.1 = bf16[16,512]{1,0:T(8,128)(2,1)S(1)} collective-permute-done((bf16[16,512]{1,0:T(8,128)(2,1)S(1)}, bf16[16,512]{1,0:T(8,128)(2,1)S(1)}, u32[]{:S(2)}, u32[]{:S(2)}) %collective-permute-start.1) | collective-permute-done | bytes 16416 | tf_op jit(solution)/shard_map/ppermute | solution.py:18
  31.0 0.8 convolution_bitcast_fusion.6
  31.8 0.8 convolution_bitcast_fusion.7
  32.6 0.8 convolution_bitcast_fusion.8
  34.3 0.8 convolution_bitcast_fusion.4
  35.0 0.8 convolution_bitcast_fusion.5
  35.8 0.8 convolution_bitcast_fusion.2
  36.6 0.8 convolution_bitcast_fusion
  37.4 0.8 convolution_bitcast_fusion.1
  39.7 1.5 %scatter_fusion = f32[16,9,9,64]{3,0,2,1:T(8,128)S(1)} fusion(f32[16,9,9,64]{3,0,2,1:T(8,128)S(1)} %broadcast_in_dim.225, s32[16]{0:T(128)} %reshape.354, f32[16,16,64]{2,1,0:T(8,128)S(1)} %bitcast.353), kind=kCustom, calls=%fused_computation.9 | custom fusion | flops 16384 | bytes 196736 | tf_op jit(solution)/shard_map/scatter-add | solution.py:143
  41.2 1.3 %scatter_fusion.1 = f32[16,9,9,64]{3,0,2,1:T(8,128)S(1)} fusion(f32[16,9,9,64]{3,0,2,1:T(8,128)S(1)} %scatter_fusion, s32[16]{0:T(128)S(1)} %reshape.360, f32[16,16,64]{2,1,0:T(8,128)S(1)} %bitcast.352), kind=kCustom, calls=%fused_computation.10 | custom fusion | flops 16384 | bytes 196736 | tf_op jit(solution)/shard_map/scatter-add | solution.py:143
  42.5 1.3 %scatter_fusion.2 = f32[16,9,9,64]{3,0,2,1:T(8,128)S(1)} fusion(f32[16,9,9,64]{3,0,2,1:T(8,128)S(1)} %scatter_fusion.1, s32[16]{0:T(128)S(1)} %reshape.366, f32[16,16,64]{2,1,0:T(8,128)S(1)} %bitcast.351), kind=kCustom, calls=%fused_computation.11 | custom fusion | flops 16384 | bytes 196736 | tf_op jit(solution)/shard_map/scatter-add | solution.py:143
  43.8 1.3 %scatter_fusion.3 = f32[16,9,9,64]{3,0,2,1:T(8,128)S(1)} fusion(f32[16,9,9,64]{3,0,2,1:T(8,128)S(1)} %scatter_fusion.2, s32[16]{0:T(128)S(1)} %reshape.372, f32[16,16,64]{2,1,0:T(8,128)S(1)} %bitcast.350), kind=kCustom, calls=%fused_computation.12 | custom fusion | flops 16384 | bytes 196736 | tf_op jit(solution)/shard_map/scatter-add | solution.py:143
  45.2 1.3 %scatter_fusion.4 = f32[16,9,9,64]{3,0,2,1:T(8,128)S(1)} fusion(f32[16,9,9,64]{3,0,2,1:T(8,128)S(1)} %scatter_fusion.3, s32[16]{0:T(128)S(1)} %reshape.378, f32[16,16,64]{2,1,0:T(8,128)S(1)} %bitcast.349), kind=kCustom, calls=%fused_computation.13 | custom fusion | flops 16384 | bytes 196736 | tf_op jit(solution)/shard_map/scatter-add | solution.py:143
  46.5 1.3 %scatter_fusion.5 = f32[16,9,9,64]{3,0,2,1:T(8,128)S(1)} fusion(f32[16,9,9,64]{3,0,2,1:T(8,128)S(1)} %scatter_fusion.4, s32[16]{0:T(128)S(1)} %reshape.384, f32[16,16,64]{2,1,0:T(8,128)S(1)} %bitcast.348), kind=kCustom, calls=%fused_computation.14 | custom fusion | flops 16384 | bytes 196736 | tf_op jit(solution)/shard_map/scatter-add | solution.py:143
  47.9 1.3 %scatter_fusion.6 = f32[16,9,9,64]{3,0,2,1:T(8,128)S(1)} fusion(f32[16,9,9,64]{3,0,2,1:T(8,128)S(1)} %scatter_fusion.5, s32[16]{0:T(128)S(1)} %reshape.390, f32[16,16,64]{2,1,0:T(8,128)S(1)} %bitcast.347), kind=kCustom, calls=%fused_computation.15 | custom fusion | flops 16384 | bytes 196736 | tf_op jit(solution)/shard_map/scatter-add | solution.py:143
  49.2 1.3 %scatter_fusion.7 = f32[16,9,9,64]{3,0,2,1:T(8,128)S(1)} fusion(f32[16,9,9,64]{3,0,2,1:T(8,128)S(1)} %scatter_fusion.6, s32[16]{0:T(128)S(1)} %reshape.396, f32[16,16,64]{2,1,0:T(8,128)S(1)} %bitcast.346), kind=kCustom, calls=%fused_computation.16 | custom fusion | flops 16384 | bytes 196736 | tf_op jit(solution)/shard_map/scatter-add | solution.py:143
  50.5 1.3 %scatter_fusion.8 = f32[16,9,9,64]{3,0,2,1:T(8,128)S(1)} fusion(f32[16,9,9,64]{3,0,2,1:T(8,128)S(1)} %scatter_fusion.7, s32[16]{0:T(128)S(1)} %reshape.402, f32[16,16,64]{2,1,0:T(8,128)S(1)} %bitcast.345), kind=kCustom, calls=%fused_computation.17 | custom fusion | flops 16384 | bytes 196736 | tf_op jit(solution)/shard_map/scatter-add | solution.py:143
  52.3 2.2 %collective-permute-start.2 = (bf16[16,576]{1,0:T(8,128)(2,1)S(1)}, bf16[16,576]{1,0:T(8,128)(2,1)S(1)}, u32[]{:S(2)}, u32[]{:S(2)}) collective-permute-start(bf16[16,576]{1,0:T(8,128)(2,1)S(1)} %convert_element_type.52), channel_id=1, source_target_pairs={{0,1},{1,2},{2,3},{3,4},{4,5},{5,6},{6,7},{7,8},{8,9},{9,10},{10,1... | collective-permute-start | bytes 55304 | tf_op jit(solution)/shard_map/ppermute | solution.py:18
  60.7 1.2 convolution_bitcast_fusion.14
  61.9 1.2 convolution_bitcast_fusion.11
  63.7 1.0 concatenate.81
  65.2 9.5 %all_to_all.25 = f32[8,64,109]{2,1,0:T(8,128)S(1)} all-to-all(f32[8,64,109]{2,1,0:T(8,128)S(1)} %copy.66), channel_id=1, replica_groups=mesh['dp'=8,'space_0'=8,'space_1'=4,'space_2'=2] {'space_1','space_2'}, dimensions={0} | all-to-all | bytes 446464 | tf_op jit(solution)/shard_map/all_to_all | solution.py:28
  74.7 26.9 %all_to_all.26 = f32[64,1,109]{2,1,0:T(1,128)S(1)} all-to-all(f32[64,1,109]{2,1,0:T(1,128)S(1)} %bitcast.354), channel_id=1, replica_groups=mesh['dp'=8,'space_0'=8,'space_1'=4,'space_2'=2] {'dp','space_0'}, dimensions={0} | all-to-all | bytes 55808 | tf_op jit(solution)/shard_map/all_to_all | solution.py:36
  101.7 14.7 %all_to_all.27 = f32[64,1,109]{2,1,0:T(1,128)S(1)} all-to-all(f32[64,1,109]{2,1,0:T(1,128)S(1)} %broadcast_in_dim.243), channel_id=1, replica_groups=mesh['dp'=8,'space_0'=8,'space_1'=4,'space_2'=2] {'dp','space_0'}, dimensions={0} | all-to-all | bytes 55808 | tf_op jit(solution)/shard_map/all_to_all | solution.py:49
  116.4 12.5 %all_to_all.28 = f32[8,64,109]{2,1,0:T(8,128)S(1)} all-to-all(f32[8,64,109]{2,1,0:T(8,128)S(1)} %broadcast_in_dim.245), channel_id=1, replica_groups=mesh['dp'=8,'space_0'=8,'space_1'=4,'space_2'=2] {'space_1','space_2'}, dimensions={0} | all-to-all | bytes 446464 | tf_op jit(solution)/shard_map/all_to_all | solution.py:49
  130.0 0.8 reshape.278
  (203 shorter events, 23.7 us)
Async XLA Ops:
  0.6 20.0 %copy-start = (bf16[3,3,32,64]{3,2,1,0:T(8,128)(2,1)S(1)}, bf16[3,3,32,64]{3,2,1,0:T(8,128)(2,1)}, u32[]{:S(2)}) copy-start(bf16[3,3,32,64]{3,2,1,0:T(8,128)(2,1)} %param.24) | copy-start | bytes 110596
  3.1 9.7 %copy-start.16 = (s32[1,16,8]{1,2,0:T(8,128)S(1)}, s32[1,16,8]{1,2,0:T(8,128)}, u32[]{:S(2)}) copy-start(s32[1,16,8]{1,2,0:T(8,128)} %param.23) | copy-start | bytes 1540
  3.1 11.8 %copy-start.6 = (bf16[1,16,4,256]{3,2,1,0:T(4,128)(2,1)S(1)}, bf16[1,16,4,256]{3,2,1,0:T(4,128)(2,1)}, u32[]{:S(2)}) copy-start(bf16[1,16,4,256]{3,2,1,0:T(4,128)(2,1)} %param.21) | copy-start | bytes 98308
  3.9 15.0 %collective-permute-start = (bf16[16,512]{1,0:T(8,128)(2,1)S(1)}, bf16[16,512]{1,0:T(8,128)(2,1)S(1)}, u32[]{:S(2)}, u32[]{:S(2)}) collective-permute-start(bf16[16,512]{1,0:T(8,128)(2,1)S(1)} %reshape_squeeze.18), channel_id=1, source_target_pairs={{1,0},{2,1},{3,2},{4,3},{5,4},{6,5},{7,6},{8,7},{9,8},{10,9},{11,1... | collective-permute-start | bytes 49160 | tf_op jit(solution)/shard_map/ppermute | solution.py:18
  20.7 1.4 %copy-start.1 = (bf16[16,17,17,32]{3,0,2,1:T(8,128)(2,1)}, bf16[16,17,17,32]{3,0,2,1:T(8,128)(2,1)S(1)}, u32[]{:S(2)}) copy-start(bf16[16,17,17,32]{3,0,2,1:T(8,128)(2,1)S(1)} %pad_maximum_fusion) | copy-start | bytes 887812
  20.7 1.4 %copy-start.17 = (f32[64]{0:T(128)S(1)}, f32[64]{0:T(128)}, u32[]{:S(2)}) copy-start(f32[64]{0:T(128)} %param.26) | copy-start | bytes 772
  22.1 7.3 %copy-start.4 = (f32[16,8,8]{0,2,1:T(8,128)}, f32[16,8,8]{0,2,1:T(8,128)S(1)}, u32[]{:S(2)}) copy-start(f32[16,8,8]{0,2,1:T(8,128)S(1)} %add_rsqrt_fusion) | copy-start | bytes 12292
  22.2 7.3 %copy-start.3 = (bf16[3,3,64,64]{3,2,1,0:T(8,128)(2,1)S(1)}, bf16[3,3,64,64]{3,2,1,0:T(8,128)(2,1)}, u32[]{:S(2)}) copy-start(bf16[3,3,64,64]{3,2,1,0:T(8,128)(2,1)} %param.25) | copy-start | bytes 221188
  22.7 5.1 %collective-permute-start.1 = (bf16[16,512]{1,0:T(8,128)(2,1)S(1)}, bf16[16,512]{1,0:T(8,128)(2,1)S(1)}, u32[]{:S(2)}, u32[]{:S(2)}) collective-permute-start(bf16[16,512]{1,0:T(8,128)(2,1)S(1)} %reshape_squeeze.20), channel_id=1, source_target_pairs={{1,0},{2,1},{3,2},{4,3},{5,4},{6,5},{7,6},{8,7},{9,8},{10,9},{11,1... | collective-permute-start | bytes 49160 | tf_op jit(solution)/shard_map/ppermute | solution.py:18
  24.8 5.2 %copy-start.19 = (f32[64]{0:T(128)S(1)}, f32[64]{0:T(128)}, u32[]{:S(2)}) copy-start(f32[64]{0:T(128)} %param.27) | copy-start | bytes 772
  51.9 3.4 %copy-start.25 = (pred[16]{0:T(512)(128)(4,1)S(1)}, pred[16]{0:T(512)(128)(4,1)}, u32[]{:S(2)}) copy-start(pred[16]{0:T(512)(128)(4,1)} %get-tuple-element.69) | copy-start | bytes 52
  51.9 3.4 %copy-start.26 = (pred[16]{0:T(512)(128)(4,1)S(1)}, pred[16]{0:T(512)(128)(4,1)}, u32[]{:S(2)}) copy-start(pred[16]{0:T(512)(128)(4,1)} %get-tuple-element.79) | copy-start | bytes 52
  52.0 3.5 %copy-start.7 = (f32[1,64,64]{2,1,0:T(8,128)S(1)}, f32[1,64,64]{2,1,0:T(8,128)}, u32[]{:S(2)}) copy-start(f32[1,64,64]{2,1,0:T(8,128)} %convolution_bitcast_fusion.6) | copy-start | bytes 49156
  52.0 3.5 %copy-start.8 = (f32[1,64,64]{2,1,0:T(8,128)S(1)}, f32[1,64,64]{2,1,0:T(8,128)}, u32[]{:S(2)}) copy-start(f32[1,64,64]{2,1,0:T(8,128)} %convolution_bitcast_fusion.7) | copy-start | bytes 49156
  52.0 3.5 %copy-start.9 = (f32[1,64,64]{2,1,0:T(8,128)S(1)}, f32[1,64,64]{2,1,0:T(8,128)}, u32[]{:S(2)}) copy-start(f32[1,64,64]{2,1,0:T(8,128)} %convolution_bitcast_fusion.8) | copy-start | bytes 49156
  52.0 3.6 %copy-start.11 = (f32[1,64,64]{2,1,0:T(8,128)S(1)}, f32[1,64,64]{2,1,0:T(8,128)}, u32[]{:S(2)}) copy-start(f32[1,64,64]{2,1,0:T(8,128)} %convolution_bitcast_fusion.3) | copy-start | bytes 49156
  52.0 3.6 %copy-start.12 = (f32[1,64,64]{2,1,0:T(8,128)S(1)}, f32[1,64,64]{2,1,0:T(8,128)}, u32[]{:S(2)}) copy-start(f32[1,64,64]{2,1,0:T(8,128)} %convolution_bitcast_fusion.4) | copy-start | bytes 49156
  52.0 3.6 %copy-start.13 = (f32[1,64,64]{2,1,0:T(8,128)S(1)}, f32[1,64,64]{2,1,0:T(8,128)}, u32[]{:S(2)}) copy-start(f32[1,64,64]{2,1,0:T(8,128)} %convolution_bitcast_fusion.5) | copy-start | bytes 49156
  52.0 3.6 %copy-start.10 = (f32[1,64,64]{2,1,0:T(8,128)S(1)}, f32[1,64,64]{2,1,0:T(8,128)}, u32[]{:S(2)}) copy-start(f32[1,64,64]{2,1,0:T(8,128)} %convolution_bitcast_fusion.2) | copy-start | bytes 49156
  52.0 3.6 %copy-start.14 = (f32[1,64,64]{2,1,0:T(8,128)S(1)}, f32[1,64,64]{2,1,0:T(8,128)}, u32[]{:S(2)}) copy-start(f32[1,64,64]{2,1,0:T(8,128)} %convolution_bitcast_fusion) | copy-start | bytes 49156
  52.0 3.6 %copy-start.15 = (f32[1,64,64]{2,1,0:T(8,128)S(1)}, f32[1,64,64]{2,1,0:T(8,128)}, u32[]{:S(2)}) copy-start(f32[1,64,64]{2,1,0:T(8,128)} %convolution_bitcast_fusion.1) | copy-start | bytes 49156
  52.3 3.5 %collective-permute-start.2 = (bf16[16,576]{1,0:T(8,128)(2,1)S(1)}, bf16[16,576]{1,0:T(8,128)(2,1)S(1)}, u32[]{:S(2)}, u32[]{:S(2)}) collective-permute-start(bf16[16,576]{1,0:T(8,128)(2,1)S(1)} %convert_element_type.52), channel_id=1, source_target_pairs={{0,1},{1,2},{2,3},{3,4},{4,5},{5,6},{6,7},{7,8},{8,9},{9,10},{10,1... | collective-permute-start | bytes 55304 | tf_op jit(solution)/shard_map/ppermute | solution.py:18
  54.5 2.0 %copy-start.22 = (pred[16]{0:T(512)(128)(4,1)S(1)}, pred[16]{0:T(512)(128)(4,1)}, u32[]{:S(2)}) copy-start(pred[16]{0:T(512)(128)(4,1)} %get-tuple-element.68) | copy-start | bytes 52
  54.5 2.0 %copy-start.24 = (pred[16]{0:T(512)(128)(4,1)S(1)}, pred[16]{0:T(512)(128)(4,1)}, u32[]{:S(2)}) copy-start(pred[16]{0:T(512)(128)(4,1)} %get-tuple-element.81) | copy-start | bytes 52
  55.5 2.0 %copy-start.21 = (pred[16]{0:T(512)(128)(4,1)S(1)}, pred[16]{0:T(512)(128)(4,1)}, u32[]{:S(2)}) copy-start(pred[16]{0:T(512)(128)(4,1)} %get-tuple-element.67) | copy-start | bytes 52
  55.5 2.0 %copy-start.23 = (pred[16]{0:T(512)(128)(4,1)S(1)}, pred[16]{0:T(512)(128)(4,1)}, u32[]{:S(2)}) copy-start(pred[16]{0:T(512)(128)(4,1)} %get-tuple-element.50) | copy-start | bytes 52
  55.6 2.1 %copy-start.5 = (f32[16,8,8]{0,2,1:T(8,128)S(1)}, f32[16,8,8]{0,2,1:T(8,128)}, u32[]{:S(2)}) copy-start(f32[16,8,8]{0,2,1:T(8,128)} %copy-done.4) | copy-start | bytes 12292
  55.6 2.1 %copy-start.18 = (f32[64]{0:T(128)S(1)}, f32[64]{0:T(128)}, u32[]{:S(2)}) copy-start(f32[64]{0:T(128)} %param.26) | copy-start | bytes 772
  58.5 1.3 copy-start.2
  63.0 0.7 copy-start.20

commit v3 on v2

--- a/solution.py
+++ b/solution.py
@@ -112,36 +112,27 @@
 
 
 def weight_grad(padded, grad_z):
-    size = grad_z.shape[1]
-    blocks = []
-    for row_off in range(3):
-        line = []
-        for col_off in range(3):
-            window = padded[
-                :, row_off : row_off + 2 * size : 2, col_off : col_off + 2 * size : 2, :
-            ]
-            line.append(
-                jnp.einsum("nijc,nijo->co", window, grad_z, preferred_element_type=jnp.float32)
-            )
-        blocks.append(jnp.stack(line))
-    return jnp.stack(blocks)
+    return lax.conv_general_dilated(
+        padded,
+        grad_z,
+        (1, 1),
+        "VALID",
+        rhs_dilation=(2, 2),
+        dimension_numbers=("CHWN", "IHWO", "HWNC"),
+        preferred_element_type=jnp.float32,
+    )
 
 
 def input_grad(grad_z, weight):
-    size = grad_z.shape[1]
-    total = jnp.zeros((grad_z.shape[0], 2 * size + 1, 2 * size + 1, weight.shape[2]), jnp.float32)
-    for row_off in range(3):
-        for col_off in range(3):
-            term = jnp.einsum(
-                "nijo,co->nijc",
-                grad_z,
-                weight[row_off, col_off],
-                preferred_element_type=jnp.float32,
-            )
-            total = total.at[
-                :, row_off : row_off + 2 * size : 2, col_off : col_off + 2 * size : 2, :
-            ].add(term)
-    return total
+    return lax.conv_general_dilated(
+        grad_z,
+        weight[::-1, ::-1],
+        (1, 1),
+        ((2, 2), (2, 2)),
+        lhs_dilation=(2, 2),
+        dimension_numbers=("NHWC", "HWOI", "NHWC"),
+        preferred_element_type=jnp.float32,
+    )
 
 
 def on_device(image, cotangent, live_count, neighbours, weight_one, weight_two, gain_one, gain_two):

time: 132 us -> 108 us (0.82)
  other arithmetic: 21.1 us -> 7.22 us
  matrix products: 13.8 us -> 3.59 us
  blocking collectives: 63.6 us -> 66.2 us
  local copies, waits for them, and re-layouts: 15.4 us -> 13.4 us
    dot_general x27 -> x0, matrix products: 12.4 us -> none  [the longest x18 11 us: weight_grad(): jnp.einsum('nijc,nijo->co', window, grad_z, preferred_element_type=jnp.fl...]
    scatter-add x9 -> x0, other arithmetic: 12.1 us -> none  [input_grad(): total = total.at[:, row_off:row_off + 2 * size:2, col_off:col_off + 2 * s...]
    all_to_all x1, blocking collectives: 26.9 us -> 29.1 us  [summed_rows(): lax.all_to_all(nearer, far, split_axis=0, concat_axis=0, tiled=True)]
    conv_general_dilated x0 -> x3, matrix products: none -> 2.03 us  [the longest x2 1.67 us: weight_grad(): lax.conv_general_dilated(padded, grad_z, (1, 1), 'VALID', rhs_dilation=(2...]
    concatenate x10 -> x0, other arithmetic: 1.78 us -> none  [the longest x2 1.32 us: assemble(): lower = jnp.concatenate([field, south_rows[:, None]], axis=1)]
    concatenate x9 -> x0, local copies, waits for them, and re-layouts: 1.33 us -> none  [input_grad(): total = total.at[:, row_off:row_off + 2 * size:2, col_off:col_off + 2 * s...]
  transfers between devices with their start and end apart: 3 -> 3, of which waited for: 1 -> 2; matrix products, arithmetic and copies ran while one was open for 6% -> 5% of each run, Pallas kernels for 0% -> 0%
where the time goes in v3:
time: 108 us; the launch traced here: 107 us
  blocking collectives  66.2 us (61%)
  local copies, waits for them, and re-layouts  13.4 us (12%)
  starting transfers between devices  12.6 us (12%)
  other arithmetic  7.22 us (7%)
  matrix products  3.59 us (3%)
  waiting for transfers between devices  2.28 us (2%)
  between operations  1.96 us (2%)
    all_to_all x1, blocking collectives, summed_rows(): lax.all_to_all(nearer, far, split_axis=0, concat_axis=0, tiled=True)  29.1 us
    all_to_all x2, blocking collectives, from_everyone(): lax.all_to_all(jnp.broadcast_to(value[None], (peers, *value.shape)), axis...  27.2 us
    ppermute x3, starting transfers between devices, from_behind(): lax.ppermute(value, axis, [(source, source + steps) for source in range(f...  12.6 us
    all_to_all x1, blocking collectives, sent_and_summed(): lax.all_to_all(cut_along(value, dim, peers), axis, 0, 0, tiled=True)  9.98 us
    gather x9, local copies, waits for them, and re-layouts, select_rows(): picked = jnp.take(source, positions, axis=0)  5.56 us
    ppermute x3, waiting for transfers between devices, from_behind(): lax.ppermute(value, axis, [(source, source + steps) for source in range(f...  2.28 us
  transfers between devices with their start and end apart: 3, of which 2 were waited for; matrix products, arithmetic and copies ran while one was open for 5% of the time, Pallas kernels for 0%

profile of v3, /device:TPU:1, one launch (start us, length us, event | category | flops | bytes accessed | tf_op | source)
XLA Modules:
  0.0 107.3 jit_solution(1997877108203846342)
XLA Ops:
  1.3 1.7 %reshape_squeeze.16 = bf16[16,16,16,32]{3,2,1,0:T(8,128)(2,1)S(1)} reshape(bf16[1,16,16,512]{3,2,1,0:T(8,128)(2,1)} %param.20) | data formatting | bytes 524288 | tf_op jit(solution)/shard_map/reshape;squeeze | solution.py:149
  3.1 0.6 copy_select_fusion
  3.9 8.7 %collective-permute-start = (bf16[16,512]{1,0:T(8,128)(2,1)S(1)}, bf16[16,512]{1,0:T(8,128)(2,1)S(1)}, u32[]{:S(2)}, u32[]{:S(2)}) collective-permute-start(bf16[16,512]{1,0:T(8,128)(2,1)S(1)} %reshape_squeeze.18), channel_id=1, source_target_pairs={{1,0},{2,1},{3,2},{4,3},{5,4},{6,5},{7,6},{8,7},{9,8},{10,9},{11,1... | collective-permute-start | bytes 49160 | tf_op jit(solution)/shard_map/ppermute | solution.py:18
  12.7 0.6 compare_bitcast_fusion
  13.3 0.6 compare_and_fusion
  13.9 0.6 pad_clamp_fusion.2
  14.7 0.6 gather_fusion
  15.4 0.6 pad_clamp_fusion.1
  16.2 0.6 gather_fusion.2
  16.8 0.6 gather_fusion.1
  17.8 1.2 %fusion.24 = (f32[16,8,8]{0,2,1:T(8,128)S(1)}, f32[16,8,8,64]{3,0,2,1:T(8,128)S(1)}) fusion(bf16[3,3,32,64]{3,2,1,0:T(8,128)(2,1)S(1)} %copy-done.9, bf16[16,17,1,32]{3,0,2,1:T(8,128)(2,1)S(1)} %maximum_bitcast_fusion, bf16[16,1,16,32]{3,0,2,1:T(8,128)(2,1)S(1)} %copy.52, bf16[16,16,16,32]{3,0,2,1:T(8,128)(2,1)S(1)} %copy_select_fusion), kind=kOutput, calls=%fused_computation.108 | convolution fusion | flops 38109184 | bytes 599040 | tf_op jit(solution)/shard_map/conv_general_dilated | solution.py:104
  19.9 1.9 %collective-permute-start.1 = (bf16[16,512]{1,0:T(8,128)(2,1)S(1)}, bf16[16,512]{1,0:T(8,128)(2,1)S(1)}, u32[]{:S(2)}, u32[]{:S(2)}) collective-permute-start(bf16[16,512]{1,0:T(8,128)(2,1)S(1)} %reshape_squeeze.20), channel_id=1, source_target_pairs={{1,0},{2,1},{3,2},{4,3},{5,4},{6,5},{7,6},{8,7},{9,8},{10,9},{11,1... | collective-permute-start | bytes 49160 | tf_op jit(solution)/shard_map/ppermute | solution.py:18
  21.9 0.6 gather_fusion.3
  22.7 2.2 %collective-permute-done.1 = bf16[16,512]{1,0:T(8,128)(2,1)S(1)} collective-permute-done((bf16[16,512]{1,0:T(8,128)(2,1)S(1)}, bf16[16,512]{1,0:T(8,128)(2,1)S(1)}, u32[]{:S(2)}, u32[]{:S(2)}) %collective-permute-start.1) | collective-permute-done | bytes 16416 | tf_op jit(solution)/shard_map/ppermute | solution.py:18
  24.9 0.6 gather_fusion.5
  25.5 0.6 gather_fusion.4
  27.1 0.7 multiply_reduce_fusion.4
  29.0 1.9 %collective-permute-start.2 = (bf16[16,576]{1,0:T(8,128)(2,1)S(1)}, bf16[16,576]{1,0:T(8,128)(2,1)S(1)}, u32[]{:S(2)}, u32[]{:S(2)}) collective-permute-start(bf16[16,576]{1,0:T(8,128)(2,1)S(1)} %convert_element_type.52), channel_id=1, source_target_pairs={{0,1},{1,2},{2,3},{3,4},{4,5},{5,6},{6,7},{7,8},{8,9},{9,10},{10,1... | collective-permute-start | bytes 55304 | tf_op jit(solution)/shard_map/ppermute | solution.py:18
  31.0 0.7 gather_fusion.6
  32.1 0.6 gather_fusion.8
  32.7 0.7 gather_fusion.7
  33.4 0.8 select_select_fusion
  34.5 0.7 multiply_reduce_fusion
  35.3 1.3 %fusion = f32[3,3,32,64]{3,2,1,0:T(8,128)S(1)} fusion(bf16[16,17,1,32]{3,0,2,1:T(8,128)(2,1)S(1)} %maximum_bitcast_fusion, bf16[16,1,16,32]{3,0,2,1:T(8,128)(2,1)S(1)} %copy.52, bf16[16,16,16,32]{3,0,2,1:T(8,128)(2,1)S(1)} %copy_select_fusion, f32[16,8,8,64]{3,0,2,1:T(8,128)S(1)} %get-tuple-element.49, f32[16,8,8,64]{3,0,2,1:T(8,128)S(1)} %get-tuple-element.84, ...), kind=kOutput, calls=%fused_computation.19 | convolution fusion | flops 38568960 | bytes 910592 | tf_op jit(solution)/shard_map/conv_general_dilated | solution.py:115
  36.7 1.1 concatenate.45
  38.2 10.0 %all_to_all.25 = f32[8,64,109]{2,1,0:T(8,128)S(1)} all-to-all(f32[8,64,109]{2,1,0:T(8,128)S(1)} %copy.66), channel_id=1, replica_groups=mesh['dp'=8,'space_0'=8,'space_1'=4,'space_2'=2] {'space_1','space_2'}, dimensions={0} | all-to-all | bytes 446464 | tf_op jit(solution)/shard_map/all_to_all | solution.py:28
  48.3 29.1 %all_to_all.26 = f32[64,1,109]{2,1,0:T(1,128)S(1)} all-to-all(f32[64,1,109]{2,1,0:T(1,128)S(1)} %bitcast.91), channel_id=1, replica_groups=mesh['dp'=8,'space_0'=8,'space_1'=4,'space_2'=2] {'dp','space_0'}, dimensions={0} | all-to-all | bytes 55808 | tf_op jit(solution)/shard_map/all_to_all | solution.py:36
  77.5 14.7 %all_to_all.27 = f32[64,1,109]{2,1,0:T(1,128)S(1)} all-to-all(f32[64,1,109]{2,1,0:T(1,128)S(1)} %broadcast_in_dim.179), channel_id=1, replica_groups=mesh['dp'=8,'space_0'=8,'space_1'=4,'space_2'=2] {'dp','space_0'}, dimensions={0} | all-to-all | bytes 55808 | tf_op jit(solution)/shard_map/all_to_all | solution.py:49
  92.2 12.5 %all_to_all.28 = f32[8,64,109]{2,1,0:T(8,128)S(1)} all-to-all(f32[8,64,109]{2,1,0:T(8,128)S(1)} %broadcast_in_dim.181), channel_id=1, replica_groups=mesh['dp'=8,'space_0'=8,'space_1'=4,'space_2'=2] {'space_1','space_2'}, dimensions={0} | all-to-all | bytes 446464 | tf_op jit(solution)/shard_map/all_to_all | solution.py:49
  105.1 0.6 fusion.23
  105.7 0.7 reshape.277
  106.4 0.8 reshape.278
  (107 shorter events, 6.0 us)
Async XLA Ops:
  0.6 25.8 %copy-start = (bf16[3,3,64,64]{3,2,1,0:T(8,128)(2,1)S(1)}, bf16[3,3,64,64]{3,2,1,0:T(8,128)(2,1)}, u32[]{:S(2)}) copy-start(bf16[3,3,64,64]{3,2,1,0:T(8,128)(2,1)} %param.25) | copy-start | bytes 221188
  3.1 9.6 %copy-start.2 = (s32[1,16,8]{1,2,0:T(8,128)S(1)}, s32[1,16,8]{1,2,0:T(8,128)}, u32[]{:S(2)}) copy-start(s32[1,16,8]{1,2,0:T(8,128)} %param.23) | copy-start | bytes 1540
  3.1 11.4 %copy-start.1 = (bf16[1,16,4,256]{3,2,1,0:T(4,128)(2,1)S(1)}, bf16[1,16,4,256]{3,2,1,0:T(4,128)(2,1)}, u32[]{:S(2)}) copy-start(bf16[1,16,4,256]{3,2,1,0:T(4,128)(2,1)} %param.21) | copy-start | bytes 98308
  3.7 14.0 %copy-start.9 = (bf16[3,3,32,64]{3,2,1,0:T(8,128)(2,1)S(1)}, bf16[3,3,32,64]{3,2,1,0:T(8,128)(2,1)}, u32[]{:S(2)}) copy-start(bf16[3,3,32,64]{3,2,1,0:T(8,128)(2,1)} %param.24) | copy-start | bytes 110596
  3.9 12.3 %collective-permute-start = (bf16[16,512]{1,0:T(8,128)(2,1)S(1)}, bf16[16,512]{1,0:T(8,128)(2,1)S(1)}, u32[]{:S(2)}, u32[]{:S(2)}) collective-permute-start(bf16[16,512]{1,0:T(8,128)(2,1)S(1)} %reshape_squeeze.18), channel_id=1, source_target_pairs={{1,0},{2,1},{3,2},{4,3},{5,4},{6,5},{7,6},{8,7},{9,8},{10,9},{11,1... | collective-permute-start | bytes 49160 | tf_op jit(solution)/shard_map/ppermute | solution.py:18
  17.8 1.6 %copy-start.4 = (f32[64]{0:T(128)S(1)}, f32[64]{0:T(128)}, u32[]{:S(2)}) copy-start(f32[64]{0:T(128)} %param.26) | copy-start | bytes 772
  19.9 5.1 %collective-permute-start.1 = (bf16[16,512]{1,0:T(8,128)(2,1)S(1)}, bf16[16,512]{1,0:T(8,128)(2,1)S(1)}, u32[]{:S(2)}, u32[]{:S(2)}) collective-permute-start(bf16[16,512]{1,0:T(8,128)(2,1)S(1)} %reshape_squeeze.20), channel_id=1, source_target_pairs={{1,0},{2,1},{3,2},{4,3},{5,4},{6,5},{7,6},{8,7},{9,8},{10,9},{11,1... | collective-permute-start | bytes 49160 | tf_op jit(solution)/shard_map/ppermute | solution.py:18
  22.6 4.5 %copy-start.3 = (f32[64]{0:T(128)S(1)}, f32[64]{0:T(128)}, u32[]{:S(2)}) copy-start(f32[64]{0:T(128)} %param.27) | copy-start | bytes 772
  28.3 3.3 %copy-start.7 = (pred[16]{0:T(512)(128)(4,1)S(1)}, pred[16]{0:T(512)(128)(4,1)}, u32[]{:S(2)}) copy-start(pred[16]{0:T(512)(128)(4,1)} %get-tuple-element.69) | copy-start | bytes 52
  28.4 3.3 %copy-start.8 = (pred[16]{0:T(512)(128)(4,1)S(1)}, pred[16]{0:T(512)(128)(4,1)}, u32[]{:S(2)}) copy-start(pred[16]{0:T(512)(128)(4,1)} %get-tuple-element.79) | copy-start | bytes 52
  29.0 3.1 %collective-permute-start.2 = (bf16[16,576]{1,0:T(8,128)(2,1)S(1)}, bf16[16,576]{1,0:T(8,128)(2,1)S(1)}, u32[]{:S(2)}, u32[]{:S(2)}) collective-permute-start(bf16[16,576]{1,0:T(8,128)(2,1)S(1)} %convert_element_type.52), channel_id=1, source_target_pairs={{0,1},{1,2},{2,3},{3,4},{4,5},{5,6},{6,7},{7,8},{8,9},{9,10},{10,1... | collective-permute-start | bytes 55304 | tf_op jit(solution)/shard_map/ppermute | solution.py:18
  31.9 2.6 %copy-start.5 = (f32[64]{0:T(128)S(1)}, f32[64]{0:T(128)}, u32[]{:S(2)}) copy-start(f32[64]{0:T(128)} %param.26) | copy-start | bytes 772
  35.3 1.5 %copy-start.6 = (f32[64]{0:T(128)S(1)}, f32[64]{0:T(128)}, u32[]{:S(2)}) copy-start(f32[64]{0:T(128)} %get-tuple-element.46) | copy-start | bytes 772

commit v4 on v3

--- a/solution.py
+++ b/solution.py
@@ -92,6 +92,13 @@
     positions = jnp.clip(idents - offset, 0, source.shape[0] - 1)
     picked = jnp.take(source, positions, axis=0)
     return jnp.where((idents >= 0)[:, None], picked, jnp.zeros_like(picked))
+
+
+def select_many(source, requests):
+    idents = jnp.concatenate([wanted for wanted, _ in requests])
+    shifts = jnp.concatenate([jnp.full(wanted.shape, shift) for wanted, shift in requests])
+    picked = select_rows(source, idents, shifts)
+    return jnp.split(picked, len(requests))
 
 
 def assemble(field, south_rows, east_cols, corners):
@@ -148,12 +155,14 @@
     live = jnp.arange(slots) < live_count[0, 0]
     field = image[0].reshape(slots, tile, tile, chan_in)
     field = jnp.where(live[:, None, None, None], field, jnp.zeros_like(field))
-    south_image = select_rows(field[:, 0].reshape(slots, tile * chan_in), nearby[:, 6], offset)
+    image_rows = field[:, 0].reshape(slots, tile * chan_in)
     image_cols = field[:, :, 0, :].reshape(slots, tile * chan_in)
     following = from_behind(image_cols, SPACE, -1)
-    source = jnp.concatenate([image_cols, following], axis=0)
-    east_image = select_rows(source, nearby[:, 4], offset)
-    diag_image = select_rows(source, nearby[:, 7], offset)
+    source = jnp.concatenate([image_rows, image_cols, following], axis=0)
+    south_image, east_image, diag_image = select_many(
+        source,
+        ((nearby[:, 6], offset), (nearby[:, 4], offset - slots), (nearby[:, 7], offset - slots)),
+    )
     padded_one = assemble(
         field,
         south_image.reshape(slots, tile, chan_in),
@@ -163,12 +172,14 @@
     normed_one, inverse_one = norm_forward(conv_forward(padded_one, weight_one))
     hidden_one = normed_one * gain_one
     act_one = jax.nn.silu(hidden_one).astype(jnp.bfloat16)
-    south_act = select_rows(act_one[:, 0].reshape(slots, half * chan_mid), nearby[:, 6], offset)
+    act_rows = act_one[:, 0].reshape(slots, half * chan_mid)
     act_cols = act_one[:, :, 0, :].reshape(slots, half * chan_mid)
     act_following = from_behind(act_cols, SPACE, -1)
-    act_source = jnp.concatenate([act_cols, act_following], axis=0)
-    east_act = select_rows(act_source, nearby[:, 4], offset)
-    diag_act = select_rows(act_source, nearby[:, 7], offset)
+    act_source = jnp.concatenate([act_rows, act_cols, act_following], axis=0)
+    south_act, east_act, diag_act = select_many(
+        act_source,
+        ((nearby[:, 6], offset), (nearby[:, 4], offset - slots), (nearby[:, 7], offset - slots)),
+    )
     padded_two = assemble(
         act_one,
         south_act.reshape(slots, half, chan_mid),
@@ -188,15 +199,20 @@
     grad_padded = input_grad(grad_z_two, weight_two)
     bottom = grad_padded[:, half, :half, :].astype(jnp.bfloat16).reshape(slots, half * chan_mid)
     right = grad_padded[:, :, half, :].astype(jnp.bfloat16).reshape(slots, (half + 1) * chan_mid)
-    from_north = select_rows(bottom, nearby[:, 1], offset).reshape(slots, half, chan_mid)
     previous = from_behind(right, SPACE, 1)
-    rim_source = jnp.concatenate([previous, right], axis=0)
-    from_west = select_rows(rim_source, nearby[:, 3], offset - slots).reshape(
-        slots, half + 1, chan_mid
-    )
-    from_diag = select_rows(rim_source, nearby[:, 0], offset - slots).reshape(
-        slots, half + 1, chan_mid
-    )
+    bottom_wide = jnp.concatenate([bottom, jnp.zeros((slots, chan_mid), bottom.dtype)], axis=1)
+    rim_source = jnp.concatenate([previous, right, bottom_wide], axis=0)
+    from_west, from_diag, from_north = select_many(
+        rim_source,
+        (
+            (nearby[:, 3], offset - slots),
+            (nearby[:, 0], offset - slots),
+            (nearby[:, 1], offset - 2 * slots),
+        ),
+    )
+    from_west = from_west.reshape(slots, half + 1, chan_mid)
+    from_diag = from_diag.reshape(slots, half + 1, chan_mid)
+    from_north = from_north[:, : half * chan_mid].reshape(slots, half, chan_mid)
     grad_act = grad_padded[:, :half, :half, :]
     grad_act = grad_act.at[:, 0].add(from_north.astype(jnp.float32))
     grad_act = grad_act.at[:, :, 0].add(from_west[:, :half].astype(jnp.float32))

time: 108 us -> 105 us (0.972)
  local copies, waits for them, and re-layouts: 13.4 us -> 9.88 us
  other arithmetic: 7.22 us -> 5.16 us
  blocking collectives: 66.2 us -> 67.9 us
    gather x9 -> x3, local copies, waits for them, and re-layouts: 5.56 us -> 2 us  [select_rows(): picked = jnp.take(source, positions, axis=0)]
    gather x6 -> x2, other arithmetic: 1.22 us -> 0.01 us  [the longest x1 0.01 us: select_rows(): picked = jnp.take(source, positions, axis=0)]
    all_to_all x1, blocking collectives: 29.1 us -> 30.3 us  [summed_rows(): lax.all_to_all(nearer, far, split_axis=0, concat_axis=0, tiled=True)]
  transfers between devices with their start and end apart: 3 -> 3, of which waited for: 2 -> 1; matrix products, arithmetic and copies ran while one was open for 5% -> 3% of each run, Pallas kernels for 0% -> 0%
where the time goes in v4:
time: 105 us
  blocking collectives  67.9 us (65%)
  starting transfers between devices  12.6 us (12%)
  local copies, waits for them, and re-layouts  9.88 us (9%)
  other arithmetic  5.16 us (5%)
  matrix products  4.33 us (4%)
  waiting for transfers between devices  2.86 us (3%)
  between operations  2.05 us (2%)
    all_to_all x1, blocking collectives, summed_rows(): lax.all_to_all(nearer, far, split_axis=0, concat_axis=0, tiled=True)  30.3 us
    all_to_all x2, blocking collectives, from_everyone(): lax.all_to_all(jnp.broadcast_to(value[None], (peers, *value.shape)), axis...  27.2 us
    ppermute x3, starting transfers between devices, from_behind(): lax.ppermute(value, axis, [(source, source + steps) for source in range(f...  12.6 us
    all_to_all x1, blocking collectives, sent_and_summed(): lax.all_to_all(cut_along(value, dim, peers), axis, 0, 0, tiled=True)  10.5 us
    ppermute x3, waiting for transfers between devices, from_behind(): lax.ppermute(value, axis, [(source, source + steps) for source in range(f...  2.86 us
    conv_general_dilated x2, matrix products, weight_grad(): lax.conv_general_dilated(padded, grad_z, (1, 1), 'VALID', rhs_dilation=(2...  2.41 us
  transfers between devices with their start and end apart: 3, of which 1 were waited for; matrix products, arithmetic and copies ran while one was open for 3% of the time, Pallas kernels for 0%

profile of v4, /device:TPU:1, one launch (start us, length us, event | category | flops | bytes accessed | tf_op | source)
XLA Modules:
  0.0 104.8 jit_solution(8717588666562049384)
XLA Ops:
  1.3 1.7 %reshape_squeeze.16 = bf16[16,16,16,32]{3,2,1,0:T(8,128)(2,1)S(1)} reshape(bf16[1,16,16,512]{3,2,1,0:T(8,128)(2,1)} %param.16) | data formatting | bytes 524288 | tf_op jit(solution)/shard_map/reshape;squeeze | solution.py:156
  3.1 0.6 copy_select_fusion
  3.9 8.7 %collective-permute-start = (bf16[16,512]{1,0:T(8,128)(2,1)S(1)}, bf16[16,512]{1,0:T(8,128)(2,1)S(1)}, u32[]{:S(2)}, u32[]{:S(2)}) collective-permute-start(bf16[16,512]{1,0:T(8,128)(2,1)S(1)} %reshape_squeeze.18), channel_id=1, source_target_pairs={{1,0},{2,1},{3,2},{4,3},{5,4},{6,5},{7,6},{8,7},{9,8},{10,9},{11,1... | collective-permute-start | bytes 49160 | tf_op jit(solution)/shard_map/ppermute | solution.py:18
  12.7 0.6 broadcast_compare_fusion
  13.4 0.6 compare_and_fusion
  14.3 0.7 gather_fusion.1
  15.4 1.2 %fusion.32 = (f32[16,8,8]{0,2,1:T(8,128)S(1)}, f32[16,8,8,64]{3,0,2,1:T(8,128)S(1)}) fusion(bf16[3,3,32,64]{3,2,1,0:T(8,128)(2,1)S(1)} %copy-done.12, bf16[16,17,1,32]{3,0,2,1:T(8,128)(2,1)S(1)} %maximum_bitcast_fusion, bf16[16,1,16,32]{3,0,2,1:T(8,128)(2,1)S(1)} %copy.52, bf16[16,16,16,32]{3,0,2,1:T(8,128)(2,1)S(1)} %copy_select_fusion), kind=kOutput, calls=%fused_computation.101 | convolution fusion | flops 38109184 | bytes 599040 | tf_op jit(solution)/shard_map/conv_general_dilated | solution.py:111
  16.6 0.4 multiply_reduce_fusion.2
  17.0 0.4 multiply_convert_fusion.1
  17.5 1.9 %collective-permute-start.1 = (bf16[16,512]{1,0:T(8,128)(2,1)S(1)}, bf16[16,512]{1,0:T(8,128)(2,1)S(1)}, u32[]{:S(2)}, u32[]{:S(2)}) collective-permute-start(bf16[16,512]{1,0:T(8,128)(2,1)S(1)} %reshape_squeeze.20), channel_id=1, source_target_pairs={{1,0},{2,1},{3,2},{4,3},{5,4},{6,5},{7,6},{8,7},{9,8},{10,9},{11,1... | collective-permute-start | bytes 49160 | tf_op jit(solution)/shard_map/ppermute | solution.py:18
  19.7 2.9 %collective-permute-done.1 = bf16[16,512]{1,0:T(8,128)(2,1)S(1)} collective-permute-done((bf16[16,512]{1,0:T(8,128)(2,1)S(1)}, bf16[16,512]{1,0:T(8,128)(2,1)S(1)}, u32[]{:S(2)}, u32[]{:S(2)}) %collective-permute-start.1) | collective-permute-done | bytes 16416 | tf_op jit(solution)/shard_map/ppermute | solution.py:18
  22.5 0.7 gather_fusion.2
  23.6 0.4 fusion.33
  24.0 0.2 multiply_reduce_fusion.6
  24.2 0.8 multiply_reduce_fusion.4
  25.0 0.2 multiply_convert_fusion.3
  25.2 0.4 fusion.34
  25.8 1.9 %collective-permute-start.2 = (bf16[16,576]{1,0:T(8,128)(2,1)S(1)}, bf16[16,576]{1,0:T(8,128)(2,1)S(1)}, u32[]{:S(2)}, u32[]{:S(2)}) collective-permute-start(bf16[16,576]{1,0:T(8,128)(2,1)S(1)} %convert_element_type.49), channel_id=1, source_target_pairs={{0,1},{1,2},{2,3},{3,4},{4,5},{5,6},{6,7},{7,8},{8,9},{9,10},{10,1... | collective-permute-start | bytes 55304 | tf_op jit(solution)/shard_map/ppermute | solution.py:18
  27.7 1.1 %fusion.7 = f32[3,3,64,64]{3,2,1,0:T(8,128)S(1)} fusion(bf16[16,4,4,64]{3,0,2,1:T(8,128)(2,1)S(1)} %multiply_convert_fusion.3, bf16[16,9,1,64]{3,0,2,1:T(8,128)(2,1)S(1)} %maximum_bitcast_fusion.1, bf16[16,1,8,64]{3,0,2,1:T(8,128)(2,1)} %copy-done.4, bf16[16,8,8,64]{3,0,2,1:T(8,128)(2,1)S(1)} %multiply_convert_fusion.1), kind=kOutput, calls=%fused_computation.22 | convolution fusion | flops 19040256 | bytes 346112 | tf_op jit(solution)/shard_map/conv_general_dilated | solution.py:122
  29.1 0.7 gather_fusion
  30.3 0.7 multiply_reduce_fusion
  31.1 1.3 %fusion = f32[3,3,32,64]{3,2,1,0:T(8,128)S(1)} fusion(bf16[16,17,1,32]{3,0,2,1:T(8,128)(2,1)S(1)} %maximum_bitcast_fusion, bf16[16,1,16,32]{3,0,2,1:T(8,128)(2,1)S(1)} %copy-done.2, bf16[16,16,16,32]{3,0,2,1:T(8,128)(2,1)S(1)} %copy_select_fusion, f32[16,8,8,64]{3,0,2,1:T(8,128)S(1)} %get-tuple-element.47, f32[16,8,8,64]{3,0,2,1:T(8,128)S(1)} %get-tuple-element.76, ...), kind=kOutput, calls=%fused_computation.13 | convolution fusion | flops 38568960 | bytes 910592 | tf_op jit(solution)/shard_map/conv_general_dilated | solution.py:122
  32.6 1.1 %concatenate.117 = f32[55808]{0:T(1024)S(1)} concatenate(f32[18432]{0:T(1024)S(1)} %reshape.370, f32[36864]{0:T(1024)S(1)} %reshape.371, f32[64]{0:T(128)S(1)} %get-tuple-element.41, f32[64]{0:T(128)S(1)} %copy-done.9, f32[384]{0:T(512)S(1)} %broadcast_in_dim.147), dimensions={0} | concatenate | bytes 446464 | tf_op jit(solution)/shard_map/concatenate | solution.py:44
  33.6 0.4 reshape_reshape.6
  34.1 10.5 %all_to_all.25 = f32[8,64,109]{2,1,0:T(8,128)S(1)} all-to-all(f32[8,64,109]{2,1,0:T(8,128)S(1)} %copy.65), channel_id=1, replica_groups=mesh['dp'=8,'space_0'=8,'space_1'=4,'space_2'=2] {'space_1','space_2'}, dimensions={0} | all-to-all | bytes 446464 | tf_op jit(solution)/shard_map/all_to_all | solution.py:28
  44.6 30.3 %all_to_all.26 = f32[64,1,109]{2,1,0:T(1,128)S(1)} all-to-all(f32[64,1,109]{2,1,0:T(1,128)S(1)} %bitcast.83), channel_id=1, replica_groups=mesh['dp'=8,'space_0'=8,'space_1'=4,'space_2'=2] {'dp','space_0'}, dimensions={0} | all-to-all | bytes 55808 | tf_op jit(solution)/shard_map/all_to_all | solution.py:36
  75.0 14.7 %all_to_all.27 = f32[64,1,109]{2,1,0:T(1,128)S(1)} all-to-all(f32[64,1,109]{2,1,0:T(1,128)S(1)} %broadcast_in_dim.148), channel_id=1, replica_groups=mesh['dp'=8,'space_0'=8,'space_1'=4,'space_2'=2] {'dp','space_0'}, dimensions={0} | all-to-all | bytes 55808 | tf_op jit(solution)/shard_map/all_to_all | solution.py:49
  89.7 12.5 %all_to_all.28 = f32[8,64,109]{2,1,0:T(8,128)S(1)} all-to-all(f32[8,64,109]{2,1,0:T(8,128)S(1)} %broadcast_in_dim.150), channel_id=1, replica_groups=mesh['dp'=8,'space_0'=8,'space_1'=4,'space_2'=2] {'space_1','space_2'}, dimensions={0} | all-to-all | bytes 446464 | tf_op jit(solution)/shard_map/all_to_all | solution.py:49
  102.4 0.3 reshape_reshape.7
  102.6 0.6 fusion.28
  103.2 0.7 reshape.372
  104.0 0.8 reshape.373
  (107 shorter events, 3.0 us)
Async XLA Ops:
  0.6 23.0 %copy-start = (bf16[3,3,64,64]{3,2,1,0:T(8,128)(2,1)S(1)}, bf16[3,3,64,64]{3,2,1,0:T(8,128)(2,1)}, u32[]{:S(2)}) copy-start(bf16[3,3,64,64]{3,2,1,0:T(8,128)(2,1)} %param.21) | copy-start | bytes 221188
  3.1 9.6 %copy-start.5 = (s32[1,16,8]{1,2,0:T(8,128)S(1)}, s32[1,16,8]{1,2,0:T(8,128)}, u32[]{:S(2)}) copy-start(s32[1,16,8]{1,2,0:T(8,128)} %param.19) | copy-start | bytes 1540
  3.1 10.9 %copy-start.3 = (bf16[1,16,4,256]{3,2,1,0:T(4,128)(2,1)S(1)}, bf16[1,16,4,256]{3,2,1,0:T(4,128)(2,1)}, u32[]{:S(2)}) copy-start(bf16[1,16,4,256]{3,2,1,0:T(4,128)(2,1)} %param.17) | copy-start | bytes 98308
  3.7 11.6 %copy-start.12 = (bf16[3,3,32,64]{3,2,1,0:T(8,128)(2,1)S(1)}, bf16[3,3,32,64]{3,2,1,0:T(8,128)(2,1)}, u32[]{:S(2)}) copy-start(bf16[3,3,32,64]{3,2,1,0:T(8,128)(2,1)} %param.20) | copy-start | bytes 110596
  3.9 10.4 %collective-permute-start = (bf16[16,512]{1,0:T(8,128)(2,1)S(1)}, bf16[16,512]{1,0:T(8,128)(2,1)S(1)}, u32[]{:S(2)}, u32[]{:S(2)}) collective-permute-start(bf16[16,512]{1,0:T(8,128)(2,1)S(1)} %reshape_squeeze.18), channel_id=1, source_target_pairs={{1,0},{2,1},{3,2},{4,3},{5,4},{6,5},{7,6},{8,7},{9,8},{10,9},{11,1... | collective-permute-start | bytes 49160 | tf_op jit(solution)/shard_map/ppermute | solution.py:18
  15.2 1.4 %copy-start.1 = (bf16[16,1,16,32]{3,0,2,1:T(8,128)(2,1)}, bf16[16,1,16,32]{3,0,2,1:T(8,128)(2,1)S(1)}, u32[]{:S(2)}) copy-start(bf16[16,1,16,32]{3,0,2,1:T(8,128)(2,1)S(1)} %copy.52) | copy-start | bytes 49156
  15.4 1.6 %copy-start.7 = (f32[64]{0:T(128)S(1)}, f32[64]{0:T(128)}, u32[]{:S(2)}) copy-start(f32[64]{0:T(128)} %param.22) | copy-start | bytes 772
  17.5 5.1 %collective-permute-start.1 = (bf16[16,512]{1,0:T(8,128)(2,1)S(1)}, bf16[16,512]{1,0:T(8,128)(2,1)S(1)}, u32[]{:S(2)}, u32[]{:S(2)}) collective-permute-start(bf16[16,512]{1,0:T(8,128)(2,1)S(1)} %reshape_squeeze.20), channel_id=1, source_target_pairs={{1,0},{2,1},{3,2},{4,3},{5,4},{6,5},{7,6},{8,7},{9,8},{10,9},{11,1... | collective-permute-start | bytes 49160 | tf_op jit(solution)/shard_map/ppermute | solution.py:18
  23.2 1.0 copy-start.6
  23.4 1.6 %copy-start.4 = (bf16[16,1,8,64]{3,0,2,1:T(8,128)(2,1)}, bf16[16,1,8,64]{3,0,2,1:T(8,128)(2,1)S(1)}, u32[]{:S(2)}) copy-start(bf16[16,1,8,64]{3,0,2,1:T(8,128)(2,1)S(1)} %copy.56) | copy-start | bytes 49156
  25.8 3.4 %collective-permute-start.2 = (bf16[16,576]{1,0:T(8,128)(2,1)S(1)}, bf16[16,576]{1,0:T(8,128)(2,1)S(1)}, u32[]{:S(2)}, u32[]{:S(2)}) collective-permute-start(bf16[16,576]{1,0:T(8,128)(2,1)S(1)} %convert_element_type.49), channel_id=1, source_target_pairs={{0,1},{1,2},{2,3},{3,4},{4,5},{5,6},{6,7},{7,8},{8,9},{9,10},{10,1... | collective-permute-start | bytes 55304 | tf_op jit(solution)/shard_map/ppermute | solution.py:18
  28.8 1.0 copy-start.10
  28.8 1.0 copy-start.11
  29.1 1.2 %copy-start.8 = (f32[64]{0:T(128)S(1)}, f32[64]{0:T(128)}, u32[]{:S(2)}) copy-start(f32[64]{0:T(128)} %param.22) | copy-start | bytes 772
  30.3 0.8 copy-start.2
  31.1 1.4 %copy-start.9 = (f32[64]{0:T(128)S(1)}, f32[64]{0:T(128)}, u32[]{:S(2)}) copy-start(f32[64]{0:T(128)} %get-tuple-element.44) | copy-start | bytes 772

commit v5 on v4

--- a/solution.py
+++ b/solution.py
@@ -69,6 +69,14 @@
     own = summed_rows(rows_for(lines, lax.axis_size(axes[0]) * lax.axis_size(axes[1])), axes, 0)
     whole = gathered_by_axis(own, axes, 0)
     return whole[: len(lines)].reshape(value.shape)
+
+
+def summed_everywhere(value, far, near):
+    lines = rows_for(value, lax.axis_size(far) * lax.axis_size(near))
+    far_peers = lax.axis_size(far)
+    mine = lax.all_to_all(lines.reshape(far_peers, -1), far, 0, 0, tiled=True).sum(axis=0)
+    mine = from_everyone(mine, near).sum(axis=0)
+    return from_everyone(mine, far).reshape(-1)[: value.shape[0]]
 
 
 def norm_forward(values):
@@ -223,7 +231,7 @@
     grad_weight_one = weight_grad(padded_one, grad_z_one.astype(jnp.bfloat16))
     parts = (grad_weight_one, grad_weight_two, grad_gain_one, grad_gain_two)
     flat = jnp.concatenate([part.reshape(-1) for part in parts])
-    flat = total_of(flat, (("dp", "space_0"), ("space_1", "space_2")))
+    flat = summed_everywhere(flat, ("dp", "space_0"), ("space_1", "space_2"))
     sizes = [part.size for part in parts]
     bounds = [sum(sizes[:index]) for index in range(len(sizes) + 1)]
     grad_weight_one, grad_weight_two, grad_gain_one, grad_gain_two = (

time: 105 us -> 96.4 us (0.918)
  blocking collectives: 67.9 us -> 58.1 us
    all_to_all x2 -> x1, blocking collectives: 40.8 us -> 27.4 us  [summed_everywhere(): lax.all_to_all(lines.reshape(far_peers, -1), far, 0, 0, tiled=True)]
    all_to_all x2, blocking collectives: 27.2 us -> 30.7 us  [from_everyone(): lax.all_to_all(jnp.broadcast_to(value[None], (peers, *value.shape)), axis...]
where the time goes in v5:
time: 96.4 us; the launch traced here: 95.4 us
  blocking collectives  58.1 us (60%)
  starting transfers between devices  12.6 us (13%)
  local copies, waits for them, and re-layouts  9.63 us (10%)
  other arithmetic  5.8 us (6%)
  matrix products  4.33 us (4%)
  waiting for transfers between devices  2.86 us (3%)
  between operations  2.05 us (2%)
    all_to_all x2, blocking collectives, from_everyone(): lax.all_to_all(jnp.broadcast_to(value[None], (peers, *value.shape)), axis...  30.7 us
    all_to_all x1, blocking collectives, summed_everywhere(): lax.all_to_all(lines.reshape(far_peers, -1), far, 0, 0, tiled=True)  27.4 us
    ppermute x3, starting transfers between devices, from_behind(): lax.ppermute(value, axis, [(source, source + steps) for source in range(f...  12.6 us
    ppermute x3, waiting for transfers between devices, from_behind(): lax.ppermute(value, axis, [(source, source + steps) for source in range(f...  2.86 us
    conv_general_dilated x2, matrix products, weight_grad(): lax.conv_general_dilated(padded, grad_z, (1, 1), 'VALID', rhs_dilation=(2...  2.41 us
    gather x3, local copies, waits for them, and re-layouts, select_rows(): picked = jnp.take(source, positions, axis=0)  2 us
  transfers between devices with their start and end apart: 3, of which 1 were waited for; matrix products, arithmetic and copies ran while one was open for 3% of the time, Pallas kernels for 0%

profile of v5, /device:TPU:1, one launch (start us, length us, event | category | flops | bytes accessed | tf_op | source)
XLA Modules:
  0.0 95.4 jit_solution(3570007010067284383)
XLA Ops:
  1.3 1.7 %reshape_squeeze.16 = bf16[16,16,16,32]{3,2,1,0:T(8,128)(2,1)S(1)} reshape(bf16[1,16,16,512]{3,2,1,0:T(8,128)(2,1)} %param.16) | data formatting | bytes 524288 | tf_op jit(solution)/shard_map/reshape;squeeze | solution.py:164
  3.1 0.6 copy_select_fusion
  3.9 8.7 %collective-permute-start = (bf16[16,512]{1,0:T(8,128)(2,1)S(1)}, bf16[16,512]{1,0:T(8,128)(2,1)S(1)}, u32[]{:S(2)}, u32[]{:S(2)}) collective-permute-start(bf16[16,512]{1,0:T(8,128)(2,1)S(1)} %reshape_squeeze.18), channel_id=1, source_target_pairs={{1,0},{2,1},{3,2},{4,3},{5,4},{6,5},{7,6},{8,7},{9,8},{10,9},{11,1... | collective-permute-start | bytes 49160 | tf_op jit(solution)/shard_map/ppermute | solution.py:18
  12.7 0.6 broadcast_compare_fusion
  13.4 0.6 compare_and_fusion
  14.3 0.7 gather_fusion.1
  15.4 1.2 %fusion.32 = (f32[16,8,8]{0,2,1:T(8,128)S(1)}, f32[16,8,8,64]{3,0,2,1:T(8,128)S(1)}) fusion(bf16[3,3,32,64]{3,2,1,0:T(8,128)(2,1)S(1)} %copy-done.12, bf16[16,17,1,32]{3,0,2,1:T(8,128)(2,1)S(1)} %maximum_bitcast_fusion, bf16[16,1,16,32]{3,0,2,1:T(8,128)(2,1)S(1)} %copy.51, bf16[16,16,16,32]{3,0,2,1:T(8,128)(2,1)S(1)} %copy_select_fusion), kind=kOutput, calls=%fused_computation.101 | convolution fusion | flops 38109184 | bytes 599040 | tf_op jit(solution)/shard_map/conv_general_dilated | solution.py:119
  16.6 0.4 multiply_reduce_fusion.2
  17.0 0.4 multiply_convert_fusion.1
  17.5 1.9 %collective-permute-start.1 = (bf16[16,512]{1,0:T(8,128)(2,1)S(1)}, bf16[16,512]{1,0:T(8,128)(2,1)S(1)}, u32[]{:S(2)}, u32[]{:S(2)}) collective-permute-start(bf16[16,512]{1,0:T(8,128)(2,1)S(1)} %reshape_squeeze.20), channel_id=1, source_target_pairs={{1,0},{2,1},{3,2},{4,3},{5,4},{6,5},{7,6},{8,7},{9,8},{10,9},{11,1... | collective-permute-start | bytes 49160 | tf_op jit(solution)/shard_map/ppermute | solution.py:18
  19.7 2.9 %collective-permute-done.1 = bf16[16,512]{1,0:T(8,128)(2,1)S(1)} collective-permute-done((bf16[16,512]{1,0:T(8,128)(2,1)S(1)}, bf16[16,512]{1,0:T(8,128)(2,1)S(1)}, u32[]{:S(2)}, u32[]{:S(2)}) %collective-permute-start.1) | collective-permute-done | bytes 16416 | tf_op jit(solution)/shard_map/ppermute | solution.py:18
  22.5 0.7 gather_fusion.2
  23.6 0.4 fusion.33
  24.0 0.2 multiply_reduce_fusion.6
  24.2 0.8 multiply_reduce_fusion.4
  25.0 0.2 multiply_convert_fusion.3
  25.2 0.4 fusion.34
  25.8 1.9 %collective-permute-start.2 = (bf16[16,576]{1,0:T(8,128)(2,1)S(1)}, bf16[16,576]{1,0:T(8,128)(2,1)S(1)}, u32[]{:S(2)}, u32[]{:S(2)}) collective-permute-start(bf16[16,576]{1,0:T(8,128)(2,1)S(1)} %convert_element_type.49), channel_id=1, source_target_pairs={{0,1},{1,2},{2,3},{3,4},{4,5},{5,6},{6,7},{7,8},{8,9},{9,10},{10,1... | collective-permute-start | bytes 55304 | tf_op jit(solution)/shard_map/ppermute | solution.py:18
  27.7 1.1 %fusion.7 = f32[3,3,64,64]{3,2,1,0:T(8,128)S(1)} fusion(bf16[16,4,4,64]{3,0,2,1:T(8,128)(2,1)S(1)} %multiply_convert_fusion.3, bf16[16,9,1,64]{3,0,2,1:T(8,128)(2,1)S(1)} %maximum_bitcast_fusion.1, bf16[16,1,8,64]{3,0,2,1:T(8,128)(2,1)} %copy-done.4, bf16[16,8,8,64]{3,0,2,1:T(8,128)(2,1)S(1)} %multiply_convert_fusion.1), kind=kOutput, calls=%fused_computation.22 | convolution fusion | flops 19040256 | bytes 346112 | tf_op jit(solution)/shard_map/conv_general_dilated | solution.py:130
  29.1 0.7 gather_fusion
  30.3 0.7 multiply_reduce_fusion
  31.1 1.3 %fusion = f32[3,3,32,64]{3,2,1,0:T(8,128)S(1)} fusion(bf16[16,17,1,32]{3,0,2,1:T(8,128)(2,1)S(1)} %maximum_bitcast_fusion, bf16[16,1,16,32]{3,0,2,1:T(8,128)(2,1)S(1)} %copy-done.2, bf16[16,16,16,32]{3,0,2,1:T(8,128)(2,1)S(1)} %copy_select_fusion, f32[16,8,8,64]{3,0,2,1:T(8,128)S(1)} %get-tuple-element.47, f32[16,8,8,64]{3,0,2,1:T(8,128)S(1)} %get-tuple-element.76, ...), kind=kOutput, calls=%fused_computation.13 | convolution fusion | flops 38568960 | bytes 910592 | tf_op jit(solution)/shard_map/conv_general_dilated | solution.py:130
  32.6 1.1 %concatenate.117 = f32[55808]{0:T(1024)S(1)} concatenate(f32[18432]{0:T(1024)S(1)} %reshape.380, f32[36864]{0:T(1024)S(1)} %reshape.381, f32[64]{0:T(128)S(1)} %get-tuple-element.41, f32[64]{0:T(128)S(1)} %copy-done.9, f32[384]{0:T(512)S(1)} %broadcast_in_dim.145), dimensions={0} | concatenate | bytes 446464 | tf_op jit(solution)/shard_map/concatenate | solution.py:44
  33.6 0.4 all_to_all.14
  34.0 27.4 %all_to_all.21 = f32[64,1,872]{2,1,0:T(1,128)S(1)} all-to-all(f32[64,1,872]{2,1,0:T(1,128)S(1)} %all_to_all.14), channel_id=1, replica_groups=mesh['dp'=8,'space_0'=8,'space_1'=4,'space_2'=2] {'dp','space_0'}, dimensions={0} | all-to-all | bytes 446464 | tf_op jit(solution)/shard_map/all_to_all | solution.py:77
  61.4 0.2 reduce_sum.118
  61.6 14.3 %all_to_all.22 = f32[8,1,872]{2,1,0:T(1,128)S(1)} all-to-all(f32[8,1,872]{2,1,0:T(1,128)S(1)} %broadcast_in_dim.146), channel_id=1, replica_groups=mesh['dp'=8,'space_0'=8,'space_1'=4,'space_2'=2] {'space_1','space_2'}, dimensions={0} | all-to-all | bytes 55808 | tf_op jit(solution)/shard_map/all_to_all | solution.py:49
  76.1 16.4 %all_to_all.23 = f32[64,1,872]{2,1,0:T(1,128)S(1)} all-to-all(f32[64,1,872]{2,1,0:T(1,128)S(1)} %broadcast_in_dim.147), channel_id=1, replica_groups=mesh['dp'=8,'space_0'=8,'space_1'=4,'space_2'=2] {'dp','space_0'}, dimensions={0} | all-to-all | bytes 446464 | tf_op jit(solution)/shard_map/all_to_all | solution.py:49
  92.5 0.5 reduce.8
  93.2 0.6 fusion.28
  93.8 0.7 reshape.383
  94.6 0.8 reshape.384
  (105 shorter events, 3.0 us)
Async XLA Ops:
  0.6 23.0 %copy-start = (bf16[3,3,64,64]{3,2,1,0:T(8,128)(2,1)S(1)}, bf16[3,3,64,64]{3,2,1,0:T(8,128)(2,1)}, u32[]{:S(2)}) copy-start(bf16[3,3,64,64]{3,2,1,0:T(8,128)(2,1)} %param.21) | copy-start | bytes 221188
  3.1 9.6 %copy-start.5 = (s32[1,16,8]{1,2,0:T(8,128)S(1)}, s32[1,16,8]{1,2,0:T(8,128)}, u32[]{:S(2)}) copy-start(s32[1,16,8]{1,2,0:T(8,128)} %param.19) | copy-start | bytes 1540
  3.1 10.9 %copy-start.3 = (bf16[1,16,4,256]{3,2,1,0:T(4,128)(2,1)S(1)}, bf16[1,16,4,256]{3,2,1,0:T(4,128)(2,1)}, u32[]{:S(2)}) copy-start(bf16[1,16,4,256]{3,2,1,0:T(4,128)(2,1)} %param.17) | copy-start | bytes 98308
  3.7 11.6 %copy-start.12 = (bf16[3,3,32,64]{3,2,1,0:T(8,128)(2,1)S(1)}, bf16[3,3,32,64]{3,2,1,0:T(8,128)(2,1)}, u32[]{:S(2)}) copy-start(bf16[3,3,32,64]{3,2,1,0:T(8,128)(2,1)} %param.20) | copy-start | bytes 110596
  3.9 10.4 %collective-permute-start = (bf16[16,512]{1,0:T(8,128)(2,1)S(1)}, bf16[16,512]{1,0:T(8,128)(2,1)S(1)}, u32[]{:S(2)}, u32[]{:S(2)}) collective-permute-start(bf16[16,512]{1,0:T(8,128)(2,1)S(1)} %reshape_squeeze.18), channel_id=1, source_target_pairs={{1,0},{2,1},{3,2},{4,3},{5,4},{6,5},{7,6},{8,7},{9,8},{10,9},{11,1... | collective-permute-start | bytes 49160 | tf_op jit(solution)/shard_map/ppermute | solution.py:18
  15.2 1.4 %copy-start.1 = (bf16[16,1,16,32]{3,0,2,1:T(8,128)(2,1)}, bf16[16,1,16,32]{3,0,2,1:T(8,128)(2,1)S(1)}, u32[]{:S(2)}) copy-start(bf16[16,1,16,32]{3,0,2,1:T(8,128)(2,1)S(1)} %copy.51) | copy-start | bytes 49156
  15.4 1.6 %copy-start.7 = (f32[64]{0:T(128)S(1)}, f32[64]{0:T(128)}, u32[]{:S(2)}) copy-start(f32[64]{0:T(128)} %param.22) | copy-start | bytes 772
  17.5 5.1 %collective-permute-start.1 = (bf16[16,512]{1,0:T(8,128)(2,1)S(1)}, bf16[16,512]{1,0:T(8,128)(2,1)S(1)}, u32[]{:S(2)}, u32[]{:S(2)}) collective-permute-start(bf16[16,512]{1,0:T(8,128)(2,1)S(1)} %reshape_squeeze.20), channel_id=1, source_target_pairs={{1,0},{2,1},{3,2},{4,3},{5,4},{6,5},{7,6},{8,7},{9,8},{10,9},{11,1... | collective-permute-start | bytes 49160 | tf_op jit(solution)/shard_map/ppermute | solution.py:18
  23.2 1.0 %copy-start.6 = (f32[64]{0:T(128)S(1)}, f32[64]{0:T(128)}, u32[]{:S(2)}) copy-start(f32[64]{0:T(128)} %param.23) | copy-start | bytes 772
  23.4 1.6 %copy-start.4 = (bf16[16,1,8,64]{3,0,2,1:T(8,128)(2,1)}, bf16[16,1,8,64]{3,0,2,1:T(8,128)(2,1)S(1)}, u32[]{:S(2)}) copy-start(bf16[16,1,8,64]{3,0,2,1:T(8,128)(2,1)S(1)} %copy.55) | copy-start | bytes 49156
  25.8 3.4 %collective-permute-start.2 = (bf16[16,576]{1,0:T(8,128)(2,1)S(1)}, bf16[16,576]{1,0:T(8,128)(2,1)S(1)}, u32[]{:S(2)}, u32[]{:S(2)}) collective-permute-start(bf16[16,576]{1,0:T(8,128)(2,1)S(1)} %convert_element_type.49), channel_id=1, source_target_pairs={{0,1},{1,2},{2,3},{3,4},{4,5},{5,6},{6,7},{7,8},{8,9},{9,10},{10,1... | collective-permute-start | bytes 55304 | tf_op jit(solution)/shard_map/ppermute | solution.py:18
  28.8 1.0 %copy-start.10 = (pred[48]{0:T(512)(128)(4,1)S(1)}, pred[48]{0:T(512)(128)(4,1)}, u32[]{:S(2)}) copy-start(pred[48]{0:T(512)(128)(4,1)} %get-tuple-element.50) | copy-start | bytes 148
  28.8 1.0 %copy-start.11 = (pred[48]{0:T(512)(128)(4,1)S(1)}, pred[48]{0:T(512)(128)(4,1)}, u32[]{:S(2)}) copy-start(pred[48]{0:T(512)(128)(4,1)} %get-tuple-element.74) | copy-start | bytes 148
  29.1 1.2 %copy-start.8 = (f32[64]{0:T(128)S(1)}, f32[64]{0:T(128)}, u32[]{:S(2)}) copy-start(f32[64]{0:T(128)} %param.22) | copy-start | bytes 772
  30.3 0.8 copy-start.2
  31.1 1.4 %copy-start.9 = (f32[64]{0:T(128)S(1)}, f32[64]{0:T(128)}, u32[]{:S(2)}) copy-start(f32[64]{0:T(128)} %get-tuple-element.44) | copy-start | bytes 772

commit v6 on v5

--- a/solution.py
+++ b/solution.py
@@ -72,11 +72,13 @@
 
 
 def summed_everywhere(value, far, near):
-    lines = rows_for(value, lax.axis_size(far) * lax.axis_size(near))
+    lines = rows_for(value, lax.axis_size(far))
     far_peers = lax.axis_size(far)
-    mine = lax.all_to_all(lines.reshape(far_peers, -1), far, 0, 0, tiled=True).sum(axis=0)
+    pieces = lines.reshape(far_peers, -1, *lines.shape[1:])
+    mine = lax.all_to_all(pieces, far, 0, 0, tiled=True).sum(axis=0)
     mine = from_everyone(mine, near).sum(axis=0)
-    return from_everyone(mine, far).reshape(-1)[: value.shape[0]]
+    whole = from_everyone(mine, far)
+    return whole.reshape(-1, *value.shape[1:])[: value.shape[0]]
 
 
 def norm_forward(values):
@@ -230,12 +232,12 @@
     )
     grad_weight_one = weight_grad(padded_one, grad_z_one.astype(jnp.bfloat16))
     parts = (grad_weight_one, grad_weight_two, grad_gain_one, grad_gain_two)
-    flat = jnp.concatenate([part.reshape(-1) for part in parts])
-    flat = summed_everywhere(flat, ("dp", "space_0"), ("space_1", "space_2"))
-    sizes = [part.size for part in parts]
+    rows = jnp.concatenate([part.reshape(-1, chan_mid) for part in parts])
+    rows = summed_everywhere(rows, ("dp", "space_0"), ("space_1", "space_2"))
+    sizes = [part.size // chan_mid for part in parts]
     bounds = [sum(sizes[:index]) for index in range(len(sizes) + 1)]
     grad_weight_one, grad_weight_two, grad_gain_one, grad_gain_two = (
-        flat[start:end].reshape(part.shape)
+        rows[start:end].reshape(part.shape)
         for start, end, part in zip(bounds[:-1], bounds[1:], parts)
     )
     return (grad_weight_one, grad_weight_two, grad_gain_one, grad_gain_two)

time: 96.4 us -> 99.7 us (1.034)
  other arithmetic: 5.8 us -> 8.9 us
    all_to_all x1 -> x2, other arithmetic: 0.54 us -> 1.89 us  [from_everyone(): lax.all_to_all(jnp.broadcast_to(value[None], (peers, *value.shape)), axis...]
    reshape x5 -> x3, local copies, waits for them, and re-layouts: 1.93 us -> 0.6 us  [the longest x1 0.52 us: on_device(): rows[start:end].reshape(part.shape)]
    all_to_all x0 -> x1, other arithmetic: none -> 1.18 us  [summed_everywhere(): mine = lax.all_to_all(pieces, far, 0, 0, tiled=True).sum(axis=0)]
    unnamed x26 -> x36, local copies, waits for them, and re-layouts: 0.1 us -> 1.17 us
where the time goes in v6:
time: 99.7 us; the launch traced here: 98.6 us
  blocking collectives  58.3 us (58%)
  starting transfers between devices  12.6 us (13%)
  local copies, waits for them, and re-layouts  9.44 us (9%)
  other arithmetic  8.9 us (9%)
  matrix products  4.34 us (4%)
  waiting for transfers between devices  2.86 us (3%)
  between operations  2.12 us (2%)
    all_to_all x2, blocking collectives, from_everyone(): lax.all_to_all(jnp.broadcast_to(value[None], (peers, *value.shape)), axis...  30.6 us
    all_to_all x1, blocking collectives, summed_everywhere(): mine = lax.all_to_all(pieces, far, 0, 0, tiled=True).sum(axis=0)  27.7 us
    ppermute x3, starting transfers between devices, from_behind(): lax.ppermute(value, axis, [(source, source + steps) for source in range(f...  12.6 us
    ppermute x3, waiting for transfers between devices, from_behind(): lax.ppermute(value, axis, [(source, source + steps) for source in range(f...  2.86 us
    conv_general_dilated x2, matrix products, weight_grad(): lax.conv_general_dilated(padded, grad_z, (1, 1), 'VALID', rhs_dilation=(2...  2.42 us
    gather x3, local copies, waits for them, and re-layouts, select_rows(): picked = jnp.take(source, positions, axis=0)  2 us
  transfers between devices with their start and end apart: 3, of which 1 were waited for; matrix products, arithmetic and copies ran while one was open for 3% of the time, Pallas kernels for 0%

profile of v6, /device:TPU:1, one launch (start us, length us, event | category | flops | bytes accessed | tf_op | source)
XLA Modules:
  0.0 98.6 jit_solution(13516731332869625745)
XLA Ops:
  1.3 1.7 %reshape_squeeze.16 = bf16[16,16,16,32]{3,2,1,0:T(8,128)(2,1)S(1)} reshape(bf16[1,16,16,512]{3,2,1,0:T(8,128)(2,1)} %param.16) | data formatting | bytes 524288 | tf_op jit(solution)/shard_map/reshape;squeeze | solution.py:166
  3.1 0.6 copy_select_fusion
  3.9 8.7 %collective-permute-start = (bf16[16,512]{1,0:T(8,128)(2,1)S(1)}, bf16[16,512]{1,0:T(8,128)(2,1)S(1)}, u32[]{:S(2)}, u32[]{:S(2)}) collective-permute-start(bf16[16,512]{1,0:T(8,128)(2,1)S(1)} %reshape_squeeze.18), channel_id=1, source_target_pairs={{1,0},{2,1},{3,2},{4,3},{5,4},{6,5},{7,6},{8,7},{9,8},{10,9},{11,1... | collective-permute-start | bytes 49160 | tf_op jit(solution)/shard_map/ppermute | solution.py:18
  12.7 0.6 broadcast_compare_fusion
  13.4 0.6 compare_and_fusion
  14.3 0.7 gather_fusion.1
  15.4 1.2 %fusion.31 = (f32[16,8,8]{0,2,1:T(8,128)S(1)}, f32[16,8,8,64]{3,0,2,1:T(8,128)S(1)}) fusion(bf16[3,3,32,64]{3,2,1,0:T(8,128)(2,1)S(1)} %copy-done.14, bf16[16,17,1,32]{3,0,2,1:T(8,128)(2,1)S(1)} %maximum_bitcast_fusion, bf16[16,1,16,32]{3,0,2,1:T(8,128)(2,1)S(1)} %copy.51, bf16[16,16,16,32]{3,0,2,1:T(8,128)(2,1)S(1)} %copy_select_fusion), kind=kOutput, calls=%fused_computation.102 | convolution fusion | flops 38109184 | bytes 599040 | tf_op jit(solution)/shard_map/conv_general_dilated | solution.py:121
  16.6 0.4 multiply_reduce_fusion.2
  17.0 0.4 multiply_convert_fusion.1
  17.5 1.9 %collective-permute-start.1 = (bf16[16,512]{1,0:T(8,128)(2,1)S(1)}, bf16[16,512]{1,0:T(8,128)(2,1)S(1)}, u32[]{:S(2)}, u32[]{:S(2)}) collective-permute-start(bf16[16,512]{1,0:T(8,128)(2,1)S(1)} %reshape_squeeze.20), channel_id=1, source_target_pairs={{1,0},{2,1},{3,2},{4,3},{5,4},{6,5},{7,6},{8,7},{9,8},{10,9},{11,1... | collective-permute-start | bytes 49160 | tf_op jit(solution)/shard_map/ppermute | solution.py:18
  19.7 2.9 %collective-permute-done.1 = bf16[16,512]{1,0:T(8,128)(2,1)S(1)} collective-permute-done((bf16[16,512]{1,0:T(8,128)(2,1)S(1)}, bf16[16,512]{1,0:T(8,128)(2,1)S(1)}, u32[]{:S(2)}, u32[]{:S(2)}) %collective-permute-start.1) | collective-permute-done | bytes 16416 | tf_op jit(solution)/shard_map/ppermute | solution.py:18
  22.6 0.7 gather_fusion.2
  23.6 0.4 fusion.32
  24.3 0.7 multiply_reduce_fusion.4
  25.2 0.4 fusion.33
  25.7 1.9 %collective-permute-start.2 = (bf16[16,576]{1,0:T(8,128)(2,1)S(1)}, bf16[16,576]{1,0:T(8,128)(2,1)}, u32[]{:S(2)}, u32[]{:S(2)}) collective-permute-start(bf16[16,576]{1,0:T(8,128)(2,1)S(1)} %convert_element_type.49), channel_id=1, source_target_pairs={{0,1},{1,2},{2,3},{3,4},{4,5},{5,6},{6,7},{7,8},{8,9},{9,10},{10,1... | collective-permute-start | bytes 55304 | tf_op jit(solution)/shard_map/ppermute | solution.py:18
  27.7 1.1 %fusion.7 = f32[3,3,64,64]{3,2,1,0:T(8,128)S(1)} fusion(bf16[16,4,4,64]{3,0,2,1:T(8,128)(2,1)S(1)} %multiply_convert_fusion.3, bf16[16,9,1,64]{3,0,2,1:T(8,128)(2,1)S(1)} %maximum_bitcast_fusion.1, bf16[16,1,8,64]{3,0,2,1:T(8,128)(2,1)} %copy-done.6, bf16[16,8,8,64]{3,0,2,1:T(8,128)(2,1)S(1)} %multiply_convert_fusion.1), kind=kOutput, calls=%fused_computation.22 | convolution fusion | flops 19040256 | bytes 346112 | tf_op jit(solution)/shard_map/conv_general_dilated | solution.py:132
  29.0 0.7 fusion.13
  29.7 0.7 gather_fusion
  30.9 0.7 multiply_reduce_fusion
  31.8 1.3 %fusion = f32[3,3,32,64]{3,2,1,0:T(8,128)S(1)} fusion(bf16[16,17,1,32]{3,0,2,1:T(8,128)(2,1)S(1)} %copy-done.2, bf16[16,1,16,32]{3,0,2,1:T(8,128)(2,1)S(1)} %copy-done.4, bf16[16,16,16,32]{3,0,2,1:T(8,128)(2,1)S(1)} %copy_select_fusion, f32[16,8,8,64]{3,0,2,1:T(8,128)S(1)} %get-tuple-element.47, f32[16,8,8,64]{3,0,2,1:T(8,128)S(1)} %get-tuple-element.76, ...), kind=kOutput, calls=%fused_computation.13 | convolution fusion | flops 38568960 | bytes 910592 | tf_op jit(solution)/shard_map/conv_general_dilated | solution.py:132
  33.5 0.3 reshape.425
  33.7 27.7 %all_to_all.15 = f32[64,1,896]{2,1,0:T(1,128)S(1)} all-to-all(f32[64,1,896]{2,1,0:T(1,128)S(1)} %reshape.425), channel_id=1, replica_groups=mesh['dp'=8,'space_0'=8,'space_1'=4,'space_2'=2] {'dp','space_0'}, dimensions={0} | all-to-all | bytes 458752 | tf_op jit(solution)/shard_map/all_to_all | solution.py:78
  61.4 0.5 broadcast.288
  61.9 1.2 %reduce.6 = f32[64,896]{1,0:T(8,128)S(1)} reduce(f32[64,1,896]{2,1,0:T(1,128)S(1)} %all_to_all.15, f32[]{:T(128)} %broadcast.288), dimensions={1}, to_apply=%all_to_all.9.reduce_sub_computation | reduce | bytes 458756 | tf_op jit(solution)/shard_map/all_to_all | solution.py:78
  63.5 14.3 %all_to_all.16 = f32[8,1,896]{2,1,0:T(1,128)S(1)} all-to-all(f32[8,1,896]{2,1,0:T(1,128)S(1)} %reshape.427), channel_id=1, replica_groups=mesh['dp'=8,'space_0'=8,'space_1'=4,'space_2'=2] {'space_1','space_2'}, dimensions={0} | all-to-all | bytes 57344 | tf_op jit(solution)/shard_map/all_to_all | solution.py:49
  77.7 0.7 reduce.7
  78.9 16.4 %all_to_all.17 = f32[64,1,896]{2,1,0:T(1,128)S(1)} all-to-all(f32[64,1,896]{2,1,0:T(1,128)S(1)} %reshape.429), channel_id=1, replica_groups=mesh['dp'=8,'space_0'=8,'space_1'=4,'space_2'=2] {'dp','space_0'}, dimensions={0} | all-to-all | bytes 458752 | tf_op jit(solution)/shard_map/all_to_all | solution.py:49
  95.3 1.2 %reduce.8 = f32[64,896]{1,0:T(8,128)S(1)} reduce(f32[64,1,896]{2,1,0:T(1,128)S(1)} %all_to_all.17, f32[]{:T(128)} %broadcast.288), dimensions={1}, to_apply=%all_to_all.11.reduce_sub_computation | reduce | bytes 458756 | tf_op jit(solution)/shard_map/all_to_all | solution.py:49
  96.7 0.5 slice_bitcast_fusion.2
  97.2 0.7 slice.210
  97.9 0.7 slice.211
  (114 shorter events, 4.1 us)
Async XLA Ops:
  0.6 23.0 %copy-start = (bf16[3,3,64,64]{3,2,1,0:T(8,128)(2,1)S(1)}, bf16[3,3,64,64]{3,2,1,0:T(8,128)(2,1)}, u32[]{:S(2)}) copy-start(bf16[3,3,64,64]{3,2,1,0:T(8,128)(2,1)} %param.21) | copy-start | bytes 221188
  3.1 9.6 %copy-start.7 = (s32[1,16,8]{1,2,0:T(8,128)S(1)}, s32[1,16,8]{1,2,0:T(8,128)}, u32[]{:S(2)}) copy-start(s32[1,16,8]{1,2,0:T(8,128)} %param.19) | copy-start | bytes 1540
  3.1 10.9 %copy-start.5 = (bf16[1,16,4,256]{3,2,1,0:T(4,128)(2,1)S(1)}, bf16[1,16,4,256]{3,2,1,0:T(4,128)(2,1)}, u32[]{:S(2)}) copy-start(bf16[1,16,4,256]{3,2,1,0:T(4,128)(2,1)} %param.17) | copy-start | bytes 98308
  3.7 11.6 %copy-start.14 = (bf16[3,3,32,64]{3,2,1,0:T(8,128)(2,1)S(1)}, bf16[3,3,32,64]{3,2,1,0:T(8,128)(2,1)}, u32[]{:S(2)}) copy-start(bf16[3,3,32,64]{3,2,1,0:T(8,128)(2,1)} %param.20) | copy-start | bytes 110596
  3.9 10.4 %collective-permute-start = (bf16[16,512]{1,0:T(8,128)(2,1)S(1)}, bf16[16,512]{1,0:T(8,128)(2,1)S(1)}, u32[]{:S(2)}, u32[]{:S(2)}) collective-permute-start(bf16[16,512]{1,0:T(8,128)(2,1)S(1)} %reshape_squeeze.18), channel_id=1, source_target_pairs={{1,0},{2,1},{3,2},{4,3},{5,4},{6,5},{7,6},{8,7},{9,8},{10,9},{11,1... | collective-permute-start | bytes 49160 | tf_op jit(solution)/shard_map/ppermute | solution.py:18
  15.2 1.4 %copy-start.3 = (bf16[16,1,16,32]{3,0,2,1:T(8,128)(2,1)}, bf16[16,1,16,32]{3,0,2,1:T(8,128)(2,1)S(1)}, u32[]{:S(2)}) copy-start(bf16[16,1,16,32]{3,0,2,1:T(8,128)(2,1)S(1)} %copy.51) | copy-start | bytes 49156
  15.4 1.2 %copy-start.1 = (bf16[16,17,1,32]{3,0,2,1:T(8,128)(2,1)}, bf16[16,17,1,32]{3,0,2,1:T(8,128)(2,1)S(1)}, u32[]{:S(2)}) copy-start(bf16[16,17,1,32]{3,0,2,1:T(8,128)(2,1)S(1)} %maximum_bitcast_fusion) | copy-start | bytes 52228
  15.4 1.6 %copy-start.9 = (f32[64]{0:T(128)S(1)}, f32[64]{0:T(128)}, u32[]{:S(2)}) copy-start(f32[64]{0:T(128)} %param.22) | copy-start | bytes 772
  17.5 5.1 %collective-permute-start.1 = (bf16[16,512]{1,0:T(8,128)(2,1)S(1)}, bf16[16,512]{1,0:T(8,128)(2,1)S(1)}, u32[]{:S(2)}, u32[]{:S(2)}) collective-permute-start(bf16[16,512]{1,0:T(8,128)(2,1)S(1)} %reshape_squeeze.20), channel_id=1, source_target_pairs={{1,0},{2,1},{3,2},{4,3},{5,4},{6,5},{7,6},{8,7},{9,8},{10,9},{11,1... | collective-permute-start | bytes 49160 | tf_op jit(solution)/shard_map/ppermute | solution.py:18
  23.2 1.0 %copy-start.8 = (f32[64]{0:T(128)S(1)}, f32[64]{0:T(128)}, u32[]{:S(2)}) copy-start(f32[64]{0:T(128)} %param.23) | copy-start | bytes 772
  23.5 0.8 copy-start.6
  25.7 3.2 %collective-permute-start.2 = (bf16[16,576]{1,0:T(8,128)(2,1)S(1)}, bf16[16,576]{1,0:T(8,128)(2,1)}, u32[]{:S(2)}, u32[]{:S(2)}) collective-permute-start(bf16[16,576]{1,0:T(8,128)(2,1)S(1)} %convert_element_type.49), channel_id=1, source_target_pairs={{0,1},{1,2},{2,3},{3,4},{4,5},{5,6},{6,7},{7,8},{8,9},{9,10},{10,1... | collective-permute-start | bytes 55304 | tf_op jit(solution)/shard_map/ppermute | solution.py:18
  28.8 1.6 %copy-start.12 = (pred[48]{0:T(512)(128)(4,1)S(1)}, pred[48]{0:T(512)(128)(4,1)}, u32[]{:S(2)}) copy-start(pred[48]{0:T(512)(128)(4,1)} %get-tuple-element.50) | copy-start | bytes 148
  28.8 1.6 %copy-start.13 = (pred[48]{0:T(512)(128)(4,1)S(1)}, pred[48]{0:T(512)(128)(4,1)}, u32[]{:S(2)}) copy-start(pred[48]{0:T(512)(128)(4,1)} %get-tuple-element.74) | copy-start | bytes 148
  29.0 2.0 %copy-start.10 = (f32[64]{0:T(128)S(1)}, f32[64]{0:T(128)}, u32[]{:S(2)}) copy-start(f32[64]{0:T(128)} %param.22) | copy-start | bytes 772
  30.9 0.9 copy-start.2
  30.9 0.9 copy-start.4
  31.8 1.4 %copy-start.11 = (f32[64]{0:T(128)S(1)}, f32[64]{0:T(128)}, u32[]{:S(2)}) copy-start(f32[64]{0:T(128)} %get-tuple-element.44) | copy-start | bytes 772

commit v7 on v5

--- a/solution.py
+++ b/solution.py
@@ -164,25 +164,29 @@
     field = image[0].reshape(slots, tile, tile, chan_in)
     field = jnp.where(live[:, None, None, None], field, jnp.zeros_like(field))
     image_rows = field[:, 0].reshape(slots, tile * chan_in)
+    south_image = select_rows(image_rows, nearby[:, 6], offset).reshape(slots, 1, tile, chan_in)
+    strip = jnp.concatenate([field, south_image], axis=1)[:, :, :3, :]
+    strip_following = from_behind(strip, SPACE, -1)
     image_cols = field[:, :, 0, :].reshape(slots, tile * chan_in)
-    following = from_behind(image_cols, SPACE, -1)
-    source = jnp.concatenate([image_rows, image_cols, following], axis=0)
-    south_image, east_image, diag_image = select_many(
-        source,
-        ((nearby[:, 6], offset), (nearby[:, 4], offset - slots), (nearby[:, 7], offset - slots)),
+    following = strip_following[:, :tile, 0, :].reshape(slots, tile * chan_in)
+    source = jnp.concatenate([image_cols, following], axis=0)
+    east_image, diag_image = select_many(
+        source, ((nearby[:, 4], offset), (nearby[:, 7], offset))
     )
     padded_one = assemble(
         field,
-        south_image.reshape(slots, tile, chan_in),
+        south_image[:, 0],
         east_image.reshape(slots, tile, chan_in),
         diag_image[:, :chan_in],
     )
     normed_one, inverse_one = norm_forward(conv_forward(padded_one, weight_one))
     hidden_one = normed_one * gain_one
     act_one = jax.nn.silu(hidden_one).astype(jnp.bfloat16)
+    normed_edge, _ = norm_forward(conv_forward(strip_following, weight_one))
+    act_following = jax.nn.silu(normed_edge * gain_one).astype(jnp.bfloat16)
+    act_following = act_following.reshape(slots, half * chan_mid)
     act_rows = act_one[:, 0].reshape(slots, half * chan_mid)
     act_cols = act_one[:, :, 0, :].reshape(slots, half * chan_mid)
-    act_following = from_behind(act_cols, SPACE, -1)
     act_source = jnp.concatenate([act_rows, act_cols, act_following], axis=0)
     south_act, east_act, diag_act = select_many(
         act_source,

time: 96.4 us -> 93.4 us (0.969)
  waiting for transfers between devices: 2.86 us -> 0.01 us
  starting transfers between devices: 12.6 us -> 10.8 us
  other arithmetic: 5.8 us -> 7.28 us
  blocking collectives: 58.1 us -> 56.7 us
    ppermute x3 -> x2, waiting for transfers between devices: 2.86 us -> 0.01 us  [from_behind(): lax.ppermute(value, axis, [(source, source + steps) for source in range(f...]
    ppermute x3 -> x2, starting transfers between devices: 12.6 us -> 10.8 us  [from_behind(): lax.ppermute(value, axis, [(source, source + steps) for source in range(f...]
    all_to_all x1, blocking collectives: 27.4 us -> 26 us  [summed_everywhere(): lax.all_to_all(lines.reshape(far_peers, -1), far, 0, 0, tiled=True)]
    gather x3 -> x5, local copies, waits for them, and re-layouts: 2 us -> 2.66 us  [select_rows(): picked = jnp.take(source, positions, axis=0)]
    conv_general_dilated x2 -> x3, matrix products: 1.56 us -> 2.04 us  [conv_forward(): lax.conv_general_dilated(padded, weight, (2, 2), 'VALID', dimension_numbe...]
  transfers between devices with their start and end apart: 3 -> 2, of which waited for: 1 -> 0; matrix products, arithmetic and copies ran while one was open for 3% -> 3% of each run, Pallas kernels for 0% -> 0%
where the time goes in v7:
time: 93.4 us; the launch traced here: 92.3 us
  blocking collectives  56.7 us (61%)
  starting transfers between devices  10.8 us (12%)
  local copies, waits for them, and re-layouts  10.5 us (11%)
  other arithmetic  7.28 us (8%)
  matrix products  4.83 us (5%)
  between operations  2.12 us (2%)
    all_to_all x2, blocking collectives, from_everyone(): lax.all_to_all(jnp.broadcast_to(value[None], (peers, *value.shape)), axis...  30.7 us
    all_to_all x1, blocking collectives, summed_everywhere(): lax.all_to_all(lines.reshape(far_peers, -1), far, 0, 0, tiled=True)  26 us
    ppermute x2, starting transfers between devices, from_behind(): lax.ppermute(value, axis, [(source, source + steps) for source in range(f...  10.8 us
    gather x5, local copies, waits for them, and re-layouts, select_rows(): picked = jnp.take(source, positions, axis=0)  2.66 us
    conv_general_dilated x2, matrix products, weight_grad(): lax.conv_general_dilated(padded, grad_z, (1, 1), 'VALID', rhs_dilation=(2...  2.43 us
    conv_general_dilated x3, matrix products, conv_forward(): lax.conv_general_dilated(padded, weight, (2, 2), 'VALID', dimension_numbe...  2.04 us
  transfers between devices with their start and end apart: 2, of which 0 were waited for; matrix products, arithmetic and copies ran while one was open for 3% of the time, Pallas kernels for 0%

profile of v7, /device:TPU:1, one launch (start us, length us, event | category | flops | bytes accessed | tf_op | source)
XLA Modules:
  0.0 92.3 jit_solution(16312893926929453275)
XLA Ops:
  1.4 0.7 and_bitcast_fusion
  2.1 1.7 %reshape_squeeze.19 = bf16[16,16,16,32]{3,2,1,0:T(8,128)(2,1)S(1)} reshape(bf16[1,16,16,512]{3,2,1,0:T(8,128)(2,1)} %param.14) | data formatting | bytes 524288 | tf_op jit(solution)/shard_map/reshape;squeeze | solution.py:164
  3.8 0.6 copy_select_fusion
  4.6 0.6 gather_fusion
  5.5 8.9 %collective-permute-start = (bf16[16,17,3,32]{3,0,2,1:T(8,128)(2,1)S(1)}, bf16[16,17,3,32]{3,0,2,1:T(8,128)(2,1)S(1)}, u32[]{:S(2)}, u32[]{:S(2)}) collective-permute-start(bf16[16,17,3,32]{3,0,2,1:T(8,128)(2,1)S(1)} %pad_maximum_fusion.4), channel_id=1, source_target_pairs={{1,0},{2,1},{3,2},{4,3},{5,4},{6,5},{7,6},{8,7},{9,8},{10,9},{11,1... | collective-permute-start | bytes 156680 | tf_op jit(solution)/shard_map/ppermute | solution.py:18
  14.7 0.6 broadcast_compare_fusion
  15.3 0.6 compare_and_fusion
  16.4 0.6 gather_fusion.1
  17.3 1.2 %fusion.35 = (f32[16,8,8]{0,2,1:T(8,128)S(1)}, f32[16,8,8,64]{3,0,2,1:T(8,128)S(1)}) fusion(bf16[3,3,32,64]{3,2,1,0:T(8,128)(2,1)S(1)} %copy-done.1, bf16[16,17,1,32]{3,0,2,1:T(8,128)(2,1)S(1)} %maximum_bitcast_fusion, bf16[16,1,16,32]{3,0,2,1:T(8,128)(2,1)S(1)} %fusion.13, bf16[16,16,16,32]{3,0,2,1:T(8,128)(2,1)S(1)} %copy_select_fusion), kind=kOutput, calls=%fused_computation.123 | convolution fusion | flops 38109184 | bytes 599040 | tf_op jit(solution)/shard_map/conv_general_dilated | solution.py:119
  18.5 0.4 multiply_reduce_fusion.2
  18.9 0.4 multiply_convert_fusion.1
  19.3 0.5 fusion.36
  20.5 0.7 gather_fusion.2
  21.5 0.4 fusion.37
  22.0 0.2 multiply_reduce_fusion.6
  22.3 0.3 multiply_reduce_fusion.4
  22.8 0.4 fusion.38
  23.3 1.9 %collective-permute-start.1 = (bf16[16,576]{1,0:T(8,128)(2,1)S(1)}, bf16[16,576]{1,0:T(8,128)(2,1)}, u32[]{:S(2)}, u32[]{:S(2)}) collective-permute-start(bf16[16,576]{1,0:T(8,128)(2,1)S(1)} %convert_element_type.53), channel_id=1, source_target_pairs={{0,1},{1,2},{2,3},{3,4},{4,5},{5,6},{6,7},{7,8},{8,9},{9,10},{10,1... | collective-permute-start | bytes 55304 | tf_op jit(solution)/shard_map/ppermute | solution.py:18
  25.2 1.1 %fusion.7 = f32[3,3,64,64]{3,2,1,0:T(8,128)S(1)} fusion(bf16[16,4,4,64]{3,0,2,1:T(8,128)(2,1)S(1)} %multiply_convert_fusion.3, bf16[16,9,1,64]{3,0,2,1:T(8,128)(2,1)S(1)} %maximum_bitcast_fusion.1, bf16[16,1,8,64]{3,0,2,1:T(8,128)(2,1)} %copy-done.5, bf16[16,8,8,64]{3,0,2,1:T(8,128)(2,1)S(1)} %multiply_convert_fusion.1), kind=kOutput, calls=%fused_computation.24 | convolution fusion | flops 19040256 | bytes 346112 | tf_op jit(solution)/shard_map/conv_general_dilated | solution.py:130
  26.7 0.7 fusion.14
  27.4 0.7 gather_fusion.3
  28.6 0.7 multiply_reduce_fusion
  29.4 1.3 %fusion = f32[3,3,32,64]{3,2,1,0:T(8,128)S(1)} fusion(bf16[16,17,1,32]{3,0,2,1:T(8,128)(2,1)S(1)} %copy-done.3, bf16[16,1,16,32]{3,0,2,1:T(8,128)(2,1)S(1)} %fusion.13, bf16[16,16,16,32]{3,0,2,1:T(8,128)(2,1)S(1)} %copy_select_fusion, f32[16,8,8,64]{3,0,2,1:T(8,128)S(1)} %get-tuple-element.46, f32[16,8,8,64]{3,0,2,1:T(8,128)S(1)} %get-tuple-element.81, ...), kind=kOutput, calls=%fused_computation.14 | convolution fusion | flops 38568960 | bytes 910592 | tf_op jit(solution)/shard_map/conv_general_dilated | solution.py:130
  30.9 1.1 %concatenate.152 = f32[55808]{0:T(1024)S(1)} concatenate(f32[18432]{0:T(1024)S(1)} %reshape.543, f32[36864]{0:T(1024)S(1)} %reshape.544, f32[64]{0:T(128)S(1)} %get-tuple-element.40, f32[64]{0:T(128)S(1)} %get-tuple-element.43, f32[384]{0:T(512)S(1)} %broadcast_in_dim.202), dimensions={0} | concatenate | bytes 446464 | tf_op jit(solution)/shard_map/concatenate | solution.py:44
  31.9 0.4 all_to_all.14
  32.3 26.0 %all_to_all.21 = f32[64,1,872]{2,1,0:T(1,128)S(1)} all-to-all(f32[64,1,872]{2,1,0:T(1,128)S(1)} %all_to_all.14), channel_id=1, replica_groups=mesh['dp'=8,'space_0'=8,'space_1'=4,'space_2'=2] {'dp','space_0'}, dimensions={0} | all-to-all | bytes 446464 | tf_op jit(solution)/shard_map/all_to_all | solution.py:77
  58.5 14.3 %all_to_all.22 = f32[8,1,872]{2,1,0:T(1,128)S(1)} all-to-all(f32[8,1,872]{2,1,0:T(1,128)S(1)} %broadcast_in_dim.203), channel_id=1, replica_groups=mesh['dp'=8,'space_0'=8,'space_1'=4,'space_2'=2] {'space_1','space_2'}, dimensions={0} | all-to-all | bytes 55808 | tf_op jit(solution)/shard_map/all_to_all | solution.py:49
  73.0 16.4 %all_to_all.23 = f32[64,1,872]{2,1,0:T(1,128)S(1)} all-to-all(f32[64,1,872]{2,1,0:T(1,128)S(1)} %broadcast_in_dim.204), channel_id=1, replica_groups=mesh['dp'=8,'space_0'=8,'space_1'=4,'space_2'=2] {'dp','space_0'}, dimensions={0} | all-to-all | bytes 446464 | tf_op jit(solution)/shard_map/all_to_all | solution.py:49
  89.4 0.5 reduce.10
  90.1 0.6 fusion.32
  90.7 0.7 reshape.546
  91.5 0.8 reshape.547
  (117 shorter events, 4.2 us)
Async XLA Ops:
  0.6 20.9 %copy-start = (bf16[3,3,64,64]{3,2,1,0:T(8,128)(2,1)S(1)}, bf16[3,3,64,64]{3,2,1,0:T(8,128)(2,1)}, u32[]{:S(2)}) copy-start(bf16[3,3,64,64]{3,2,1,0:T(8,128)(2,1)} %param.19) | copy-start | bytes 221188
  4.4 9.9 %copy-start.7 = (s32[1,16,8]{1,2,0:T(8,128)S(1)}, s32[1,16,8]{1,2,0:T(8,128)}, u32[]{:S(2)}) copy-start(s32[1,16,8]{1,2,0:T(8,128)} %param.17) | copy-start | bytes 1540
  4.4 10.2 %copy-start.4 = (bf16[1,16,4,256]{3,2,1,0:T(4,128)(2,1)S(1)}, bf16[1,16,4,256]{3,2,1,0:T(4,128)(2,1)}, u32[]{:S(2)}) copy-start(bf16[1,16,4,256]{3,2,1,0:T(4,128)(2,1)} %param.15) | copy-start | bytes 98308
  5.4 11.8 %copy-start.1 = (bf16[3,3,32,64]{3,2,1,0:T(8,128)(2,1)S(1)}, bf16[3,3,32,64]{3,2,1,0:T(8,128)(2,1)}, u32[]{:S(2)}) copy-start(bf16[3,3,32,64]{3,2,1,0:T(8,128)(2,1)} %param.18) | copy-start | bytes 110596
  5.5 10.7 %collective-permute-start = (bf16[16,17,3,32]{3,0,2,1:T(8,128)(2,1)S(1)}, bf16[16,17,3,32]{3,0,2,1:T(8,128)(2,1)S(1)}, u32[]{:S(2)}, u32[]{:S(2)}) collective-permute-start(bf16[16,17,3,32]{3,0,2,1:T(8,128)(2,1)S(1)} %pad_maximum_fusion.4), channel_id=1, source_target_pairs={{1,0},{2,1},{3,2},{4,3},{5,4},{6,5},{7,6},{8,7},{9,8},{10,9},{11,1... | collective-permute-start | bytes 156680 | tf_op jit(solution)/shard_map/ppermute | solution.py:18
  17.3 1.2 %copy-start.2 = (bf16[16,17,1,32]{3,0,2,1:T(8,128)(2,1)}, bf16[16,17,1,32]{3,0,2,1:T(8,128)(2,1)S(1)}, u32[]{:S(2)}) copy-start(bf16[16,17,1,32]{3,0,2,1:T(8,128)(2,1)S(1)} %maximum_bitcast_fusion) | copy-start | bytes 52228
  17.3 1.6 %copy-start.6 = (f32[64]{0:T(128)S(1)}, f32[64]{0:T(128)}, u32[]{:S(2)}) copy-start(f32[64]{0:T(128)} %param.20) | copy-start | bytes 772
  21.2 1.1 %copy-start.8 = (f32[64]{0:T(128)S(1)}, f32[64]{0:T(128)}, u32[]{:S(2)}) copy-start(f32[64]{0:T(128)} %param.21) | copy-start | bytes 772
  21.4 0.6 copy-start.5
  23.3 3.3 %collective-permute-start.1 = (bf16[16,576]{1,0:T(8,128)(2,1)S(1)}, bf16[16,576]{1,0:T(8,128)(2,1)}, u32[]{:S(2)}, u32[]{:S(2)}) collective-permute-start(bf16[16,576]{1,0:T(8,128)(2,1)S(1)} %convert_element_type.53), channel_id=1, source_target_pairs={{0,1},{1,2},{2,3},{3,4},{4,5},{5,6},{6,7},{7,8},{8,9},{9,10},{10,1... | collective-permute-start | bytes 55304 | tf_op jit(solution)/shard_map/ppermute | solution.py:18
  26.4 1.7 %copy-start.9 = (pred[48]{0:T(512)(128)(4,1)S(1)}, pred[48]{0:T(512)(128)(4,1)}, u32[]{:S(2)}) copy-start(pred[48]{0:T(512)(128)(4,1)} %get-tuple-element.49) | copy-start | bytes 148
  26.4 1.7 %copy-start.10 = (pred[48]{0:T(512)(128)(4,1)S(1)}, pred[48]{0:T(512)(128)(4,1)}, u32[]{:S(2)}) copy-start(pred[48]{0:T(512)(128)(4,1)} %get-tuple-element.78) | copy-start | bytes 148
  28.5 0.9 copy-start.3

commit v8 on v5

--- a/solution.py
+++ b/solution.py
@@ -161,38 +161,37 @@
     offset = lax.axis_index(SPACE) * slots
     nearby = neighbours[0]
     live = jnp.arange(slots) < live_count[0, 0]
-    field = image[0].reshape(slots, tile, tile, chan_in)
-    field = jnp.where(live[:, None, None, None], field, jnp.zeros_like(field))
-    image_rows = field[:, 0].reshape(slots, tile * chan_in)
-    image_cols = field[:, :, 0, :].reshape(slots, tile * chan_in)
-    following = from_behind(image_cols, SPACE, -1)
-    source = jnp.concatenate([image_rows, image_cols, following], axis=0)
-    south_image, east_image, diag_image = select_many(
-        source,
-        ((nearby[:, 6], offset), (nearby[:, 4], offset - slots), (nearby[:, 7], offset - slots)),
-    )
+    raw = image[0].reshape(slots, tile, tile, chan_in)
+    edge = raw[:, :, :3, :].reshape(slots, tile * 3 * chan_in)
+    edge_following = from_behind(edge, SPACE, -1)
+    field = jnp.where(live[:, None, None, None], raw, jnp.zeros_like(raw))
+    pool = jnp.concatenate([edge, edge_following], axis=0)
+    east_strip, diag_strip = select_many(pool, ((nearby[:, 4], offset), (nearby[:, 7], offset)))
+    east_strip = east_strip.reshape(slots, tile, 3, chan_in)
+    diag_strip = diag_strip.reshape(slots, tile, 3, chan_in)
+    south_image = select_rows(field[:, 0].reshape(slots, tile * chan_in), nearby[:, 6], offset)
     padded_one = assemble(
         field,
         south_image.reshape(slots, tile, chan_in),
-        east_image.reshape(slots, tile, chan_in),
-        diag_image[:, :chan_in],
-    )
-    normed_one, inverse_one = norm_forward(conv_forward(padded_one, weight_one))
-    hidden_one = normed_one * gain_one
-    act_one = jax.nn.silu(hidden_one).astype(jnp.bfloat16)
-    act_rows = act_one[:, 0].reshape(slots, half * chan_mid)
-    act_cols = act_one[:, :, 0, :].reshape(slots, half * chan_mid)
-    act_following = from_behind(act_cols, SPACE, -1)
-    act_source = jnp.concatenate([act_rows, act_cols, act_following], axis=0)
-    south_act, east_act, diag_act = select_many(
-        act_source,
-        ((nearby[:, 6], offset), (nearby[:, 4], offset - slots), (nearby[:, 7], offset - slots)),
-    )
+        east_strip[:, :, 0, :],
+        diag_strip[:, 0, 0, :],
+    )
+
+    def activation(padded):
+        normed, inverse = norm_forward(conv_forward(padded, weight_one))
+        hidden = normed * gain_one
+        return normed, inverse, hidden, jax.nn.silu(hidden).astype(jnp.bfloat16)
+
+    normed_one, inverse_one, hidden_one, act_one = activation(padded_one)
+    east_act = activation(jnp.concatenate([east_strip, diag_strip[:, :1]], axis=1))[3]
+    east_act = jnp.where((nearby[:, 4] >= 0)[:, None, None, None], east_act, jnp.zeros_like(east_act))
+    diag_act = activation(diag_strip[:, :3])[3]
+    south_act = select_rows(act_one[:, 0].reshape(slots, half * chan_mid), nearby[:, 6], offset)
     padded_two = assemble(
         act_one,
         south_act.reshape(slots, half, chan_mid),
         east_act.reshape(slots, half, chan_mid),
-        diag_act[:, :chan_mid],
+        diag_act.reshape(slots, chan_mid),
     )
     normed_two, inverse_two = norm_forward(conv_forward(padded_two, weight_two))
     hidden_two = normed_two * gain_two

time: 96.4 us -> 92.9 us (0.964)
  blocking collectives: 58.1 us -> 55.1 us
  waiting for transfers between devices: 2.86 us -> 0.01 us
  other arithmetic: 5.8 us -> 7.73 us
  starting transfers between devices: 12.6 us -> 10.7 us
  local copies, waits for them, and re-layouts: 9.63 us -> 11 us
  matrix products: 4.33 us -> 5.3 us
    all_to_all x1, blocking collectives: 27.4 us -> 24.5 us  [summed_everywhere(): lax.all_to_all(lines.reshape(far_peers, -1), far, 0, 0, tiled=True)]
    ppermute x3 -> x2, waiting for transfers between devices: 2.86 us -> 0.01 us  [from_behind(): lax.ppermute(value, axis, [(source, source + steps) for source in range(f...]
    ppermute x3 -> x2, starting transfers between devices: 12.6 us -> 10.7 us  [from_behind(): lax.ppermute(value, axis, [(source, source + steps) for source in range(f...]
    conv_general_dilated x2 -> x4, matrix products: 1.56 us -> 2.5 us  [conv_forward(): lax.conv_general_dilated(padded, weight, (2, 2), 'VALID', dimension_numbe...]
    gather x3 -> x4, local copies, waits for them, and re-layouts: 2 us -> 2.61 us  [select_rows(): picked = jnp.take(source, positions, axis=0)]
    another operation x5 -> x4, local copies, waits for them, and re-layouts: 2.16 us -> 1.98 us  [the longest x1 1.75 us: on_device(): raw = image[0].reshape(slots, tile, tile, chan_in)]
  transfers between devices with their start and end apart: 3 -> 2, of which waited for: 1 -> 0; matrix products, arithmetic and copies ran while one was open for 3% -> 6% of each run, Pallas kernels for 0% -> 0%
where the time goes in v8:
time: 92.9 us; the launch traced here: 91.9 us
  blocking collectives  55.1 us (59%)
  local copies, waits for them, and re-layouts  11 us (12%)
  starting transfers between devices  10.7 us (12%)
  other arithmetic  7.73 us (8%)
  matrix products  5.3 us (6%)
  between operations  2.08 us (2%)
    all_to_all x2, blocking collectives, from_everyone(): lax.all_to_all(jnp.broadcast_to(value[None], (peers, *value.shape)), axis...  30.6 us
    all_to_all x1, blocking collectives, summed_everywhere(): lax.all_to_all(lines.reshape(far_peers, -1), far, 0, 0, tiled=True)  24.5 us
    ppermute x2, starting transfers between devices, from_behind(): lax.ppermute(value, axis, [(source, source + steps) for source in range(f...  10.7 us
    gather x4, local copies, waits for them, and re-layouts, select_rows(): picked = jnp.take(source, positions, axis=0)  2.61 us
    conv_general_dilated x4, matrix products, conv_forward(): lax.conv_general_dilated(padded, weight, (2, 2), 'VALID', dimension_numbe...  2.5 us
    conv_general_dilated x2, matrix products, weight_grad(): lax.conv_general_dilated(padded, grad_z, (1, 1), 'VALID', rhs_dilation=(2...  2.44 us
  transfers between devices with their start and end apart: 2, of which 0 were waited for; matrix products, arithmetic and copies ran while one was open for 6% of the time, Pallas kernels for 0%

profile of v8, /device:TPU:1, one launch (start us, length us, event | category | flops | bytes accessed | tf_op | source)
XLA Modules:
  0.0 91.9 jit_solution(3275361211349612603)
XLA Ops:
  0.7 1.8 %reshape_squeeze.10 = bf16[16,16,16,32]{3,2,1,0:T(8,128)(2,1)S(1)} reshape(bf16[1,16,16,512]{3,2,1,0:T(8,128)(2,1)} %param.16) | data formatting | bytes 524288 | tf_op jit(solution)/shard_map/reshape;squeeze | solution.py:164
  2.8 8.7 %collective-permute-start = (bf16[16,1536]{1,0:T(8,128)(2,1)S(1)}, bf16[16,1536]{1,0:T(8,128)(2,1)S(1)}, u32[]{:S(2)}, u32[]{:S(2)}) collective-permute-start(bf16[16,1536]{1,0:T(8,128)(2,1)S(1)} %reshape.437), channel_id=1, source_target_pairs={{1,0},{2,1},{3,2},{4,3},{5,4},{6,5},{7,6},{8,7},{9,8},{10,9},{11,1... | collective-permute-start | bytes 147464 | tf_op jit(solution)/shard_map/ppermute | solution.py:18
  12.4 0.6 pad_clamp_fusion
  13.0 0.6 copy_select_fusion
  13.8 0.6 broadcast_compare_fusion.1
  14.4 0.6 compare_and_fusion.1
  15.0 0.6 gather_fusion.2
  16.0 0.6 gather_fusion
  17.7 0.5 fusion.35
  18.2 0.5 fusion.36
  19.1 1.2 %fusion.34 = (f32[16,8,8]{0,2,1:T(8,128)S(1)}, f32[16,8,8,64]{3,0,2,1:T(8,128)S(1)}) fusion(bf16[3,3,32,64]{3,2,1,0:T(8,128)(2,1)S(1)} %copy-done.1, bf16[16,17,1,32]{3,0,2,1:T(8,128)(2,1)S(1)} %maximum_bitcast_fusion, bf16[16,1,16,32]{3,0,2,1:T(8,128)(2,1)S(1)} %copy.53, bf16[16,16,16,32]{3,0,2,1:T(8,128)(2,1)S(1)} %copy_select_fusion), kind=kOutput, calls=%fused_computation.116 | convolution fusion | flops 38109184 | bytes 599040 | tf_op jit(solution)/shard_map/conv_general_dilated | solution.py:119
  20.3 0.4 multiply_reduce_fusion.2
  20.8 0.4 multiply_convert_fusion.1
  21.3 0.6 gather_fusion.3
  22.3 0.4 fusion.37
  23.0 0.7 multiply_reduce_fusion.4
  23.9 0.4 fusion.38
  24.4 1.9 %collective-permute-start.1 = (bf16[16,576]{1,0:T(8,128)(2,1)S(1)}, bf16[16,576]{1,0:T(8,128)(2,1)}, u32[]{:S(2)}, u32[]{:S(2)}) collective-permute-start(bf16[16,576]{1,0:T(8,128)(2,1)S(1)} %convert_element_type.57), channel_id=1, source_target_pairs={{0,1},{1,2},{2,3},{3,4},{4,5},{5,6},{6,7},{7,8},{8,9},{9,10},{10,1... | collective-permute-start | bytes 55304 | tf_op jit(solution)/shard_map/ppermute | solution.py:18
  26.3 1.1 %fusion.11 = f32[3,3,64,64]{3,2,1,0:T(8,128)S(1)} fusion(bf16[16,4,4,64]{3,0,2,1:T(8,128)(2,1)S(1)} %multiply_convert_fusion.3, bf16[16,9,1,64]{3,0,2,1:T(8,128)(2,1)} %copy-done.4, bf16[16,1,8,64]{3,0,2,1:T(8,128)(2,1)} %copy-done.6, bf16[16,8,8,64]{3,0,2,1:T(8,128)(2,1)S(1)} %multiply_convert_fusion.1), kind=kOutput, calls=%fused_computation.27 | convolution fusion | flops 19040256 | bytes 346112 | tf_op jit(solution)/shard_map/conv_general_dilated | solution.py:130
  27.8 0.7 fusion.17
  28.5 0.8 gather_fusion.1
  29.8 0.7 multiply_reduce_fusion
  30.7 1.3 %fusion = f32[3,3,32,64]{3,2,1,0:T(8,128)S(1)} fusion(bf16[16,17,1,32]{3,0,2,1:T(8,128)(2,1)S(1)} %copy-done.3, bf16[16,1,16,32]{3,0,2,1:T(8,128)(2,1)S(1)} %copy.53, bf16[16,16,16,32]{3,0,2,1:T(8,128)(2,1)S(1)} %copy_select_fusion, f32[16,8,8,64]{3,0,2,1:T(8,128)S(1)} %get-tuple-element.47, f32[16,8,8,64]{3,0,2,1:T(8,128)S(1)} %get-tuple-element.74, ...), kind=kOutput, calls=%fused_computation.14 | convolution fusion | flops 38568960 | bytes 910592 | tf_op jit(solution)/shard_map/conv_general_dilated | solution.py:130
  32.1 1.1 %concatenate.112 = f32[55808]{0:T(1024)S(1)} concatenate(f32[18432]{0:T(1024)S(1)} %reshape.444, f32[36864]{0:T(1024)S(1)} %reshape.445, f32[64]{0:T(128)S(1)} %get-tuple-element.41, f32[64]{0:T(128)S(1)} %copy-done.11, f32[384]{0:T(512)S(1)} %broadcast_in_dim.182), dimensions={0} | concatenate | bytes 446464 | tf_op jit(solution)/shard_map/concatenate | solution.py:44
  33.2 0.4 all_to_all.14
  33.5 24.5 %all_to_all.21 = f32[64,1,872]{2,1,0:T(1,128)S(1)} all-to-all(f32[64,1,872]{2,1,0:T(1,128)S(1)} %all_to_all.14), channel_id=1, replica_groups=mesh['dp'=8,'space_0'=8,'space_1'=4,'space_2'=2] {'dp','space_0'}, dimensions={0} | all-to-all | bytes 446464 | tf_op jit(solution)/shard_map/all_to_all | solution.py:77
  58.3 14.2 %all_to_all.22 = f32[8,1,872]{2,1,0:T(1,128)S(1)} all-to-all(f32[8,1,872]{2,1,0:T(1,128)S(1)} %broadcast_in_dim.183), channel_id=1, replica_groups=mesh['dp'=8,'space_0'=8,'space_1'=4,'space_2'=2] {'space_1','space_2'}, dimensions={0} | all-to-all | bytes 55808 | tf_op jit(solution)/shard_map/all_to_all | solution.py:49
  72.6 16.4 %all_to_all.23 = f32[64,1,872]{2,1,0:T(1,128)S(1)} all-to-all(f32[64,1,872]{2,1,0:T(1,128)S(1)} %broadcast_in_dim.184), channel_id=1, replica_groups=mesh['dp'=8,'space_0'=8,'space_1'=4,'space_2'=2] {'dp','space_0'}, dimensions={0} | all-to-all | bytes 446464 | tf_op jit(solution)/shard_map/all_to_all | solution.py:49
  89.0 0.5 reduce.12
  89.7 0.6 fusion.31
  90.3 0.7 reshape.447
  91.1 0.8 reshape.448
  (116 shorter events, 4.9 us)
Async XLA Ops:
  0.6 21.7 %copy-start = (bf16[3,3,64,64]{3,2,1,0:T(8,128)(2,1)S(1)}, bf16[3,3,64,64]{3,2,1,0:T(8,128)(2,1)}, u32[]{:S(2)}) copy-start(bf16[3,3,64,64]{3,2,1,0:T(8,128)(2,1)} %param.21) | copy-start | bytes 221188
  0.6 10.9 %copy-start.9 = (s32[1,16,8]{1,2,0:T(8,128)S(1)}, s32[1,16,8]{1,2,0:T(8,128)}, u32[]{:S(2)}) copy-start(s32[1,16,8]{1,2,0:T(8,128)} %param.19) | copy-start | bytes 1540
  0.7 12.3 %copy-start.5 = (bf16[1,16,4,256]{3,2,1,0:T(4,128)(2,1)S(1)}, bf16[1,16,4,256]{3,2,1,0:T(4,128)(2,1)}, u32[]{:S(2)}) copy-start(bf16[1,16,4,256]{3,2,1,0:T(4,128)(2,1)} %param.17) | copy-start | bytes 98308
  2.8 13.2 %collective-permute-start = (bf16[16,1536]{1,0:T(8,128)(2,1)S(1)}, bf16[16,1536]{1,0:T(8,128)(2,1)S(1)}, u32[]{:S(2)}, u32[]{:S(2)}) collective-permute-start(bf16[16,1536]{1,0:T(8,128)(2,1)S(1)} %reshape.437), channel_id=1, source_target_pairs={{1,0},{2,1},{3,2},{4,3},{5,4},{6,5},{7,6},{8,7},{9,8},{10,9},{11,1... | collective-permute-start | bytes 147464 | tf_op jit(solution)/shard_map/ppermute | solution.py:18
  16.8 0.9 %copy-start.1 = (bf16[3,3,32,64]{3,2,1,0:T(8,128)(2,1)S(1)}, bf16[3,3,32,64]{3,2,1,0:T(8,128)(2,1)}, u32[]{:S(2)}) copy-start(bf16[3,3,32,64]{3,2,1,0:T(8,128)(2,1)} %param.20) | copy-start | bytes 110596
  19.1 1.2 %copy-start.2 = (bf16[16,17,1,32]{3,0,2,1:T(8,128)(2,1)}, bf16[16,17,1,32]{3,0,2,1:T(8,128)(2,1)S(1)}, u32[]{:S(2)}) copy-start(bf16[16,17,1,32]{3,0,2,1:T(8,128)(2,1)S(1)} %maximum_bitcast_fusion) | copy-start | bytes 52228
  19.1 1.6 %copy-start.7 = (f32[64]{0:T(128)S(1)}, f32[64]{0:T(128)}, u32[]{:S(2)}) copy-start(f32[64]{0:T(128)} %param.22) | copy-start | bytes 772
  21.2 1.7 %copy-start.10 = (f32[64]{0:T(128)S(1)}, f32[64]{0:T(128)}, u32[]{:S(2)}) copy-start(f32[64]{0:T(128)} %param.23) | copy-start | bytes 772
  22.1 1.5 %copy-start.6 = (bf16[16,1,8,64]{3,0,2,1:T(8,128)(2,1)}, bf16[16,1,8,64]{3,0,2,1:T(8,128)(2,1)S(1)}, u32[]{:S(2)}) copy-start(bf16[16,1,8,64]{3,0,2,1:T(8,128)(2,1)S(1)} %copy.57) | copy-start | bytes 49156
  22.3 1.4 %copy-start.4 = (bf16[16,9,1,64]{3,0,2,1:T(8,128)(2,1)}, bf16[16,9,1,64]{3,0,2,1:T(8,128)(2,1)S(1)}, u32[]{:S(2)}) copy-start(bf16[16,9,1,64]{3,0,2,1:T(8,128)(2,1)S(1)} %maximum_bitcast_fusion.1) | copy-start | bytes 55300
  24.4 3.4 %collective-permute-start.1 = (bf16[16,576]{1,0:T(8,128)(2,1)S(1)}, bf16[16,576]{1,0:T(8,128)(2,1)}, u32[]{:S(2)}, u32[]{:S(2)}) collective-permute-start(bf16[16,576]{1,0:T(8,128)(2,1)S(1)} %convert_element_type.57), channel_id=1, source_target_pairs={{0,1},{1,2},{2,3},{3,4},{4,5},{5,6},{6,7},{7,8},{8,9},{9,10},{10,1... | collective-permute-start | bytes 55304 | tf_op jit(solution)/shard_map/ppermute | solution.py:18
  27.4 1.9 %copy-start.12 = (pred[48]{0:T(512)(128)(4,1)S(1)}, pred[48]{0:T(512)(128)(4,1)}, u32[]{:S(2)}) copy-start(pred[48]{0:T(512)(128)(4,1)} %get-tuple-element.50) | copy-start | bytes 148
  27.5 1.8 %copy-start.13 = (pred[48]{0:T(512)(128)(4,1)S(1)}, pred[48]{0:T(512)(128)(4,1)}, u32[]{:S(2)}) copy-start(pred[48]{0:T(512)(128)(4,1)} %compare_and_fusion.1) | copy-start | bytes 148
  27.7 2.1 %copy-start.8 = (f32[64]{0:T(128)S(1)}, f32[64]{0:T(128)}, u32[]{:S(2)}) copy-start(f32[64]{0:T(128)} %param.22) | copy-start | bytes 772
  29.8 0.9 copy-start.3
  30.7 1.4 %copy-start.11 = (f32[64]{0:T(128)S(1)}, f32[64]{0:T(128)}, u32[]{:S(2)}) copy-start(f32[64]{0:T(128)} %get-tuple-element.44) | copy-start | bytes 772

commit v9 on v7

--- a/solution.py
+++ b/solution.py
@@ -225,14 +225,25 @@
     from_west = from_west.reshape(slots, half + 1, chan_mid)
     from_diag = from_diag.reshape(slots, half + 1, chan_mid)
     from_north = from_north[:, : half * chan_mid].reshape(slots, half, chan_mid)
-    grad_act = grad_padded[:, :half, :half, :]
+    base = grad_padded[:, :half, :half, :]
+    inner = ((jnp.arange(half) > 0)[:, None] & (jnp.arange(half) > 0)[None, :])[None, :, :, None]
+    inner_z, inner_gain = norm_backward(
+        jnp.where(inner, base, 0.0), jnp.where(inner, hidden_one, 0.0), normed_one, inverse_one, gain_one
+    )
+    inner_low = jnp.where(inner, inner_z, 0.0).astype(jnp.bfloat16)
+    inner_weight = weight_grad(padded_one, inner_low)
+    grad_act = base
     grad_act = grad_act.at[:, 0].add(from_north.astype(jnp.float32))
     grad_act = grad_act.at[:, :, 0].add(from_west[:, :half].astype(jnp.float32))
     grad_act = grad_act.at[:, 0, 0].add(from_diag[:, half].astype(jnp.float32))
-    grad_z_one, grad_gain_one = norm_backward(
-        grad_act, hidden_one, normed_one, inverse_one, gain_one
-    )
-    grad_weight_one = weight_grad(padded_one, grad_z_one.astype(jnp.bfloat16))
+    border_z, border_gain = norm_backward(
+        jnp.where(inner, 0.0, grad_act), hidden_one, normed_one, inverse_one, gain_one
+    )
+    border_low = jnp.where(inner, 0.0, border_z).astype(jnp.bfloat16)
+    top = weight_grad(padded_one[:, :3], border_low[:, :1])
+    left = weight_grad(padded_one[:, 2:, :3], border_low[:, 1:, :1])
+    grad_weight_one = inner_weight + top + left
+    grad_gain_one = inner_gain + border_gain
     parts = (grad_weight_one, grad_weight_two, grad_gain_one, grad_gain_two)
     flat = jnp.concatenate([part.reshape(-1) for part in parts])
     flat = summed_everywhere(flat, ("dp", "space_0"), ("space_1", "space_2"))

time: 93.4 us -> 95.9 us (1.027)
  other arithmetic: 7.28 us -> 9.18 us
    reduce_sum x2, other arithmetic: 1.03 us -> 2.05 us  [norm_backward(): grad_gain = jnp.sum(grad_hidden * normed, axis=(0, 1, 2))]
    conv_general_dilated x2 -> x4, matrix products: 2.43 us -> 2.96 us  [weight_grad(): lax.conv_general_dilated(padded, grad_z, (1, 1), 'VALID', rhs_dilation=(2...]
where the time goes in v9:
time: 95.9 us; the launch traced here: 94.8 us
  blocking collectives  56.7 us (59%)
  starting transfers between devices  10.8 us (11%)
  local copies, waits for them, and re-layouts  10.7 us (11%)
  other arithmetic  9.18 us (10%)
  matrix products  5.36 us (6%)
  between operations  2.15 us (2%)
    all_to_all x2, blocking collectives, from_everyone(): lax.all_to_all(jnp.broadcast_to(value[None], (peers, *value.shape)), axis...  30.7 us
    all_to_all x1, blocking collectives, summed_everywhere(): lax.all_to_all(lines.reshape(far_peers, -1), far, 0, 0, tiled=True)  25.9 us
    ppermute x2, starting transfers between devices, from_behind(): lax.ppermute(value, axis, [(source, source + steps) for source in range(f...  10.8 us
    conv_general_dilated x4, matrix products, weight_grad(): lax.conv_general_dilated(padded, grad_z, (1, 1), 'VALID', rhs_dilation=(2...  2.96 us
    gather x5, local copies, waits for them, and re-layouts, select_rows(): picked = jnp.take(source, positions, axis=0)  2.66 us
    reduce_sum x2, other arithmetic, norm_backward(): grad_gain = jnp.sum(grad_hidden * normed, axis=(0, 1, 2))  2.05 us
    conv_general_dilated x3, matrix products, conv_forward(): lax.conv_general_dilated(padded, weight, (2, 2), 'VALID', dimension_numbe...  2.04 us
  transfers between devices with their start and end apart: 2, of which 0 were waited for; matrix products, arithmetic and copies ran while one was open for 3% of the time, Pallas kernels for 0%

profile of v9, /device:TPU:1, one launch (start us, length us, event | category | flops | bytes accessed | tf_op | source)
XLA Modules:
  0.0 94.8 jit_solution(4104585510716314668)
XLA Ops:
  1.4 0.7 and_bitcast_fusion
  2.1 1.7 %reshape_squeeze.19 = bf16[16,16,16,32]{3,2,1,0:T(8,128)(2,1)S(1)} reshape(bf16[1,16,16,512]{3,2,1,0:T(8,128)(2,1)} %param.14) | data formatting | bytes 524288 | tf_op jit(solution)/shard_map/reshape;squeeze | solution.py:164
  3.8 0.6 copy_select_fusion
  4.6 0.6 gather_fusion
  5.5 8.9 %collective-permute-start = (bf16[16,17,3,32]{3,0,2,1:T(8,128)(2,1)S(1)}, bf16[16,17,3,32]{3,0,2,1:T(8,128)(2,1)S(1)}, u32[]{:S(2)}, u32[]{:S(2)}) collective-permute-start(bf16[16,17,3,32]{3,0,2,1:T(8,128)(2,1)S(1)} %pad_maximum_fusion.2), channel_id=1, source_target_pairs={{1,0},{2,1},{3,2},{4,3},{5,4},{6,5},{7,6},{8,7},{9,8},{10,9},{11,1... | collective-permute-start | bytes 156680 | tf_op jit(solution)/shard_map/ppermute | solution.py:18
  14.8 0.6 broadcast_compare_fusion
  15.4 0.6 compare_and_fusion
  16.4 0.6 gather_fusion.1
  17.4 1.2 %fusion.41 = (f32[16,8,8]{0,2,1:T(8,128)S(1)}, f32[16,8,8,64]{3,0,2,1:T(8,128)S(1)}) fusion(bf16[3,3,32,64]{3,2,1,0:T(8,128)(2,1)S(1)} %copy-done.3, bf16[16,17,1,32]{3,0,2,1:T(8,128)(2,1)S(1)} %maximum_bitcast_fusion, bf16[16,1,16,32]{3,0,2,1:T(8,128)(2,1)S(1)} %fusion.16, bf16[16,16,16,32]{3,0,2,1:T(8,128)(2,1)S(1)} %copy_select_fusion), kind=kOutput, calls=%fused_computation.140 | convolution fusion | flops 38109184 | bytes 599040 | tf_op jit(solution)/shard_map/conv_general_dilated | solution.py:119
  18.6 0.4 multiply_reduce_fusion.4
  19.0 0.4 multiply_convert_fusion
  19.4 0.5 fusion.42
  20.6 0.7 gather_fusion.2
  21.6 0.4 fusion.43
  22.3 0.7 multiply_reduce_fusion.7
  23.3 0.4 fusion.44
  23.8 1.9 %collective-permute-start.1 = (bf16[16,576]{1,0:T(8,128)(2,1)S(1)}, bf16[16,576]{1,0:T(8,128)(2,1)}, u32[]{:S(2)}, u32[]{:S(2)}) collective-permute-start(bf16[16,576]{1,0:T(8,128)(2,1)S(1)} %convert_element_type.57), channel_id=1, source_target_pairs={{0,1},{1,2},{2,3},{3,4},{4,5},{5,6},{6,7},{7,8},{8,9},{9,10},{10,1... | collective-permute-start | bytes 55304 | tf_op jit(solution)/shard_map/ppermute | solution.py:18
  25.7 1.1 %fusion.10 = f32[3,3,64,64]{3,2,1,0:T(8,128)S(1)} fusion(bf16[16,4,4,64]{3,0,2,1:T(8,128)(2,1)S(1)} %multiply_convert_fusion.1, bf16[16,9,1,64]{3,0,2,1:T(8,128)(2,1)S(1)} %maximum_bitcast_fusion.1, bf16[16,1,8,64]{3,0,2,1:T(8,128)(2,1)} %copy-done.5, bf16[16,8,8,64]{3,0,2,1:T(8,128)(2,1)S(1)} %multiply_convert_fusion), kind=kOutput, calls=%fused_computation.34 | convolution fusion | flops 19040256 | bytes 346112 | tf_op jit(solution)/shard_map/conv_general_dilated | solution.py:130
  27.1 0.7 fusion.17
  27.8 0.7 gather_fusion.3
  29.0 1.3 %multiply_reduce_fusion.1 = (f32[64]{0:T(128)S(1)}, f32[16,8,8]{0,2,1:T(8,128)S(1)}, f32[16,8,8]{0,2,1:T(8,128)S(1)}, f32[64]{0:T(128)S(1)}, f32[16,8,8]{0,2,1:T...) fusion(f32[16,8,8]{0,2,1:T(8,128)S(1)} %add_rsqrt_fusion, ...), kind=kLoop, calls=%fused_computation.12 | loop fusion | flops 2224000 | bytes 1336128 | tf_op jit(solution)/shard_map/reduce_sum | solution.py:92
  30.4 0.8 select_convert_fusion
  31.3 1.4 %fusion.3 = f32[3,3,32,64]{3,2,1,0:T(8,128)S(1)} fusion(f32[16,8,8,64]{3,0,2,1:T(8,128)S(1)} %get-tuple-element.52, f32[16,8,8]{0,2,1:T(8,128)S(1)} %broadcast_multiply_fusion.2, f32[16,8,8]{0,2,1:T(8,128)S(1)} %broadcast_multiply_fusion.3, f32[64]{0:T(128)S(1)} %copy-done.6, f32[16,8,8]{0,2,1:T(8,128)S(1)} %add_rsqrt_fusion, ...), kind=kOutput, calls=%fused_computation.26 | convolution fusion | flops 38634496 | bytes 910656 | tf_op jit(solution)/shard_map/conv_general_dilated | solution.py:130
  33.5 1.0 %concatenate.152 = f32[55808]{0:T(1024)S(1)} concatenate(f32[18432]{0:T(1024)S(1)} %reshape.590, f32[36864]{0:T(1024)S(1)} %reshape.591, f32[64]{0:T(128)S(1)} %add.180, f32[64]{0:T(128)S(1)} %copy-done.9, f32[384]{0:T(512)S(1)} %broadcast_in_dim.250), dimensions={0} | concatenate | bytes 446464 | tf_op jit(solution)/shard_map/concatenate | solution.py:44
  34.6 0.4 all_to_all.14
  34.9 25.9 %all_to_all.21 = f32[64,1,872]{2,1,0:T(1,128)S(1)} all-to-all(f32[64,1,872]{2,1,0:T(1,128)S(1)} %all_to_all.14), channel_id=1, replica_groups=mesh['dp'=8,'space_0'=8,'space_1'=4,'space_2'=2] {'dp','space_0'}, dimensions={0} | all-to-all | bytes 446464 | tf_op jit(solution)/shard_map/all_to_all | solution.py:77
  61.0 14.3 %all_to_all.22 = f32[8,1,872]{2,1,0:T(1,128)S(1)} all-to-all(f32[8,1,872]{2,1,0:T(1,128)S(1)} %broadcast_in_dim.251), channel_id=1, replica_groups=mesh['dp'=8,'space_0'=8,'space_1'=4,'space_2'=2] {'space_1','space_2'}, dimensions={0} | all-to-all | bytes 55808 | tf_op jit(solution)/shard_map/all_to_all | solution.py:49
  75.5 16.4 %all_to_all.23 = f32[64,1,872]{2,1,0:T(1,128)S(1)} all-to-all(f32[64,1,872]{2,1,0:T(1,128)S(1)} %broadcast_in_dim.252), channel_id=1, replica_groups=mesh['dp'=8,'space_0'=8,'space_1'=4,'space_2'=2] {'dp','space_0'}, dimensions={0} | all-to-all | bytes 446464 | tf_op jit(solution)/shard_map/all_to_all | solution.py:49
  91.9 0.5 reduce.10
  92.7 0.6 fusion.38
  93.3 0.7 reshape.593
  94.0 0.8 reshape.594
  (127 shorter events, 5.2 us)
Async XLA Ops:
  0.6 21.0 %copy-start = (bf16[3,3,64,64]{3,2,1,0:T(8,128)(2,1)S(1)}, bf16[3,3,64,64]{3,2,1,0:T(8,128)(2,1)}, u32[]{:S(2)}) copy-start(bf16[3,3,64,64]{3,2,1,0:T(8,128)(2,1)} %param.19) | copy-start | bytes 221188
  4.4 9.9 %copy-start.7 = (s32[1,16,8]{1,2,0:T(8,128)S(1)}, s32[1,16,8]{1,2,0:T(8,128)}, u32[]{:S(2)}) copy-start(s32[1,16,8]{1,2,0:T(8,128)} %param.17) | copy-start | bytes 1540
  4.4 10.2 %copy-start.4 = (bf16[1,16,4,256]{3,2,1,0:T(4,128)(2,1)S(1)}, bf16[1,16,4,256]{3,2,1,0:T(4,128)(2,1)}, u32[]{:S(2)}) copy-start(bf16[1,16,4,256]{3,2,1,0:T(4,128)(2,1)} %param.15) | copy-start | bytes 98308
  5.4 11.9 %copy-start.3 = (bf16[3,3,32,64]{3,2,1,0:T(8,128)(2,1)S(1)}, bf16[3,3,32,64]{3,2,1,0:T(8,128)(2,1)}, u32[]{:S(2)}) copy-start(bf16[3,3,32,64]{3,2,1,0:T(8,128)(2,1)} %param.18) | copy-start | bytes 110596
  5.5 10.8 %collective-permute-start = (bf16[16,17,3,32]{3,0,2,1:T(8,128)(2,1)S(1)}, bf16[16,17,3,32]{3,0,2,1:T(8,128)(2,1)S(1)}, u32[]{:S(2)}, u32[]{:S(2)}) collective-permute-start(bf16[16,17,3,32]{3,0,2,1:T(8,128)(2,1)S(1)} %pad_maximum_fusion.2), channel_id=1, source_target_pairs={{1,0},{2,1},{3,2},{4,3},{5,4},{6,5},{7,6},{8,7},{9,8},{10,9},{11,1... | collective-permute-start | bytes 156680 | tf_op jit(solution)/shard_map/ppermute | solution.py:18
  17.4 1.2 %copy-start.1 = (bf16[16,17,1,32]{3,0,2,1:T(8,128)(2,1)}, bf16[16,17,1,32]{3,0,2,1:T(8,128)(2,1)S(1)}, u32[]{:S(2)}) copy-start(bf16[16,17,1,32]{3,0,2,1:T(8,128)(2,1)S(1)} %maximum_bitcast_fusion) | copy-start | bytes 52228
  17.4 1.6 %copy-start.6 = (f32[64]{0:T(128)S(1)}, f32[64]{0:T(128)}, u32[]{:S(2)}) copy-start(f32[64]{0:T(128)} %param.20) | copy-start | bytes 772
  21.2 1.1 %copy-start.8 = (f32[64]{0:T(128)S(1)}, f32[64]{0:T(128)}, u32[]{:S(2)}) copy-start(f32[64]{0:T(128)} %param.21) | copy-start | bytes 772
  21.5 0.6 copy-start.5
  23.8 3.3 %collective-permute-start.1 = (bf16[16,576]{1,0:T(8,128)(2,1)S(1)}, bf16[16,576]{1,0:T(8,128)(2,1)}, u32[]{:S(2)}, u32[]{:S(2)}) collective-permute-start(bf16[16,576]{1,0:T(8,128)(2,1)S(1)} %convert_element_type.57), channel_id=1, source_target_pairs={{0,1},{1,2},{2,3},{3,4},{4,5},{5,6},{6,7},{7,8},{8,9},{9,10},{10,1... | collective-permute-start | bytes 55304 | tf_op jit(solution)/shard_map/ppermute | solution.py:18
  26.8 1.7 %copy-start.10 = (pred[48]{0:T(512)(128)(4,1)S(1)}, pred[48]{0:T(512)(128)(4,1)}, u32[]{:S(2)}) copy-start(pred[48]{0:T(512)(128)(4,1)} %get-tuple-element.55) | copy-start | bytes 148
  26.8 1.7 %copy-start.11 = (pred[48]{0:T(512)(128)(4,1)S(1)}, pred[48]{0:T(512)(128)(4,1)}, u32[]{:S(2)}) copy-start(pred[48]{0:T(512)(128)(4,1)} %get-tuple-element.84) | copy-start | bytes 148
  30.4 0.9 copy-start.2
  32.9 0.6 copy-start.9

commit v10 on v7

--- a/solution.py
+++ b/solution.py
@@ -235,7 +235,7 @@
     grad_weight_one = weight_grad(padded_one, grad_z_one.astype(jnp.bfloat16))
     parts = (grad_weight_one, grad_weight_two, grad_gain_one, grad_gain_two)
     flat = jnp.concatenate([part.reshape(-1) for part in parts])
-    flat = summed_everywhere(flat, ("dp", "space_0"), ("space_1", "space_2"))
+    flat = summed_everywhere(flat, ("space_0", "space_1"), ("dp", "space_2"))
     sizes = [part.size for part in parts]
     bounds = [sum(sizes[:index]) for index in range(len(sizes) + 1)]
     grad_weight_one, grad_weight_two, grad_gain_one, grad_gain_two = (

time: 93.4 us -> 91.9 us (0.984)
  blocking collectives: 56.7 us -> 55.7 us
    all_to_all x1, blocking collectives: 26 us -> 18.8 us  [summed_everywhere(): lax.all_to_all(lines.reshape(far_peers, -1), far, 0, 0, tiled=True)]
    all_to_all x2, blocking collectives: 30.7 us -> 37 us  [from_everyone(): lax.all_to_all(jnp.broadcast_to(value[None], (peers, *value.shape)), axis...]
where the time goes in v10:
time: 91.9 us; the launch traced here: 91.4 us
  blocking collectives  55.7 us (61%)
  starting transfers between devices  10.8 us (12%)
  local copies, waits for them, and re-layouts  10.5 us (11%)
  other arithmetic  7.31 us (8%)
  matrix products  4.83 us (5%)
  between operations  2.12 us (2%)
    all_to_all x2, blocking collectives, from_everyone(): lax.all_to_all(jnp.broadcast_to(value[None], (peers, *value.shape)), axis...  37 us
    all_to_all x1, blocking collectives, summed_everywhere(): lax.all_to_all(lines.reshape(far_peers, -1), far, 0, 0, tiled=True)  18.8 us
    ppermute x2, starting transfers between devices, from_behind(): lax.ppermute(value, axis, [(source, source + steps) for source in range(f...  10.8 us
    gather x5, local copies, waits for them, and re-layouts, select_rows(): picked = jnp.take(source, positions, axis=0)  2.66 us
    conv_general_dilated x2, matrix products, weight_grad(): lax.conv_general_dilated(padded, grad_z, (1, 1), 'VALID', rhs_dilation=(2...  2.43 us
    conv_general_dilated x3, matrix products, conv_forward(): lax.conv_general_dilated(padded, weight, (2, 2), 'VALID', dimension_numbe...  2.04 us
  transfers between devices with their start and end apart: 2, of which 0 were waited for; matrix products, arithmetic and copies ran while one was open for 3% of the time, Pallas kernels for 0%

profile of v10, /device:TPU:1, one launch (start us, length us, event | category | flops | bytes accessed | tf_op | source)
XLA Modules:
  0.0 91.4 jit_solution(571899149954683553)
XLA Ops:
  1.4 0.7 and_bitcast_fusion
  2.1 1.7 %reshape_squeeze.19 = bf16[16,16,16,32]{3,2,1,0:T(8,128)(2,1)S(1)} reshape(bf16[1,16,16,512]{3,2,1,0:T(8,128)(2,1)} %param.14) | data formatting | bytes 524288 | tf_op jit(solution)/shard_map/reshape;squeeze | solution.py:164
  3.8 0.6 copy_select_fusion
  4.6 0.6 gather_fusion
  5.5 8.9 %collective-permute-start = (bf16[16,17,3,32]{3,0,2,1:T(8,128)(2,1)S(1)}, bf16[16,17,3,32]{3,0,2,1:T(8,128)(2,1)S(1)}, u32[]{:S(2)}, u32[]{:S(2)}) collective-permute-start(bf16[16,17,3,32]{3,0,2,1:T(8,128)(2,1)S(1)} %pad_maximum_fusion.4), channel_id=1, source_target_pairs={{1,0},{2,1},{3,2},{4,3},{5,4},{6,5},{7,6},{8,7},{9,8},{10,9},{11,1... | collective-permute-start | bytes 156680 | tf_op jit(solution)/shard_map/ppermute | solution.py:18
  14.7 0.6 broadcast_compare_fusion
  15.3 0.6 compare_and_fusion
  16.4 0.6 gather_fusion.1
  17.3 1.2 %fusion.35 = (f32[16,8,8]{0,2,1:T(8,128)S(1)}, f32[16,8,8,64]{3,0,2,1:T(8,128)S(1)}) fusion(bf16[3,3,32,64]{3,2,1,0:T(8,128)(2,1)S(1)} %copy-done.1, bf16[16,17,1,32]{3,0,2,1:T(8,128)(2,1)S(1)} %maximum_bitcast_fusion, bf16[16,1,16,32]{3,0,2,1:T(8,128)(2,1)S(1)} %fusion.13, bf16[16,16,16,32]{3,0,2,1:T(8,128)(2,1)S(1)} %copy_select_fusion), kind=kOutput, calls=%fused_computation.123 | convolution fusion | flops 38109184 | bytes 599040 | tf_op jit(solution)/shard_map/conv_general_dilated | solution.py:119
  18.5 0.4 multiply_reduce_fusion.2
  18.9 0.4 multiply_convert_fusion.1
  19.3 0.5 fusion.36
  20.5 0.7 gather_fusion.2
  21.5 0.4 fusion.37
  22.0 0.2 multiply_reduce_fusion.6
  22.3 0.3 multiply_reduce_fusion.4
  22.8 0.4 fusion.38
  23.3 1.9 %collective-permute-start.1 = (bf16[16,576]{1,0:T(8,128)(2,1)S(1)}, bf16[16,576]{1,0:T(8,128)(2,1)}, u32[]{:S(2)}, u32[]{:S(2)}) collective-permute-start(bf16[16,576]{1,0:T(8,128)(2,1)S(1)} %convert_element_type.53), channel_id=1, source_target_pairs={{0,1},{1,2},{2,3},{3,4},{4,5},{5,6},{6,7},{7,8},{8,9},{9,10},{10,1... | collective-permute-start | bytes 55304 | tf_op jit(solution)/shard_map/ppermute | solution.py:18
  25.2 1.1 %fusion.7 = f32[3,3,64,64]{3,2,1,0:T(8,128)S(1)} fusion(bf16[16,4,4,64]{3,0,2,1:T(8,128)(2,1)S(1)} %multiply_convert_fusion.3, bf16[16,9,1,64]{3,0,2,1:T(8,128)(2,1)S(1)} %maximum_bitcast_fusion.1, bf16[16,1,8,64]{3,0,2,1:T(8,128)(2,1)} %copy-done.5, bf16[16,8,8,64]{3,0,2,1:T(8,128)(2,1)S(1)} %multiply_convert_fusion.1), kind=kOutput, calls=%fused_computation.24 | convolution fusion | flops 19040256 | bytes 346112 | tf_op jit(solution)/shard_map/conv_general_dilated | solution.py:130
  26.7 0.7 fusion.14
  27.4 0.7 gather_fusion.3
  28.6 0.7 multiply_reduce_fusion
  29.4 1.3 %fusion = f32[3,3,32,64]{3,2,1,0:T(8,128)S(1)} fusion(bf16[16,17,1,32]{3,0,2,1:T(8,128)(2,1)S(1)} %copy-done.3, bf16[16,1,16,32]{3,0,2,1:T(8,128)(2,1)S(1)} %fusion.13, bf16[16,16,16,32]{3,0,2,1:T(8,128)(2,1)S(1)} %copy_select_fusion, f32[16,8,8,64]{3,0,2,1:T(8,128)S(1)} %get-tuple-element.46, f32[16,8,8,64]{3,0,2,1:T(8,128)S(1)} %get-tuple-element.81, ...), kind=kOutput, calls=%fused_computation.14 | convolution fusion | flops 38568960 | bytes 910592 | tf_op jit(solution)/shard_map/conv_general_dilated | solution.py:130
  30.9 1.1 %concatenate.152 = f32[55808]{0:T(1024)S(1)} concatenate(f32[18432]{0:T(1024)S(1)} %reshape.543, f32[36864]{0:T(1024)S(1)} %reshape.544, f32[64]{0:T(128)S(1)} %get-tuple-element.40, f32[64]{0:T(128)S(1)} %get-tuple-element.43, f32[384]{0:T(512)S(1)} %broadcast_in_dim.202), dimensions={0} | concatenate | bytes 446464 | tf_op jit(solution)/shard_map/concatenate | solution.py:44
  31.9 0.3 all_to_all.14
  32.3 18.8 %all_to_all.21 = f32[32,1,1744]{2,1,0:T(1,128)S(1)} all-to-all(f32[32,1,1744]{2,1,0:T(1,128)S(1)} %all_to_all.14), channel_id=1, replica_groups=mesh['dp'=8,'space_0'=8,'space_1'=4,'space_2'=2] {'space_0','space_1'}, dimensions={0} | all-to-all | bytes 446464 | tf_op jit(solution)/shard_map/all_to_all | solution.py:77
  51.3 22.5 %all_to_all.22 = f32[16,1,1744]{2,1,0:T(1,128)S(1)} all-to-all(f32[16,1,1744]{2,1,0:T(1,128)S(1)} %broadcast_in_dim.203), channel_id=1, replica_groups=mesh['dp'=8,'space_0'=8,'space_1'=4,'space_2'=2] {'dp','space_2'}, dimensions={0} | all-to-all | bytes 223232 | tf_op jit(solution)/shard_map/all_to_all | solution.py:49
  74.0 14.5 %all_to_all.23 = f32[32,1,1744]{2,1,0:T(1,128)S(1)} all-to-all(f32[32,1,1744]{2,1,0:T(1,128)S(1)} %broadcast_in_dim.204), channel_id=1, replica_groups=mesh['dp'=8,'space_0'=8,'space_1'=4,'space_2'=2] {'space_0','space_1'}, dimensions={0} | all-to-all | bytes 446464 | tf_op jit(solution)/shard_map/all_to_all | solution.py:49
  88.5 0.5 reduce.10
  89.2 0.6 fusion.32
  89.8 0.7 reshape.546
  90.5 0.8 reshape.547
  (117 shorter events, 4.3 us)
Async XLA Ops:
  0.6 20.9 %copy-start = (bf16[3,3,64,64]{3,2,1,0:T(8,128)(2,1)S(1)}, bf16[3,3,64,64]{3,2,1,0:T(8,128)(2,1)}, u32[]{:S(2)}) copy-start(bf16[3,3,64,64]{3,2,1,0:T(8,128)(2,1)} %param.19) | copy-start | bytes 221188
  4.4 9.9 %copy-start.7 = (s32[1,16,8]{1,2,0:T(8,128)S(1)}, s32[1,16,8]{1,2,0:T(8,128)}, u32[]{:S(2)}) copy-start(s32[1,16,8]{1,2,0:T(8,128)} %param.17) | copy-start | bytes 1540
  4.4 10.2 %copy-start.4 = (bf16[1,16,4,256]{3,2,1,0:T(4,128)(2,1)S(1)}, bf16[1,16,4,256]{3,2,1,0:T(4,128)(2,1)}, u32[]{:S(2)}) copy-start(bf16[1,16,4,256]{3,2,1,0:T(4,128)(2,1)} %param.15) | copy-start | bytes 98308
  5.4 11.8 %copy-start.1 = (bf16[3,3,32,64]{3,2,1,0:T(8,128)(2,1)S(1)}, bf16[3,3,32,64]{3,2,1,0:T(8,128)(2,1)}, u32[]{:S(2)}) copy-start(bf16[3,3,32,64]{3,2,1,0:T(8,128)(2,1)} %param.18) | copy-start | bytes 110596
  5.5 10.7 %collective-permute-start = (bf16[16,17,3,32]{3,0,2,1:T(8,128)(2,1)S(1)}, bf16[16,17,3,32]{3,0,2,1:T(8,128)(2,1)S(1)}, u32[]{:S(2)}, u32[]{:S(2)}) collective-permute-start(bf16[16,17,3,32]{3,0,2,1:T(8,128)(2,1)S(1)} %pad_maximum_fusion.4), channel_id=1, source_target_pairs={{1,0},{2,1},{3,2},{4,3},{5,4},{6,5},{7,6},{8,7},{9,8},{10,9},{11,1... | collective-permute-start | bytes 156680 | tf_op jit(solution)/shard_map/ppermute | solution.py:18
  17.3 1.2 %copy-start.2 = (bf16[16,17,1,32]{3,0,2,1:T(8,128)(2,1)}, bf16[16,17,1,32]{3,0,2,1:T(8,128)(2,1)S(1)}, u32[]{:S(2)}) copy-start(bf16[16,17,1,32]{3,0,2,1:T(8,128)(2,1)S(1)} %maximum_bitcast_fusion) | copy-start | bytes 52228
  17.3 1.6 %copy-start.6 = (f32[64]{0:T(128)S(1)}, f32[64]{0:T(128)}, u32[]{:S(2)}) copy-start(f32[64]{0:T(128)} %param.20) | copy-start | bytes 772
  21.2 1.1 %copy-start.8 = (f32[64]{0:T(128)S(1)}, f32[64]{0:T(128)}, u32[]{:S(2)}) copy-start(f32[64]{0:T(128)} %param.21) | copy-start | bytes 772
  21.4 0.6 copy-start.5
  23.3 3.3 %collective-permute-start.1 = (bf16[16,576]{1,0:T(8,128)(2,1)S(1)}, bf16[16,576]{1,0:T(8,128)(2,1)}, u32[]{:S(2)}, u32[]{:S(2)}) collective-permute-start(bf16[16,576]{1,0:T(8,128)(2,1)S(1)} %convert_element_type.53), channel_id=1, source_target_pairs={{0,1},{1,2},{2,3},{3,4},{4,5},{5,6},{6,7},{7,8},{8,9},{9,10},{10,1... | collective-permute-start | bytes 55304 | tf_op jit(solution)/shard_map/ppermute | solution.py:18
  26.4 1.7 %copy-start.9 = (pred[48]{0:T(512)(128)(4,1)S(1)}, pred[48]{0:T(512)(128)(4,1)}, u32[]{:S(2)}) copy-start(pred[48]{0:T(512)(128)(4,1)} %get-tuple-element.49) | copy-start | bytes 148
  26.4 1.7 %copy-start.10 = (pred[48]{0:T(512)(128)(4,1)S(1)}, pred[48]{0:T(512)(128)(4,1)}, u32[]{:S(2)}) copy-start(pred[48]{0:T(512)(128)(4,1)} %get-tuple-element.78) | copy-start | bytes 148
  28.5 0.9 copy-start.3
